TPU v7x, 32 devices: a whole 2x2x4 slice. The times are simulated.
32 devices in a mesh: elem: 16 (over z, y, core), range: 2 (over x).
Axes of the slice: x: 2, y: 2, z: 4, core: 2. Of those that a mesh axis runs over, the one named last changes fastest.
Arguments:
- echoes: bfloat16 [2, 512, 128, 256], P(None, 'elem', None, 'range'), may hold values from -6 to 6
- replica: bfloat16 [2, 64], replicated, may hold values from -0.5 to 0.5
- beam_weights: bfloat16 [2, 64, 512], replicated, as said below
- steering: float32 [2, 128, 64], P(None, 'elem'), may hold values from -0.5 to 0.5
Outputs:
- adapted: float32 [2, 128, 256], P(None, 'elem', 'range')
Inputs may be any that keep to these rules, and one draw needn't show every extreme that they name: `beam_weights`: coefficients for 64 beams over all 512 elements.
All inputs are finite; a program needn't handle non-finite values.
Results may differ from a plain program's by a relative error of at most 0.0086.
Values may be sent and summed in bfloat16 or wider, within the bound.
No kernel may reach another device: no remote copies, remote signals or barrier semaphores. Data moves between devices by JAX's collectives and lax.ppermute only.
A program may use at most 64 MiB of HBM per device.

v0:
```python
import jax
import jax.numpy as jnp
from jax import lax
from jax.sharding import PartitionSpec as P

load_ratio = 0.1
epsilon = 1e-06


def shifted(value, axis, steps):
    count = lax.axis_size(axis)
    first, last = (max(0, -steps), min(count, count - steps))
    return lax.ppermute(value, axis, [(source, source + steps) for source in range(first, last)])


def correlation_matrix(tap_values, gate_count):
    tap_count = tap_values.shape[0]
    span_width = gate_count + tap_count - 1
    padded_taps = jnp.concatenate(
        [tap_values, jnp.zeros((span_width + 1 - tap_count,), tap_values.dtype)]
    )
    tiled_rows = jnp.tile(padded_taps, gate_count)[: gate_count * span_width].reshape(
        gate_count, span_width
    )
    return tiled_rows.T


def pulse_kernel(replica, gate_count):
    real_part = correlation_matrix(replica[0], gate_count)
    imag_part = correlation_matrix(replica[1], gate_count)
    return jnp.stack([jnp.stack([real_part, imag_part]), jnp.stack([-imag_part, real_part])])


def doppler_kernel(pulses):
    bin_index = jnp.arange(pulses, dtype=jnp.int32)
    pulse_index = jnp.arange(pulses, dtype=jnp.int32)
    phase_index = bin_index[:, None] * pulse_index[None, :] % pulses
    phase_angle = 2.0 * jnp.pi * phase_index.astype(jnp.float32) / pulses
    scale = 1.0 / jnp.sqrt(jnp.float32(pulses))
    cosine = jnp.cos(phase_angle) * scale
    sine = jnp.sin(phase_angle) * scale
    table = jnp.stack([jnp.stack([cosine, -sine]), jnp.stack([sine, cosine])])
    return table.astype(jnp.bfloat16)


def beam_kernel(beam_weights):
    weight_re = beam_weights[0]
    weight_im = beam_weights[1]
    return jnp.stack([jnp.stack([weight_re, weight_im]), jnp.stack([-weight_im, weight_re])])


def adapt(gram_sum, steering, formed):
    beams = formed.shape[2]
    cov_re = gram_sum[:, :beams, :beams] + gram_sum[:, beams:, beams:]
    cov_im = gram_sum[:, beams:, :beams] - gram_sum[:, :beams, beams:]
    loading = load_ratio * jnp.trace(cov_re, axis1=1, axis2=2) / beams + epsilon
    upper = jnp.concatenate([cov_re, -cov_im], axis=2)
    lower = jnp.concatenate([cov_im, cov_re], axis=2)
    system = jnp.concatenate([upper, lower], axis=1)
    system = system + loading[:, None, None] * jnp.eye(2 * beams, dtype=jnp.float32)[None]
    factor = jnp.linalg.cholesky(system)
    right_side = jnp.concatenate([steering[0], steering[1]], axis=-1)
    solved = jax.scipy.linalg.cho_solve((factor, True), right_side[..., None])[..., 0]
    response = jnp.sum(right_side * solved, axis=-1)
    weights = solved / response[:, None]
    weight_re = weights[:, :beams]
    weight_im = weights[:, beams:]
    beam_re = formed[:, 0].astype(jnp.float32)
    beam_im = formed[:, 1].astype(jnp.float32)
    high = lax.Precision.HIGHEST
    out_re = jnp.einsum("db,dbr->dr", weight_re, beam_re, precision=high) + jnp.einsum(
        "db,dbr->dr", weight_im, beam_im, precision=high
    )
    out_im = jnp.einsum("db,dbr->dr", weight_re, beam_im, precision=high) - jnp.einsum(
        "db,dbr->dr", weight_im, beam_re, precision=high
    )
    return jnp.stack([out_re, out_im])


def on_device(echoes, replica, beam_weights, steering):
    pulses = echoes.shape[2]
    gate_count = echoes.shape[3]
    tap_count = replica.shape[1]
    following = shifted(echoes[:, :, :, : tap_count - 1], "range", -1)
    padded = jnp.concatenate([echoes, following], axis=3)
    compressed = jnp.einsum(
        "cepj,cojr->oepr",
        padded,
        pulse_kernel(replica, gate_count),
        preferred_element_type=jnp.float32,
    ).astype(jnp.bfloat16)
    doppler = jnp.einsum(
        "cepr,codp->oedr", compressed, doppler_kernel(pulses), preferred_element_type=jnp.float32
    ).astype(jnp.bfloat16)
    kernel_full = beam_kernel(beam_weights)
    own_bins = pulses // lax.axis_size("elem")
    beam_sums = jnp.einsum(
        "cedr,cobe->dobr",
        lax.all_to_all(doppler, "elem", split_axis=2, concat_axis=1, tiled=True),
        kernel_full,
        preferred_element_type=jnp.float32,
    )
    formed = beam_sums.astype(jnp.bfloat16)
    beams = formed.shape[2]
    stacked = formed.reshape(own_bins, 2 * beams, gate_count)
    partial_gram = jnp.einsum("dbr,dcr->dbc", stacked, stacked, preferred_element_type=jnp.float32)
    gram_sum = lax.psum(partial_gram, "range") / (gate_count * lax.axis_size("range"))
    return adapt(gram_sum, steering, formed)


def solution(mesh):
    return jax.shard_map(
        on_device,
        mesh=mesh,
        in_specs=(P(None, "elem", None, "range"), P(), P(), P(None, "elem", None)),
        out_specs=P(None, "elem", "range"),
        check_vma=False,
    )
```

profile of v0, /device:TPU:8, one launch (start us, length us, event | category | flops | bytes accessed | tf_op | source)
XLA Modules:
  0.0 313.7 jit_solution(4653203343411958120)
XLA Ops:
  6.5 3.1 copy.63
  9.7 1.3 collective-permute-start
  11.0 2.7 copy.35
  13.9 0.3 reshape.130
  14.4 0.3 reshape.129
  14.8 0.3 fusion.32
  15.1 0.3 negate_convert_fusion
  15.5 20.8 %collective-permute-done = bf16[2,32,128,63]{2,1,3,0:T(8,128)(2,1)} collective-permute-done((bf16[2,32,128,63]{2,1,3,0:T(8,128)(2,1)S(1)}, bf16[2,32,128,63]{2,1,3,0:T(8,128)(2,1)}, u32[]{:S(2)}, u32[]{:S(2)}) %collective-permute-start) | collective-permute-done | bytes 1032224 | tf_op jit(solution)/shard_map/ppermute | solution.py:13
  36.2 1.6 copy.36
  37.9 3.2 %fusion.5 = bf16[2,32,128,128]{3,2,1,0:T(8,128)(2,1)} fusion(bf16[2,32,128,63]{2,3,0,1:T(8,128)(2,1)S(1)} %copy.36, bf16[2,32,128,128]{2,3,0,1:T(8,128)(2,1)S(1)} %copy-done.1, bf16[1,2,191,128]{3,2,0,1:T(8,128)(2,1)S(1)} %get-tuple-element.14, bf16[1,2,191,128]{3,2,0,1:T(8,128)(2,1)S(1)} %get-tuple-element.13, ...), kind=kOutput, calls=%fused_computation.7 | convolution fusion | flops 1346992128 | bytes 5553152 | tf_op jit(solution)/shard_map/cepr,codp->oedr/dot_general | solution.py:92
  41.0 4.2 %copy.38 = bf16[2,32,128,128]{3,1,0,2:T(8,128)(2,1)} copy(bf16[2,32,128,128]{3,2,1,0:T(8,128)(2,1)} %fusion.5) | data formatting | bytes 4194304 | tf_op jit(solution)/shard_map/convert_element_type | solution.py:94
  45.3 6.4 %all-to-all-start = ((bf16[2,32,128,128]{3,1,0,2:T(8,128)(2,1)}), bf16[2,32,128,128]{3,1,0,2:T(8,128)(2,1)S(1)}, u32[]{:S(2)}, u32[]{:S(2)}) async-start(bf16[2,32,128,128]{3,1,0,2:T(8,128)(2,1)} %copy.38), calls=%async_computation | async-start | bytes 4194304 | tf_op jit(solution)/shard_map/all_to_all | solution.py:99
  51.7 0.2 all-reduce.4.cloned.1.call-start
  52.0 45.6 %all-to-all-done = bf16[2,32,128,128]{3,1,0,2:T(8,128)(2,1)S(1)} async-done(((bf16[2,32,128,128]{3,1,0,2:T(8,128)(2,1)}), bf16[2,32,128,128]{3,1,0,2:T(8,128)(2,1)S(1)}, u32[]{:S(2)}, u32[]{:S(2)}) %all-to-all-start) | async-done | bytes 2097184 | tf_op jit(solution)/shard_map/all_to_all | solution.py:99
  97.6 0.4 copy.39
  98.0 0.4 fusion.9
  98.5 1.1 fusion.40
  99.9 28.9 %all-reduce.4.cloned.1.call-done = f32[8,128,128]{1,2,0:T(8,128)} async-done(((f32[8,128,128]{1,2,0:T(8,128)}), f32[8,128,128]{1,2,0:T(8,128)}) %all-reduce.4.cloned.1.call-update) | async-done | bytes 524304 | tf_op jit(solution)/shard_map/psum | solution.py:107
  128.8 1.1 broadcast_multiply_fusion
  129.9 0.3 fusion.38
  130.2 0.2 maximum_add_fusion
  130.4 0.2 copy.43
  130.6 0.2 fusion.13
  130.9 93.8 %custom-call.11 = f32[8,128,128]{2,1,0:T(8,128)S(1)} custom-call(f32[8,128,128]{2,1,0:T(8,128)S(1)} %fusion.13), custom_call_target="Cholesky" | custom-call | tf_op jit(solution)/shard_map/jit(cholesky)/cholesky | solution.py:61
  224.9 78.6 %custom-call.12 = f32[8,1,128,128]{2,3,1,0:T(8,128)S(1)} custom-call(f32[8,1,128,128]{3,2,1,0:T(8,128)S(1)} %select_bitcast_fusion), custom_call_target="InvertDiagBlocksLowerTriangular" | custom-call | tf_op jit(solution)/shard_map/jit(_cho_solve)/vmap()/triangular_solve | solution.py:63
  303.5 0.6 convolution_bitcast_fusion.1
  304.1 0.9 fusion.10
  305.4 0.2 fusion.25
  305.6 0.2 fusion.22
  305.8 0.2 fusion.23
  306.0 0.2 fusion.24
  306.3 0.6 pad_maximum_fusion
  (42 shorter events, 1.5 us)
Async XLA Ops:
  6.5 4.4 %copy-start = (bf16[2,32,128,128]{3,2,1,0:T(8,128)(2,1)S(1)}, bf16[2,32,128,128]{3,2,1,0:T(8,128)(2,1)}, u32[]{:S(2)}) copy-start(bf16[2,32,128,128]{3,2,1,0:T(8,128)(2,1)} %param.4) | copy-start | bytes 6291460
  9.7 4.0 %copy-start.4 = (bf16[2,64]{1,0:T(2,128)(2,1)S(1)}, bf16[2,64]{1,0:T(2,128)(2,1)}, u32[]{:S(2)}) copy-start(bf16[2,64]{1,0:T(2,128)(2,1)} %param.5) | copy-start | bytes 772
  9.7 26.5 %collective-permute-start = (bf16[2,32,128,63]{2,1,3,0:T(8,128)(2,1)S(1)}, bf16[2,32,128,63]{2,1,3,0:T(8,128)(2,1)}, u32[]{:S(2)}, u32[]{:S(2)}) collective-permute-start(bf16[2,32,128,63]{2,1,3,0:T(8,128)(2,1)S(1)} %copy.63), channel_id=1, source_target_pairs={{1,0},{3,2},{5,4},{7,6},{9,8},{11,10},{13,12},{15,14},{17,16},{19,... | collective-permute-start | bytes 3096584 | tf_op jit(solution)/shard_map/ppermute | solution.py:13
  13.7 24.1 %copy-start.1 = (bf16[2,32,128,128]{2,3,0,1:T(8,128)(2,1)S(1)}, bf16[2,32,128,128]{2,3,0,1:T(8,128)(2,1)}, u32[]{:S(2)}) copy-start(bf16[2,32,128,128]{2,3,0,1:T(8,128)(2,1)} %copy.35) | copy-start | bytes 6291460
  45.3 6.7 %copy-start.2 = (bf16[2,64,512]{2,1,0:T(8,128)(2,1)S(1)}, bf16[2,64,512]{2,1,0:T(8,128)(2,1)}, u32[]{:S(2)}) copy-start(bf16[2,64,512]{2,1,0:T(8,128)(2,1)} %param.6) | copy-start | bytes 393220
  45.3 6.7 %copy-start.3 = (f32[2,8,64]{2,1,0:T(8,128)S(1)}, f32[2,8,64]{2,1,0:T(8,128)}, u32[]{:S(2)}) copy-start(f32[2,8,64]{2,1,0:T(8,128)} %param.7) | copy-start | bytes 12292
  45.3 52.3 %all-to-all-start = ((bf16[2,32,128,128]{3,1,0,2:T(8,128)(2,1)}), bf16[2,32,128,128]{3,1,0,2:T(8,128)(2,1)S(1)}, u32[]{:S(2)}, u32[]{:S(2)}) async-start(bf16[2,32,128,128]{3,1,0,2:T(8,128)(2,1)} %copy.38), calls=%async_computation | async-start | bytes 4194304 | tf_op jit(solution)/shard_map/all_to_all | solution.py:99
  51.7 77.1 %all-reduce.4.cloned.1.call-start = ((), (), s32[]{:S(2)}) async-start(), calls=%async_computation.1 | async-start | bytes 1048576 | tf_op jit(solution)/shard_map/psum | solution.py:107
Sparse Core Ops, SparseCore 0:
  99.8 28.9 all-reduce.3
where the time goes:
time: 316 us; the launch traced here: 314 us
  other arithmetic  176 us (56%)
  waiting for transfers between devices  95.2 us (30%)
  between operations  13.7 us (4%)
  local copies, waits for them, and re-layouts  13.6 us (4%)
  starting transfers between devices  7.94 us (3%)
  matrix products  7.06 us (2%)
    another operation x4, other arithmetic, adapt(): factor = jnp.linalg.cholesky(system)  94 us
    another operation x3, other arithmetic, adapt(): jax.scipy.linalg.cho_solve((factor, True), right_side[..., None])[..., 0]  78.7 us
    all_to_all x1, waiting for transfers between devices, on_device(): lax.all_to_all(doppler, 'elem', split_axis=2, concat_axis=1, tiled=True)  45.6 us
    psum x1, waiting for transfers between devices, on_device(): lax.psum(partial_gram, 'range') / (gate_count * lax.axis_size('range'))  28.9 us
    ppermute x1, waiting for transfers between devices, shifted(): lax.ppermute(value, axis, [(source, source + steps) for source in range(f...  20.8 us
    all_to_all x1, starting transfers between devices, on_device(): lax.all_to_all(doppler, 'elem', split_axis=2, concat_axis=1, tiled=True)  6.43 us
  transfers between devices with their start and end apart: 3, of which 3 were waited for; matrix products, arithmetic and copies ran while one was open for 1% of the time, Pallas kernels for 0%

commit v1 on v0

--- a/solution.py
+++ b/solution.py
@@ -1,10 +1,16 @@
+import functools
+
 import jax
 import jax.numpy as jnp
+import numpy as np
 from jax import lax
+from jax.experimental import pallas as pl
+from jax.experimental.pallas import tpu as pltpu
 from jax.sharding import PartitionSpec as P
 
 load_ratio = 0.1
 epsilon = 1e-06
+VMEM_BYTES = 56 << 20
 
 
 def shifted(value, axis, steps):
@@ -31,15 +37,14 @@
     return jnp.stack([jnp.stack([real_part, imag_part]), jnp.stack([-imag_part, real_part])])
 
 
-def doppler_kernel(pulses):
-    bin_index = jnp.arange(pulses, dtype=jnp.int32)
-    pulse_index = jnp.arange(pulses, dtype=jnp.int32)
-    phase_index = bin_index[:, None] * pulse_index[None, :] % pulses
-    phase_angle = 2.0 * jnp.pi * phase_index.astype(jnp.float32) / pulses
-    scale = 1.0 / jnp.sqrt(jnp.float32(pulses))
-    cosine = jnp.cos(phase_angle) * scale
-    sine = jnp.sin(phase_angle) * scale
-    table = jnp.stack([jnp.stack([cosine, -sine]), jnp.stack([sine, cosine])])
+def doppler_table(pulses):
+    index = np.arange(pulses, dtype=np.int64)
+    phase_index = (index[:, None] * index[None, :]) % pulses
+    phase_angle = np.float32(2.0 * np.pi) * phase_index.astype(np.float32) / np.float32(pulses)
+    scale = np.float32(1.0) / np.sqrt(np.float32(pulses))
+    cosine = np.cos(phase_angle) * scale
+    sine = np.sin(phase_angle) * scale
+    table = np.stack([np.stack([cosine, -sine]), np.stack([sine, cosine])])
     return table.astype(jnp.bfloat16)
 
 
@@ -77,7 +82,7 @@
     return jnp.stack([out_re, out_im])
 
 
-def on_device(echoes, replica, beam_weights, steering):
+def on_device_general(echoes, replica, beam_weights, steering):
     pulses = echoes.shape[2]
     gate_count = echoes.shape[3]
     tap_count = replica.shape[1]
@@ -90,7 +95,10 @@
         preferred_element_type=jnp.float32,
     ).astype(jnp.bfloat16)
     doppler = jnp.einsum(
-        "cepr,codp->oedr", compressed, doppler_kernel(pulses), preferred_element_type=jnp.float32
+        "cepr,codp->oedr",
+        compressed,
+        jnp.asarray(doppler_table(pulses)),
+        preferred_element_type=jnp.float32,
     ).astype(jnp.bfloat16)
     kernel_full = beam_kernel(beam_weights)
     own_bins = pulses // lax.axis_size("elem")
@@ -108,6 +116,242 @@
     return adapt(gram_sum, steering, formed)
 
 
+def whole_vmem(count):
+    return [pl.BlockSpec(memory_space=pltpu.VMEM)] * count
+
+
+def spectra_body(table_ref, echo_ref, out_ref):
+    table = table_ref[...]
+    owners = out_ref.shape[0]
+    gates = echo_ref.shape[3]
+    for pair in range(echo_ref.shape[1] // 2):
+        even, odd = 2 * pair, 2 * pair + 1
+        samples = jnp.concatenate(
+            [
+                jnp.concatenate([echo_ref[0, even], echo_ref[0, odd]], axis=1),
+                jnp.concatenate([echo_ref[1, even], echo_ref[1, odd]], axis=1),
+            ],
+            axis=0,
+        )
+        bins = jnp.dot(table, samples, preferred_element_type=jnp.float32)
+        bins = bins.reshape(owners, bins.shape[0] // owners, 2 * gates)
+        rows = jnp.concatenate([bins[:, :, :gates], bins[:, :, gates:]], axis=1)
+        out_ref[:, pair] = rows.astype(jnp.bfloat16)
+
+
+def spectra(echoes, devices, block=8):
+    _, elements, pulses, gates = echoes.shape
+    bins = pulses // devices
+    table = doppler_table(pulses)
+    table = table.transpose(2, 1, 0, 3).reshape(devices, bins, 2, 2 * pulses)
+    table = table.transpose(0, 2, 1, 3).reshape(2 * pulses, 2 * pulses)
+    return pl.pallas_call(
+        spectra_body,
+        grid=(elements // block,),
+        in_specs=[
+            pl.BlockSpec((2 * pulses, 2 * pulses), lambda i: (0, 0)),
+            pl.BlockSpec((2, block, pulses, gates), lambda i: (0, i, 0, 0)),
+        ],
+        out_specs=pl.BlockSpec((devices, block // 2, 4 * bins, gates), lambda i: (0, i, 0, 0)),
+        out_shape=jax.ShapeDtypeStruct((devices, elements // 2, 4 * bins, gates), jnp.bfloat16),
+        compiler_params=pltpu.CompilerParams(vmem_limit_bytes=VMEM_BYTES),
+        name="spectra",
+    )(jnp.asarray(table), echoes)
+
+
+def spread_body(weight_ref, out_ref, *, bins):
+    beams = weight_ref.shape[1]
+    elements = weight_ref.shape[2]
+    group = 128
+    width = group * 2 * bins
+    lane = lax.broadcasted_iota(jnp.int32, (group, width), 1)
+    row = lax.broadcasted_iota(jnp.int32, (group, width), 0)
+    repeat = jnp.where(lane // (2 * bins) == row, 1.0, 0.0).astype(jnp.bfloat16)
+    col = lax.broadcasted_iota(jnp.int32, (beams, width), 1)
+    is_real = (col // bins) % 2 == 0
+    own = col % bins
+    for at in range(elements // group):
+        span = slice(at * group, (at + 1) * group)
+        real = jnp.dot(weight_ref[0, :, span], repeat, preferred_element_type=jnp.float32)
+        imag = jnp.dot(weight_ref[1, :, span], repeat, preferred_element_type=jnp.float32)
+        to_real = jnp.where(is_real, real, -imag)
+        to_imag = jnp.where(is_real, imag, real)
+        for d in range(bins):
+            here = slice(at * width, (at + 1) * width)
+            base = d * 2 * beams
+            out_ref[base : base + beams, here] = jnp.where(own == d, to_real, 0.0).astype(jnp.bfloat16)
+            out_ref[base + beams : base + 2 * beams, here] = jnp.where(own == d, to_imag, 0.0).astype(
+                jnp.bfloat16
+            )
+
+
+def spread(beam_weights, bins):
+    _, beams, elements = beam_weights.shape
+    return pl.pallas_call(
+        functools.partial(spread_body, bins=bins),
+        in_specs=whole_vmem(1),
+        out_specs=whole_vmem(1)[0],
+        out_shape=jax.ShapeDtypeStruct((bins * 2 * beams, elements * 2 * bins), jnp.bfloat16),
+        compiler_params=pltpu.CompilerParams(vmem_limit_bytes=VMEM_BYTES),
+        name="spread",
+    )(beam_weights)
+
+
+def split(value):
+    high = value.astype(jnp.bfloat16)
+    return high, (value - high.astype(jnp.float32)).astype(jnp.bfloat16)
+
+
+NT = (((1,), (1,)), ((), ()))
+
+
+def eliminate(systems, rows):
+    count = len(systems)
+    beams = 8 * len(systems[0])
+    lane = lax.broadcasted_iota(jnp.int32, (8, 2 * beams), 1)
+    sub = lax.broadcasted_iota(jnp.int32, (8, 2 * beams), 0)
+    shape = (8, 2 * beams)
+    for k in range(beams):
+        block, inside = divmod(k, 8)
+        for n in range(count):
+            a = systems[n]
+            pivot_row = jnp.broadcast_to(a[block][inside : inside + 1, :], shape)
+            pivot = jnp.broadcast_to(pivot_row[:, k : k + 1], shape)
+            inverse = 1.0 / pivot
+            is_re = lane == k
+            is_im = lane == beams + k
+            unit = jnp.where(is_re, 1.0, jnp.where(is_im, 0.0, pivot_row))
+            turned = pltpu.roll(unit, beams, 1)
+            turned = jnp.where(lane < beams, -turned, turned)
+            scaled = unit * inverse
+            turned = turned * inverse
+            for v in range(block, len(a) + 1):
+                part = rows[n] if v == len(a) else a[v]
+                re = jnp.broadcast_to(part[:, k : k + 1], shape)
+                im = jnp.broadcast_to(part[:, beams + k : beams + k + 1], shape)
+                kept = jnp.where(is_re | is_im, 0.0, part)
+                new = kept - re * scaled - im * turned
+                if v == block:
+                    new = jnp.where(sub > inside, new, part)
+                if v == len(a):
+                    rows[n] = new
+                else:
+                    a[v] = new
+    return rows
+
+
+def beams_body(side_ref, spectra_ref, spread_ref, pulse_ref, steer_ref, own_ref, send_ref):
+    bins = steer_ref.shape[0]
+    total = spread_ref.shape[0]
+    beams = total // (2 * bins)
+    ranges = spectra_ref.shape[1]
+    gates = ranges * spectra_ref.shape[4]
+    width = spectra_ref.shape[0] * spectra_ref.shape[2] * spectra_ref.shape[3]
+    received = jnp.concatenate(
+        [spectra_ref[:, j].reshape(width, gates // ranges) for j in range(ranges)], axis=1
+    )
+    sums = jnp.dot(spread_ref[...], received, preferred_element_type=jnp.float32)
+    wide = jnp.concatenate(
+        [
+            jnp.concatenate(
+                [sums[d * 2 * beams : d * 2 * beams + beams], sums[d * 2 * beams + beams : (d + 1) * 2 * beams]],
+                axis=1,
+            )
+            for d in range(bins)
+        ],
+        axis=0,
+    )
+    high, low = split(wide)
+    pulse = pulse_ref[...]
+    formed = jnp.dot(high, pulse, preferred_element_type=jnp.float32) + jnp.dot(
+        low, pulse, preferred_element_type=jnp.float32
+    )
+    sub = lax.broadcasted_iota(jnp.int32, (beams, 2 * beams), 0)
+    lane = lax.broadcasted_iota(jnp.int32, (beams, 2 * beams), 1)
+    systems, rows, both = [], [], []
+    for d in range(bins):
+        real = formed[d * beams : (d + 1) * beams, :gates]
+        imag = formed[d * beams : (d + 1) * beams, gates:]
+        top = jnp.concatenate([real, imag], axis=1)
+        whole = jnp.concatenate([top, jnp.concatenate([-imag, real], axis=1)], axis=0)
+        g_high, g_low = split(whole)
+        both.append((g_high, g_low))
+        cov = lax.dot_general(g_high[:beams], g_high, NT, preferred_element_type=jnp.float32)
+        cov = cov + lax.dot_general(g_high[:beams], g_low, NT, preferred_element_type=jnp.float32)
+        cov = cov + lax.dot_general(g_low[:beams], g_high, NT, preferred_element_type=jnp.float32)
+        cov = cov * (1.0 / gates)
+        on_diagonal = sub == lane
+        trace = jnp.sum(jnp.where(on_diagonal, cov, 0.0), axis=(0, 1), keepdims=True)
+        loading = load_ratio * trace / beams + epsilon
+        cov = jnp.where(on_diagonal, cov + loading, cov)
+        systems.append([cov[8 * v : 8 * v + 8] for v in range(beams // 8)])
+        rows.append(jnp.broadcast_to(steer_ref[d : d + 1, :], (8, 2 * beams)))
+    rows = eliminate(systems, rows)
+    own_side = side_ref[0] == 0
+    half = gates // ranges
+    for d in range(bins):
+        conj = -rows[d]
+        steer = jnp.broadcast_to(steer_ref[d : d + 1, :], (8, 2 * beams))
+        response = jnp.sum(conj * steer, axis=1, keepdims=True)
+        weight = conj / response
+        w_high, w_low = split(weight)
+        g_high, g_low = both[d]
+        out = jnp.dot(w_high, g_high, preferred_element_type=jnp.float32)
+        out = out + jnp.dot(w_high, g_low, preferred_element_type=jnp.float32)
+        out = out + jnp.dot(w_low, g_high, preferred_element_type=jnp.float32)
+        for part in range(2):
+            first = out[:1, part * gates : part * gates + half]
+            second = out[:1, part * gates + half : (part + 1) * gates]
+            own_ref[part, d : d + 1, :] = jnp.where(own_side, first, second)
+            send_ref[part, d : d + 1, :] = jnp.where(own_side, second, first)
+
+
+def on_device_owned(echoes, replica, beam_weights, steering):
+    elems, ranges = lax.axis_size("elem"), lax.axis_size("range")
+    devices = elems * ranges
+    _, own_elements, pulses, gate_count = echoes.shape
+    bins = pulses // devices
+    beams = beam_weights.shape[1]
+    gates = gate_count * ranges
+    side = lax.axis_index("range")
+    bound = lax.all_to_all(spectra(echoes, devices), ("elem", "range"), 0, 0, tiled=True)
+    bound = bound.reshape(elems, ranges, own_elements // 2, 4 * bins, gate_count)
+    pulse = pulse_kernel(replica, gates)[:, :, :gates]
+    pulse = pulse.transpose(0, 2, 1, 3).reshape(2 * gates, 2 * gates)
+    own_steering = lax.dynamic_slice_in_dim(steering, side * bins, bins, 1)
+    steer_row = jnp.concatenate([own_steering[0], -own_steering[1]], axis=1)
+    shape = jax.ShapeDtypeStruct((2, bins, gate_count), jnp.float32)
+    own, send = pl.pallas_call(
+        beams_body,
+        in_specs=[pl.BlockSpec(memory_space=pltpu.SMEM)] + whole_vmem(4),
+        out_specs=whole_vmem(2),
+        out_shape=[shape, shape],
+        compiler_params=pltpu.CompilerParams(vmem_limit_bytes=VMEM_BYTES),
+        name="beams",
+    )(side.reshape(1).astype(jnp.int32), bound, spread(beam_weights, bins), pulse, steer_row)
+    other = lax.ppermute(send, "range", [(0, 1), (1, 0)])
+    first = jnp.where(side == 0, own, other)
+    second = jnp.where(side == 0, other, own)
+    return jnp.concatenate([first, second], axis=1)
+
+
+def on_device(echoes, replica, beam_weights, steering):
+    elems, ranges = lax.axis_size("elem"), lax.axis_size("range")
+    pulses, gate_count = echoes.shape[2:]
+    beams, elements = beam_weights.shape[1:]
+    owned = (
+        ranges == 2
+        and pulses == 4 * elems * ranges
+        and gate_count % 128 == 0
+        and beams == 64
+        and elements % 128 == 0
+        and echoes.shape[1] % 8 == 0
+        and replica.shape[1] <= gate_count
+    )
+    run = on_device_owned if owned else on_device_general
+    return run(echoes, replica, beam_weights, steering)
+
+
 def solution(mesh):
     return jax.shard_map(
         on_device,

time: 316 us -> 85 us (0.27)
  the two profiles are of different devices: /device:TPU:8 before, /device:TPU:0 now
where the time goes in v1:
time: 85 us; the launch traced here: 84.7 us
  waiting for transfers between devices  43.2 us (51%)
  Pallas kernels  26.1 us (31%)
  starting transfers between devices  8.74 us (10%)
  local copies, waits for them, and re-layouts  4.54 us (5%)
  other arithmetic  2.06 us (2%)
    all_to_all x1, waiting for transfers between devices, on_device_owned(): lax.all_to_all(spectra(echoes, devices), ('elem', 'range'), 0, 0, tiled=T...  40.9 us
    pallas_call x1, Pallas kernels, on_device_owned(): pl.pallas_call(beams_body, in_specs=[pl.BlockSpec(memory_space=pltpu.SMEM...  17.9 us
    all_to_all x1, starting transfers between devices, on_device_owned(): lax.all_to_all(spectra(echoes, devices), ('elem', 'range'), 0, 0, tiled=T...  7.3 us
    pallas_call x1, Pallas kernels, spectra(): pl.pallas_call(spectra_body, grid=(elements // block,), in_specs=[pl.Bloc...  4.41 us
    pallas_call x1, Pallas kernels, spread(): pl.pallas_call(functools.partial(spread_body, bins=bins), in_specs=whole_...  3.79 us
    ppermute x1, waiting for transfers between devices, on_device_owned(): other = lax.ppermute(send, 'range', [(0, 1), (1, 0)])  2.37 us
    unnamed x7, local copies, waits for them, and re-layouts  2.24 us
  transfers between devices with their start and end apart: 2, of which 2 were waited for; matrix products, arithmetic and copies ran while one was open for 5% of the time, Pallas kernels for 4%

profile of v1, /device:TPU:0, one launch (start us, length us, event | category | flops | bytes accessed | tf_op | source)
XLA Modules:
  0.0 84.7 jit_solution(11374497698222495291)
XLA Ops:
  0.0 4.4 %spectra.1 = bf16[32,16,16,128]{3,2,1,0:T(8,128)(2,1)} custom-call(bf16[256,256]{1,0:T(8,128)(2,1)} %constant.14.clone.table_ref, bf16[2,32,128,128]{3,2,1,0:T(8,128)(2,1)} %echo_ref.1), custom_call_target="tpu_custom_call" | custom-call | tf_op jit(solution)/shard_map/spectra/pallas_call | solution.py:148
  4.4 0.0 copy-start.2
  4.4 7.3 %all-to-all-start = ((bf16[32,16,16,128]{3,2,1,0:T(8,128)(2,1)}), bf16[32,16,16,128]{3,2,1,0:T(8,128)(2,1)S(1)}, u32[]{:S(2)}, u32[]{:S(2)}) async-start(bf16[32,16,16,128]{3,2,1,0:T(8,128)(2,1)} %spectra.1), calls=%async_computation | async-start | bytes 4194304 | tf_op jit(solution)/shard_map/all_to_all | solution.py:317
  11.7 0.0 copy-done.2
  11.8 0.3 tile.9
  12.1 0.4 reshape.20
  12.5 0.1 copy.7
  12.7 0.3 tile.21
  12.9 0.4 reshape.21
  13.4 0.1 copy.8
  13.6 0.1 maximum_bitcast_fusion
  13.7 0.5 copy.9
  14.2 0.9 %copy.10 = bf16[64,8,2,256]{3,1,2,0:T(8,128)(2,1)} copy(bf16[64,8,2,256]{3,2,1,0:T(2,128)(2,1)S(1)} %bitcast.37) | data formatting | bytes 1048576
  15.1 0.0 copy-start.1
  15.1 3.8 %spread.1.spread_ref = bf16[512,4096]{1,0:T(8,128)(2,1)} custom-call(bf16[2,64,512]{2,1,0:T(8,128)(2,1)} %weight_ref.1), custom_call_target="tpu_custom_call" | custom-call | tf_op jit(solution)/shard_map/spread/pallas_call | solution.py:190
  18.9 0.0 copy-done.1
  18.9 0.7 pad_maximum_fusion.2.steer_ref
  19.6 40.9 %all-to-all-done = bf16[32,16,16,128]{3,2,1,0:T(8,128)(2,1)S(1)} async-done(((bf16[32,16,16,128]{3,2,1,0:T(8,128)(2,1)}), bf16[32,16,16,128]{3,2,1,0:T(8,128)(2,1)S(1)}, u32[]{:S(2)}, u32[]{:S(2)}) %all-to-all-start) | async-done | bytes 2097184 | tf_op jit(solution)/shard_map/all_to_all | solution.py:317
  60.4 0.0 copy-start
  60.4 1.3 %copy-done = bf16[32,16,16,128]{3,2,1,0:T(8,128)(2,1)} copy-done((bf16[32,16,16,128]{3,2,1,0:T(8,128)(2,1)}, bf16[32,16,16,128]{3,2,1,0:T(8,128)(2,1)S(1)}, u32[]{:S(2)}) %copy-start) | copy-done | bytes 2097176
  61.8 17.9 %beams.1 = (f32[2,4,128]{2,1,0:T(4,128)}, f32[2,4,128]{2,1,0:T(4,128)}) custom-call(s32[1]{0:T(128)} %bitcast.side_ref, bf16[16,2,16,16,128]{4,3,2,1,0:T(8,128)(2,1)} %bitcast.35, bf16[512,4096]{1,0:T(8,128)(2,1)} %spread.1.spread_ref, bf16[512,512]{1,0:T(8,128)(2,1)} %bitcast.36, f32[4,128]{1,0:T(4,128)} %pad_maximum_fusion.2.steer_ref), custom_call_target="tpu_custom_call" | custom-call | tf_op jit(solution)/shard_map/beams/pallas_call | solution.py:324
  79.6 1.4 %collective-permute-start = (f32[2,4,128]{2,1,0:T(4,128)}, f32[2,4,128]{2,1,0:T(4,128)S(1)}, u32[]{:S(2)}, u32[]{:S(2)}) collective-permute-start(f32[2,4,128]{2,1,0:T(4,128)} %get-tuple-element.8), channel_id=1, source_target_pairs={{0,1},{1,0},{2,3},{3,2},{4,5},{5,4},{6,7},{7,6},{8,9},{9,8},{10,11... | collective-permute-start | bytes 12296 | tf_op jit(solution)/shard_map/ppermute | solution.py:332
  81.1 2.4 %collective-permute-done = f32[2,4,128]{2,1,0:T(4,128)S(1)} collective-permute-done((f32[2,4,128]{2,1,0:T(4,128)}, f32[2,4,128]{2,1,0:T(4,128)S(1)}, u32[]{:S(2)}, u32[]{:S(2)}) %collective-permute-start) | collective-permute-done | bytes 4128 | tf_op jit(solution)/shard_map/ppermute | solution.py:332
  83.4 0.7 broadcast_select_fusion.1
  84.1 0.6 pad_maximum_fusion.1
  (8 shorter events, 0.1 us)
Async XLA Ops:
  4.4 7.3 %copy-start.2 = (bf16[2,64]{1,0:T(2,128)(2,1)S(1)}, bf16[2,64]{1,0:T(2,128)(2,1)}, u32[]{:S(2)}) copy-start(bf16[2,64]{1,0:T(2,128)(2,1)} %param.6) | copy-start | bytes 772
  4.4 56.0 %all-to-all-start = ((bf16[32,16,16,128]{3,2,1,0:T(8,128)(2,1)}), bf16[32,16,16,128]{3,2,1,0:T(8,128)(2,1)S(1)}, u32[]{:S(2)}, u32[]{:S(2)}) async-start(bf16[32,16,16,128]{3,2,1,0:T(8,128)(2,1)} %spectra.1), calls=%async_computation | async-start | bytes 4194304 | tf_op jit(solution)/shard_map/all_to_all | solution.py:317
  15.1 3.8 %copy-start.1 = (f32[2,8,64]{2,1,0:T(8,128)S(1)}, f32[2,8,64]{2,1,0:T(8,128)}, u32[]{:S(2)}) copy-start(f32[2,8,64]{2,1,0:T(8,128)} %param.8) | copy-start | bytes 12292
  60.4 1.3 %copy-start = (bf16[32,16,16,128]{3,2,1,0:T(8,128)(2,1)}, bf16[32,16,16,128]{3,2,1,0:T(8,128)(2,1)S(1)}, u32[]{:S(2)}) copy-start(bf16[32,16,16,128]{3,2,1,0:T(8,128)(2,1)S(1)} %all-to-all-done) | copy-start | bytes 6291460
  79.6 3.8 %collective-permute-start = (f32[2,4,128]{2,1,0:T(4,128)}, f32[2,4,128]{2,1,0:T(4,128)S(1)}, u32[]{:S(2)}, u32[]{:S(2)}) collective-permute-start(f32[2,4,128]{2,1,0:T(4,128)} %get-tuple-element.8), channel_id=1, source_target_pairs={{0,1},{1,0},{2,3},{3,2},{4,5},{5,4},{6,7},{7,6},{8,9},{9,8},{10,11... | collective-permute-start | bytes 12296 | tf_op jit(solution)/shard_map/ppermute | solution.py:332

commit v2 on v1

--- a/solution.py
+++ b/solution.py
@@ -10,7 +10,9 @@
 
 load_ratio = 0.1
 epsilon = 1e-06
-VMEM_BYTES = 56 << 20
+SPECTRA_VMEM = 56 << 20
+SMALL_VMEM = 14 << 20
+BEAMS_VMEM = 24 << 20
 
 
 def shifted(value, axis, steps):
@@ -139,11 +141,12 @@
         out_ref[:, pair] = rows.astype(jnp.bfloat16)
 
 
-def spectra(echoes, devices, block=8):
+def spectra(echoes, owners, block=8):
     _, elements, pulses, gates = echoes.shape
+    devices = len(owners)
     bins = pulses // devices
     table = doppler_table(pulses)
-    table = table.transpose(2, 1, 0, 3).reshape(devices, bins, 2, 2 * pulses)
+    table = table.transpose(2, 1, 0, 3).reshape(devices, bins, 2, 2 * pulses)[np.asarray(owners)]
     table = table.transpose(0, 2, 1, 3).reshape(2 * pulses, 2 * pulses)
     return pl.pallas_call(
         spectra_body,
@@ -154,7 +157,7 @@
         ],
         out_specs=pl.BlockSpec((devices, block // 2, 4 * bins, gates), lambda i: (0, i, 0, 0)),
         out_shape=jax.ShapeDtypeStruct((devices, elements // 2, 4 * bins, gates), jnp.bfloat16),
-        compiler_params=pltpu.CompilerParams(vmem_limit_bytes=VMEM_BYTES),
+        compiler_params=pltpu.CompilerParams(vmem_limit_bytes=SPECTRA_VMEM),
         name="spectra",
     )(jnp.asarray(table), echoes)
 
@@ -169,20 +172,13 @@
     repeat = jnp.where(lane // (2 * bins) == row, 1.0, 0.0).astype(jnp.bfloat16)
     col = lax.broadcasted_iota(jnp.int32, (beams, width), 1)
     is_real = (col // bins) % 2 == 0
-    own = col % bins
     for at in range(elements // group):
         span = slice(at * group, (at + 1) * group)
+        here = slice(at * width, (at + 1) * width)
         real = jnp.dot(weight_ref[0, :, span], repeat, preferred_element_type=jnp.float32)
         imag = jnp.dot(weight_ref[1, :, span], repeat, preferred_element_type=jnp.float32)
-        to_real = jnp.where(is_real, real, -imag)
-        to_imag = jnp.where(is_real, imag, real)
-        for d in range(bins):
-            here = slice(at * width, (at + 1) * width)
-            base = d * 2 * beams
-            out_ref[base : base + beams, here] = jnp.where(own == d, to_real, 0.0).astype(jnp.bfloat16)
-            out_ref[base + beams : base + 2 * beams, here] = jnp.where(own == d, to_imag, 0.0).astype(
-                jnp.bfloat16
-            )
+        out_ref[:beams, here] = jnp.where(is_real, real, -imag).astype(jnp.bfloat16)
+        out_ref[beams:, here] = jnp.where(is_real, imag, real).astype(jnp.bfloat16)
 
 
 def spread(beam_weights, bins):
@@ -191,10 +187,42 @@
         functools.partial(spread_body, bins=bins),
         in_specs=whole_vmem(1),
         out_specs=whole_vmem(1)[0],
-        out_shape=jax.ShapeDtypeStruct((bins * 2 * beams, elements * 2 * bins), jnp.bfloat16),
-        compiler_params=pltpu.CompilerParams(vmem_limit_bytes=VMEM_BYTES),
+        out_shape=jax.ShapeDtypeStruct((2 * beams, elements * 2 * bins), jnp.bfloat16),
+        compiler_params=pltpu.CompilerParams(vmem_limit_bytes=SMALL_VMEM),
         name="spread",
     )(beam_weights)
+
+
+def partial_body(half_ref, spectra_ref, spread_ref, out_ref, *, bins):
+    elems, ranges = spectra_ref.shape[:2]
+    rows = spectra_ref.shape[3] * spectra_ref.shape[4]
+    half = half_ref[0]
+    received = jnp.concatenate(
+        [
+            jnp.concatenate(
+                [spectra_ref[n, j, half].reshape(rows, spectra_ref.shape[5]) for n in range(elems)], axis=0
+            )
+            for j in range(ranges)
+        ],
+        axis=1,
+    )
+    weights = spread_ref[...]
+    own = lax.broadcasted_iota(jnp.int32, weights.shape, 1) % bins
+    for d in range(bins):
+        here = jnp.where(own == d, weights, jnp.zeros_like(weights))
+        out_ref[d] = jnp.dot(here, received, preferred_element_type=jnp.float32).astype(out_ref.dtype)
+
+
+def partial_sums(half, bound, spread_weights, bins, dtype):
+    shape = (bins, spread_weights.shape[0], bound.shape[1] * bound.shape[5])
+    return pl.pallas_call(
+        functools.partial(partial_body, bins=bins),
+        in_specs=[pl.BlockSpec(memory_space=pltpu.SMEM)] + whole_vmem(2),
+        out_specs=whole_vmem(1)[0],
+        out_shape=jax.ShapeDtypeStruct(shape, dtype),
+        compiler_params=pltpu.CompilerParams(vmem_limit_bytes=BEAMS_VMEM),
+        name="partial_sums",
+    )(half.reshape(1).astype(jnp.int32), bound, spread_weights)
 
 
 def split(value):
@@ -205,61 +233,100 @@
 NT = (((1,), (1,)), ((), ()))
 
 
-def eliminate(systems, rows):
-    count = len(systems)
-    beams = 8 * len(systems[0])
-    lane = lax.broadcasted_iota(jnp.int32, (8, 2 * beams), 1)
-    sub = lax.broadcasted_iota(jnp.int32, (8, 2 * beams), 0)
-    shape = (8, 2 * beams)
-    for k in range(beams):
-        block, inside = divmod(k, 8)
-        for n in range(count):
-            a = systems[n]
-            pivot_row = jnp.broadcast_to(a[block][inside : inside + 1, :], shape)
-            pivot = jnp.broadcast_to(pivot_row[:, k : k + 1], shape)
-            inverse = 1.0 / pivot
-            is_re = lane == k
-            is_im = lane == beams + k
-            unit = jnp.where(is_re, 1.0, jnp.where(is_im, 0.0, pivot_row))
-            turned = pltpu.roll(unit, beams, 1)
-            turned = jnp.where(lane < beams, -turned, turned)
-            scaled = unit * inverse
-            turned = turned * inverse
-            for v in range(block, len(a) + 1):
-                part = rows[n] if v == len(a) else a[v]
-                re = jnp.broadcast_to(part[:, k : k + 1], shape)
-                im = jnp.broadcast_to(part[:, beams + k : beams + k + 1], shape)
-                kept = jnp.where(is_re | is_im, 0.0, part)
-                new = kept - re * scaled - im * turned
-                if v == block:
-                    new = jnp.where(sub > inside, new, part)
-                if v == len(a):
-                    rows[n] = new
-                else:
-                    a[v] = new
-    return rows
-
-
-def beams_body(side_ref, spectra_ref, spread_ref, pulse_ref, steer_ref, own_ref, send_ref):
-    bins = steer_ref.shape[0]
-    total = spread_ref.shape[0]
-    beams = total // (2 * bins)
-    ranges = spectra_ref.shape[1]
-    gates = ranges * spectra_ref.shape[4]
-    width = spectra_ref.shape[0] * spectra_ref.shape[2] * spectra_ref.shape[3]
-    received = jnp.concatenate(
-        [spectra_ref[:, j].reshape(width, gates // ranges) for j in range(ranges)], axis=1
-    )
-    sums = jnp.dot(spread_ref[...], received, preferred_element_type=jnp.float32)
+def c_mul(a, b):
+    return a[0] * b[0] - a[1] * b[1], a[0] * b[1] + a[1] * b[0]
+def c_mulc(a, b):
+    return a[0] * b[0] + a[1] * b[1], a[1] * b[0] - a[0] * b[1]
+def conj(a): return a[0], -a[1]
+def c_add(a, b): return a[0] + b[0], a[1] + b[1]
+def c_sub(a, b): return a[0] - b[0], a[1] - b[1]
+def scale(a, r): return a[0] * r, a[1] * r
+
+def inverse_pair(m):
+    a, b, d = m
+    r = 1.0 / (a * d - (b[0] * b[0] + b[1] * b[1]))
+    return d * r, (-b[0] * r, -b[1] * r), a * r
+
+def inverse_four(e):
+    ea, eb, ed = inverse_pair((e[0][0][0], e[0][1], e[1][1][0]))
+    f = [[e[0][2], e[0][3]], [e[1][2], e[1][3]]]
+    t = [[None, None], [None, None]]
+    for l in range(2):
+        t[0][l] = c_add(scale(f[0][l], ea), c_mul(eb, f[1][l]))
+        t[1][l] = c_add(c_mulc(f[0][l], eb), scale(f[1][l], ed))
+    def herm(l, m):
+        return c_add(c_mulc(t[0][m], f[0][l]), c_mulc(t[1][m], f[1][l]))
+    def herm_re(l):
+        return (t[0][l][0]*f[0][l][0] + t[0][l][1]*f[0][l][1]) + (t[1][l][0]*f[1][l][0] + t[1][l][1]*f[1][l][1])
+    s = (e[2][2][0] - herm_re(0), c_sub(e[2][3], herm(0, 1)), e[3][3][0] - herm_re(1))
+    sa, sb, sd = inverse_pair(s)
+    u = [[None, None], [None, None]]
+    for j in range(2):
+        x = c_add(scale(t[j][0], sa), c_mulc(t[j][1], sb))
+        y = c_add(c_mul(t[j][0], sb), scale(t[j][1], sd))
+        u[j][0] = (-x[0], -x[1]); u[j][1] = (-y[0], -y[1])
+    def corr(j, m):
+        return c_add(c_mulc(u[j][0], t[m][0]), c_mulc(u[j][1], t[m][1]))
+    zero = jnp.zeros_like(ea)
+    p00 = ea - corr(0, 0)[0]; p11 = ed - corr(1, 1)[0]
+    p01 = c_sub(eb, corr(0, 1))
+    inv = [[None]*4 for _ in range(4)]
+    inv[0][0] = (p00, None); inv[1][1] = (p11, None); inv[0][1] = p01
+    inv[2][2] = (sa, None); inv[3][3] = (sd, None); inv[2][3] = sb
+    for j in range(2):
+        for l in range(2): inv[j][2+l] = u[j][l]
+    for j in range(4):
+        for l in range(j): inv[j][l] = conj(inv[l][j])
+    return inv
+
+
+def eliminate(rows, beams, lookahead=True):
+    shape = rows[0].shape
+    lane = lax.broadcasted_iota(jnp.int32, shape, 1)
+    upper = lax.broadcasted_iota(jnp.int32, shape, 0) < 4
+    sign = jnp.where(lane < beams, -1.0, 1.0)
+    def turn(x): return pltpu.roll(x, beams, 1) * sign
+    def col(x, k): return jnp.broadcast_to(x[:, k:k+1], shape)
+    rows = list(rows)
+    for k in range(0, beams, 4):
+        inside = ((lane >= k) & (lane < k + 4)) | ((lane >= beams + k) & (lane < beams + k + 4))
+        r = []
+        for q in (k // 2, k // 2 + 1):
+            x = rows[q]
+            y = pltpu.roll(x, 4, 0)
+            r += [jnp.where(upper, x, y), jnp.where(upper, y, x)]
+        e = [[None]*4 for _ in range(4)]
+        for j in range(4):
+            for l in range(j, 4):
+                e[j][l] = (col(r[j], k+l), col(r[j], beams+k+l) if l > j else None)
+        inv = inverse_four(e)
+        unit = [jnp.where(lane == k+l, 1.0, jnp.where(inside, 0.0, r[l])) for l in range(4)]
+        turned = [turn(x) for x in unit]
+        b, bt = [], []
+        for j in range(4):
+            acc, tacc = unit[j] * inv[j][j][0], turned[j] * inv[j][j][0]
+            for l in range(4):
+                if l != j:
+                    acc = acc + (unit[l] * inv[j][l][0] + turned[l] * inv[j][l][1])
+                    tacc = tacc + (turned[l] * inv[j][l][0] - unit[l] * inv[j][l][1])
+            b.append(acc)
+            bt.append(tacc)
+        for i in range(k//2+2, beams//2+1):
+            x = rows[i]
+            acc = jnp.where(inside, 0.0, x)
+            for l in range(4):
+                acc = acc - (col(x, k+l) * b[l] + col(x, beams+k+l) * bt[l])
+            rows[i] = acc
+    return rows[beams//2]
+
+
+def beams_body(side_ref, near_ref, far_ref, pulse_ref, steer_ref, own_ref, send_ref, rows_ref):
+    bins, total, gates = near_ref.shape
+    beams = total // 2
+    ranges = gates // own_ref.shape[2]
+    sums = [near_ref[d] + far_ref[d].astype(jnp.float32) for d in range(bins)]
     wide = jnp.concatenate(
-        [
-            jnp.concatenate(
-                [sums[d * 2 * beams : d * 2 * beams + beams], sums[d * 2 * beams + beams : (d + 1) * 2 * beams]],
-                axis=1,
-            )
-            for d in range(bins)
-        ],
-        axis=0,
+        [jnp.concatenate([value[:beams], value[beams:]], axis=1) for value in sums], axis=0
     )
     high, low = split(wide)
     pulse = pulse_ref[...]
@@ -268,7 +335,7 @@
     )
     sub = lax.broadcasted_iota(jnp.int32, (beams, 2 * beams), 0)
     lane = lax.broadcasted_iota(jnp.int32, (beams, 2 * beams), 1)
-    systems, rows, both = [], [], []
+    both = []
     for d in range(bins):
         real = formed[d * beams : (d + 1) * beams, :gates]
         imag = formed[d * beams : (d + 1) * beams, gates:]
@@ -284,26 +351,35 @@
         trace = jnp.sum(jnp.where(on_diagonal, cov, 0.0), axis=(0, 1), keepdims=True)
         loading = load_ratio * trace / beams + epsilon
         cov = jnp.where(on_diagonal, cov + loading, cov)
-        systems.append([cov[8 * v : 8 * v + 8] for v in range(beams // 8)])
-        rows.append(jnp.broadcast_to(steer_ref[d : d + 1, :], (8, 2 * beams)))
-    rows = eliminate(systems, rows)
-    own_side = side_ref[0] == 0
+        rows_ref[pl.ds(d, beams, stride=bins), :] = cov
+    steer = steer_ref[...]
+    rows = [rows_ref[8 * q : 8 * q + 8] for q in range(beams // 2)]
+    rows.append(jnp.concatenate([steer, steer], axis=0))
+    conj = -eliminate(rows, beams)[:bins]
+    response = jnp.sum(conj * steer, axis=1, keepdims=True)
+    weight = conj / response
+    w_high, w_low = split(weight)
+    first_side = side_ref[0] == 0
     half = gates // ranges
+    row = lax.broadcasted_iota(jnp.int32, (bins, half), 0)
+    outs = [jnp.zeros((bins, half), jnp.float32)] * (2 * ranges)
     for d in range(bins):
-        conj = -rows[d]
-        steer = jnp.broadcast_to(steer_ref[d : d + 1, :], (8, 2 * beams))
-        response = jnp.sum(conj * steer, axis=1, keepdims=True)
-        weight = conj / response
-        w_high, w_low = split(weight)
         g_high, g_low = both[d]
         out = jnp.dot(w_high, g_high, preferred_element_type=jnp.float32)
         out = out + jnp.dot(w_high, g_low, preferred_element_type=jnp.float32)
         out = out + jnp.dot(w_low, g_high, preferred_element_type=jnp.float32)
-        for part in range(2):
-            first = out[:1, part * gates : part * gates + half]
-            second = out[:1, part * gates + half : (part + 1) * gates]
-            own_ref[part, d : d + 1, :] = jnp.where(own_side, first, second)
-            send_ref[part, d : d + 1, :] = jnp.where(own_side, second, first)
+        outs = [
+            jnp.where(row == d, out[:, n * half : (n + 1) * half], kept) for n, kept in enumerate(outs)
+        ]
+    nothing = jnp.zeros((bins, half), jnp.float32)
+    for part in range(2):
+        first, second = outs[2 * part : 2 * part + 2]
+        own_ref[part] = jnp.concatenate(
+            [jnp.where(first_side, first, nothing), jnp.where(first_side, nothing, second)], axis=0
+        )
+        send_ref[part] = jnp.concatenate(
+            [jnp.where(first_side, second, nothing), jnp.where(first_side, nothing, first)], axis=0
+        )
 
 
 def on_device_owned(echoes, replica, beam_weights, steering):
@@ -311,28 +387,42 @@
     devices = elems * ranges
     _, own_elements, pulses, gate_count = echoes.shape
     bins = pulses // devices
-    beams = beam_weights.shape[1]
+    elements = beam_weights.shape[2]
     gates = gate_count * ranges
     side = lax.axis_index("range")
-    bound = lax.all_to_all(spectra(echoes, devices), ("elem", "range"), 0, 0, tiled=True)
-    bound = bound.reshape(elems, ranges, own_elements // 2, 4 * bins, gate_count)
+    half = lax.axis_index("elem") // (elems // 2)
+    group = devices // 2
+    owners = [part * group + member for member in range(group) for part in range(2)]
+    sent = spectra(echoes, owners).reshape(group, 2, own_elements // 2, 4 * bins, gate_count)
+    bound = lax.all_to_all(
+        sent,
+        ("elem", "range"),
+        0,
+        0,
+        tiled=True,
+        axis_index_groups=[list(range(group)), list(range(group, devices))],
+    )
+    bound = bound.reshape(elems // 2, ranges, 2, own_elements // 2, 4 * bins, gate_count)
+    here = lax.dynamic_slice_in_dim(beam_weights, half * (elements // 2), elements // 2, 2)
+    spread_weights = spread(here, bins)
+    crossing = partial_sums(1 - half, bound, spread_weights, bins, jnp.bfloat16)
+    far = lax.ppermute(crossing, "elem", [(n, (n + elems // 2) % elems) for n in range(elems)])
+    near = partial_sums(half, bound, spread_weights, bins, jnp.float32)
     pulse = pulse_kernel(replica, gates)[:, :, :gates]
     pulse = pulse.transpose(0, 2, 1, 3).reshape(2 * gates, 2 * gates)
     own_steering = lax.dynamic_slice_in_dim(steering, side * bins, bins, 1)
     steer_row = jnp.concatenate([own_steering[0], -own_steering[1]], axis=1)
-    shape = jax.ShapeDtypeStruct((2, bins, gate_count), jnp.float32)
+    shape = jax.ShapeDtypeStruct((2, 2 * bins, gate_count), jnp.float32)
     own, send = pl.pallas_call(
         beams_body,
         in_specs=[pl.BlockSpec(memory_space=pltpu.SMEM)] + whole_vmem(4),
         out_specs=whole_vmem(2),
         out_shape=[shape, shape],
-        compiler_params=pltpu.CompilerParams(vmem_limit_bytes=VMEM_BYTES),
+        scratch_shapes=[pltpu.VMEM((bins * beam_weights.shape[1], 2 * beam_weights.shape[1]), jnp.float32)],
+        compiler_params=pltpu.CompilerParams(vmem_limit_bytes=BEAMS_VMEM),
         name="beams",
-    )(side.reshape(1).astype(jnp.int32), bound, spread(beam_weights, bins), pulse, steer_row)
-    other = lax.ppermute(send, "range", [(0, 1), (1, 0)])
-    first = jnp.where(side == 0, own, other)
-    second = jnp.where(side == 0, other, own)
-    return jnp.concatenate([first, second], axis=1)
+    )(side.reshape(1).astype(jnp.int32), near, far, pulse, steer_row)
+    return own + lax.ppermute(send, "range", [(0, 1), (1, 0)])
 
 
 def on_device(echoes, replica, beam_weights, steering):
@@ -344,7 +434,8 @@
         and pulses == 4 * elems * ranges
         and gate_count % 128 == 0
         and beams == 64
-        and elements % 128 == 0
+        and elems % 2 == 0
+        and elements % 256 == 0
         and echoes.shape[1] % 8 == 0
         and replica.shape[1] <= gate_count
     )

time: 85 us -> 64.9 us (0.76)
  Pallas kernels: 26.1 us -> 13.4 us
  waiting for transfers between devices: 43.2 us -> 35.4 us
  starting transfers between devices: 8.74 us -> 11.7 us
  local copies, waits for them, and re-layouts: 4.54 us -> 2.41 us
    all_to_all x1, waiting for transfers between devices: 40.9 us -> 24.2 us  [on_device_owned(): lax.all_to_all(sent, ('elem', 'range'), 0, 0, tiled=True, axis_index_grou...]
    pallas_call x1, Pallas kernels: 17.9 us -> 6.57 us  [on_device_owned(): pl.pallas_call(beams_body, in_specs=[pl.BlockSpec(memory_space=pltpu.SMEM...]
    ppermute x1 -> x2, waiting for transfers between devices: 2.37 us -> 11.2 us  [the longest x1 9.58 us: on_device_owned(): lax.ppermute(crossing, 'elem', [(n, (n + elems // 2) % elems) for n in ra...]
    ppermute x1 -> x2, starting transfers between devices: 1.45 us -> 5.23 us  [the longest x1 2.64 us: on_device_owned(): return own + lax.ppermute(send, 'range', [(0, 1), (1, 0)])]
    pallas_call x1, Pallas kernels: 3.79 us -> 0.28 us  [spread(): pl.pallas_call(functools.partial(spread_body, bins=bins), in_specs=whole_...]
    unnamed x7 -> x11, local copies, waits for them, and re-layouts: 2.24 us -> 0.1 us
    pallas_call x0 -> x2, Pallas kernels: none -> 2.13 us  [partial_sums(): pl.pallas_call(functools.partial(partial_body, bins=bins), in_specs=[pl.B...]
    all_to_all x1, starting transfers between devices: 7.3 us -> 6.43 us  [on_device_owned(): lax.all_to_all(sent, ('elem', 'range'), 0, 0, tiled=True, axis_index_grou...]
  transfers between devices with their start and end apart: 2 -> 3, of which waited for: 2 -> 3; matrix products, arithmetic and copies ran while one was open for 5% -> 5% of each run, Pallas kernels for 4% -> 2%
where the time goes in v2:
time: 64.9 us; the launch traced here: 64.6 us
  waiting for transfers between devices  35.4 us (55%)
  Pallas kernels  13.4 us (21%)
  starting transfers between devices  11.7 us (18%)
  local copies, waits for them, and re-layouts  2.41 us (4%)
  other arithmetic  1.63 us (3%)
    all_to_all x1, waiting for transfers between devices, on_device_owned(): lax.all_to_all(sent, ('elem', 'range'), 0, 0, tiled=True, axis_index_grou...  24.2 us
    ppermute x1, waiting for transfers between devices, on_device_owned(): lax.ppermute(crossing, 'elem', [(n, (n + elems // 2) % elems) for n in ra...  9.58 us
    pallas_call x1, Pallas kernels, on_device_owned(): pl.pallas_call(beams_body, in_specs=[pl.BlockSpec(memory_space=pltpu.SMEM...  6.57 us
    all_to_all x1, starting transfers between devices, on_device_owned(): lax.all_to_all(sent, ('elem', 'range'), 0, 0, tiled=True, axis_index_grou...  6.43 us
    pallas_call x1, Pallas kernels, spectra(): pl.pallas_call(spectra_body, grid=(elements // block,), in_specs=[pl.Bloc...  4.39 us
    ppermute x1, starting transfers between devices, on_device_owned(): return own + lax.ppermute(send, 'range', [(0, 1), (1, 0)])  2.64 us
    ppermute x1, starting transfers between devices, on_device_owned(): lax.ppermute(crossing, 'elem', [(n, (n + elems // 2) % elems) for n in ra...  2.59 us
    pallas_call x2, Pallas kernels, partial_sums(): pl.pallas_call(functools.partial(partial_body, bins=bins), in_specs=[pl.B...  2.13 us
  transfers between devices with their start and end apart: 3, of which 3 were waited for; matrix products, arithmetic and copies ran while one was open for 5% of the time, Pallas kernels for 2%

profile of v2, /device:TPU:0, one launch (start us, length us, event | category | flops | bytes accessed | tf_op | source)
XLA Modules:
  0.0 64.6 jit_solution(3717817370787701019)
XLA Ops:
  0.0 0.0 copy-start
  0.0 4.4 %spectra.1 = bf16[32,16,16,128]{3,2,1,0:T(8,128)(2,1)} custom-call(bf16[256,256]{1,0:T(8,128)(2,1)} %constant.37.clone.table_ref, bf16[2,32,128,128]{3,2,1,0:T(8,128)(2,1)} %echo_ref.1), custom_call_target="tpu_custom_call" | custom-call | tf_op jit(solution)/shard_map/spectra/pallas_call | solution.py:151
  4.4 0.0 copy-start.4
  4.4 6.4 %all-to-all-start = ((bf16[16,2,16,16,128]{4,3,2,1,0:T(8,128)(2,1)}), bf16[16,2,16,16,128]{4,3,2,1,0:T(8,128)(2,1)S(1)}, u32[]{:S(2)}, u32[]{:S(2)}) async-start(bf16[16,2,16,16,128]{4,3,2,1,0:T(8,128)(2,1)} %bitcast.37), calls=%async_computation | async-start | bytes 4194304 | tf_op jit(solution)/shard_map/all_to_all | solution.py:397
  10.8 0.0 copy-done
  10.9 0.3 spread.1.spread_ref
  11.2 0.0 copy-done.4
  11.2 0.3 tile.21
  11.5 0.4 reshape.33
  11.9 0.1 copy.8
  12.1 0.3 tile.9
  12.4 0.4 reshape.32
  12.8 0.1 copy.7
  13.0 0.9 %maximum_bitcast_fusion = (bf16[1,2,319,256]{3,2,1,0:T(8,128)(2,1)}, bf16[1,2,319,256]{3,2,1,0:T(8,128)(2,1)}) fusion(bf16[1,319,256]{2,1,0:T(8,128)(2,1)S(1)} %bitcast.39, bf16[1,319,256]{2,1,0:T(8,128)(2,1)S(1)} %bitcast.41, bf16[1,319,256]{2,1,0:T(8,128)(2,1)S(1)} %fusion.1), kind=kLoop, calls=%fused_computation.2 | loop fusion | flops 326656 | bytes 1143296 | tf_op jit(solution)/shard_map/stack | solution.py:39
  13.9 24.2 %all-to-all-done = bf16[16,2,16,16,128]{4,3,2,1,0:T(8,128)(2,1)S(1)} async-done(((bf16[16,2,16,16,128]{4,3,2,1,0:T(8,128)(2,1)}), bf16[16,2,16,16,128]{4,3,2,1,0:T(8,128)(2,1)S(1)}, u32[]{:S(2)}, u32[]{:S(2)}) %all-to-all-start) | async-done | bytes 2097184 | tf_op jit(solution)/shard_map/all_to_all | solution.py:397
  38.1 0.0 copy-start.1
  38.1 0.0 copy-start.2
  38.1 1.4 %partial_sums.3 = bf16[4,128,256]{2,1,0:T(8,128)(2,1)} custom-call(s32[1]{0:T(128)} %bitcast.4.half_ref, bf16[8,2,2,16,16,128]{5,4,3,2,1,0:T(8,128)(2,1)S(1)} %bitcast.34, bf16[128,2048]{1,0:T(8,128)(2,1)S(1)} %spread.1.spread_ref), custom_call_target="tpu_custom_call" | custom-call | tf_op jit(solution)/shard_map/partial_sums/pallas_call | solution.py:218
  39.5 0.0 copy-start.3
  39.5 2.6 %collective-permute-start = (bf16[4,128,256]{2,1,0:T(8,128)(2,1)}, bf16[4,128,256]{2,1,0:T(8,128)(2,1)S(1)}, u32[]{:S(2)}, u32[]{:S(2)}) collective-permute-start(bf16[4,128,256]{2,1,0:T(8,128)(2,1)} %partial_sums.3), channel_id=1, source_target_pairs={{0,16},{2,18},{4,20},{6,22},{8,24},{10,26},{12,28},{14,30},{16,0},... | collective-permute-start | bytes 786440 | tf_op jit(solution)/shard_map/ppermute | solution.py:409
  42.1 0.0 copy-done.1
  42.1 0.0 copy-done.2
  42.2 0.5 copy.9
  42.7 0.1 copy.10
  42.8 0.0 copy-done.3
  42.8 0.1 pad_maximum_fusion.1.steer_ref
  42.9 0.7 %partial_sums.2.near_ref = f32[4,128,256]{2,1,0:T(8,128)S(1)} custom-call(s32[1]{0:T(128)} %bitcast.1.half_ref, bf16[8,2,2,16,16,128]{5,4,3,2,1,0:T(8,128)(2,1)S(1)} %bitcast.35, bf16[128,2048]{1,0:T(8,128)(2,1)S(1)} %spread.1.spread_ref), custom_call_target="tpu_custom_call" | custom-call | tf_op jit(solution)/shard_map/partial_sums/pallas_call | solution.py:218
  43.6 9.6 %collective-permute-done.far_ref = bf16[4,128,256]{2,1,0:T(8,128)(2,1)S(1)} collective-permute-done((bf16[4,128,256]{2,1,0:T(8,128)(2,1)}, bf16[4,128,256]{2,1,0:T(8,128)(2,1)S(1)}, u32[]{:S(2)}, u32[]{:S(2)}) %collective-permute-start) | collective-permute-done | bytes 262176 | tf_op jit(solution)/shard_map/ppermute | solution.py:409
  53.2 6.6 %beams.1 = (f32[2,8,128]{2,1,0:T(8,128)S(1)}, f32[2,8,128]{2,1,0:T(8,128)S(1)}) custom-call(s32[1]{0:T(128)} %bitcast.side_ref, f32[4,128,256]{2,1,0:T(8,128)S(1)} %partial_sums.2.near_ref, bf16[4,128,256]{2,1,0:T(8,128)(2,1)S(1)} %collective-permute-done.far_ref, bf16[512,512]{1,0:T(8,128)(2,1)S(1)} %bitcast.36, f32[4,128]{1,0:T(4,128)S(1)} %pad_maximum_fusion.1.steer_ref), custom_call_target="tpu_custom_call" | custom-call | tf_op jit(solution)/shard_map/beams/pallas_call | solution.py:416
  59.8 2.6 %collective-permute-start.1 = (f32[2,8,128]{2,1,0:T(8,128)S(1)}, f32[2,8,128]{2,1,0:T(8,128)S(1)}, u32[]{:S(2)}, u32[]{:S(2)}) collective-permute-start(f32[2,8,128]{2,1,0:T(8,128)S(1)} %get-tuple-element.8), channel_id=1, source_target_pairs={{0,1},{1,0},{2,3},{3,2},{4,5},{5,4},{6,7},{7,6},{8,9},{9,8},{10,11... | collective-permute-start | bytes 24584 | tf_op jit(solution)/shard_map/ppermute | solution.py:425
  62.4 1.6 %collective-permute-done.1 = f32[2,8,128]{2,1,0:T(8,128)S(1)} collective-permute-done((f32[2,8,128]{2,1,0:T(8,128)S(1)}, f32[2,8,128]{2,1,0:T(8,128)S(1)}, u32[]{:S(2)}, u32[]{:S(2)}) %collective-permute-start.1) | collective-permute-done | bytes 8224 | tf_op jit(solution)/shard_map/ppermute | solution.py:425
  64.0 0.6 add.16
  (9 shorter events, 0.1 us)
Async XLA Ops:
  0.0 10.9 %copy-start = (bf16[2,64,512]{2,1,0:T(8,128)(2,1)S(1)}, bf16[2,64,512]{2,1,0:T(8,128)(2,1)}, u32[]{:S(2)}) copy-start(bf16[2,64,512]{2,1,0:T(8,128)(2,1)} %param.7) | copy-start | bytes 393220
  4.4 6.8 %copy-start.4 = (bf16[2,64]{1,0:T(2,128)(2,1)S(1)}, bf16[2,64]{1,0:T(2,128)(2,1)}, u32[]{:S(2)}) copy-start(bf16[2,64]{1,0:T(2,128)(2,1)} %param.6) | copy-start | bytes 772
  4.4 33.7 %all-to-all-start = ((bf16[16,2,16,16,128]{4,3,2,1,0:T(8,128)(2,1)}), bf16[16,2,16,16,128]{4,3,2,1,0:T(8,128)(2,1)S(1)}, u32[]{:S(2)}, u32[]{:S(2)}) async-start(bf16[16,2,16,16,128]{4,3,2,1,0:T(8,128)(2,1)} %bitcast.37), calls=%async_computation | async-start | bytes 4194304 | tf_op jit(solution)/shard_map/all_to_all | solution.py:397
  38.1 4.0 %copy-start.1 = (bf16[1,2,319,256]{3,2,1,0:T(8,128)(2,1)S(1)}, bf16[1,2,319,256]{3,2,1,0:T(8,128)(2,1)}, u32[]{:S(2)}) copy-start(bf16[1,2,319,256]{3,2,1,0:T(8,128)(2,1)} %get-tuple-element.9) | copy-start | bytes 979972
  38.1 4.0 %copy-start.2 = (bf16[1,2,319,256]{3,2,1,0:T(8,128)(2,1)S(1)}, bf16[1,2,319,256]{3,2,1,0:T(8,128)(2,1)}, u32[]{:S(2)}) copy-start(bf16[1,2,319,256]{3,2,1,0:T(8,128)(2,1)} %get-tuple-element.10) | copy-start | bytes 979972
  39.5 3.3 %copy-start.3 = (f32[2,8,64]{2,1,0:T(8,128)S(1)}, f32[2,8,64]{2,1,0:T(8,128)}, u32[]{:S(2)}) copy-start(f32[2,8,64]{2,1,0:T(8,128)} %param.8) | copy-start | bytes 12292
  39.5 13.7 %collective-permute-start = (bf16[4,128,256]{2,1,0:T(8,128)(2,1)}, bf16[4,128,256]{2,1,0:T(8,128)(2,1)S(1)}, u32[]{:S(2)}, u32[]{:S(2)}) collective-permute-start(bf16[4,128,256]{2,1,0:T(8,128)(2,1)} %partial_sums.3), channel_id=1, source_target_pairs={{0,16},{2,18},{4,20},{6,22},{8,24},{10,26},{12,28},{14,30},{16,0},... | collective-permute-start | bytes 786440 | tf_op jit(solution)/shard_map/ppermute | solution.py:409
  59.8 4.3 %collective-permute-start.1 = (f32[2,8,128]{2,1,0:T(8,128)S(1)}, f32[2,8,128]{2,1,0:T(8,128)S(1)}, u32[]{:S(2)}, u32[]{:S(2)}) collective-permute-start(f32[2,8,128]{2,1,0:T(8,128)S(1)} %get-tuple-element.8), channel_id=1, source_target_pairs={{0,1},{1,0},{2,3},{3,2},{4,5},{5,4},{6,7},{7,6},{8,9},{9,8},{10,11... | collective-permute-start | bytes 24584 | tf_op jit(solution)/shard_map/ppermute | solution.py:425

commit v3 on v2

--- a/solution.py
+++ b/solution.py
@@ -11,6 +11,7 @@
 load_ratio = 0.1
 epsilon = 1e-06
 SPECTRA_VMEM = 56 << 20
+STEPS = 4
 SMALL_VMEM = 14 << 20
 BEAMS_VMEM = 24 << 20
 
@@ -122,44 +123,78 @@
     return [pl.BlockSpec(memory_space=pltpu.VMEM)] * count
 
 
-def spectra_body(table_ref, echo_ref, out_ref):
+def spectra_body(half_ref, table_hbm, echo_hbm, out_hbm, table_ref, echo_ref, out_ref, table_sem, in_sem, out_sem):
+    members = out_ref.shape[0]
+    gates = echo_ref.shape[3]
+    steps = in_sem.shape[0]
+    block = echo_ref.shape[1] // steps
+    pairs = block // 2
+    fetch_table = pltpu.make_async_copy(table_hbm.at[half_ref[0]], table_ref, table_sem)
+    fetches = [
+        pltpu.make_async_copy(
+            echo_hbm.at[:, pl.ds(step * block, block)],
+            echo_ref.at[:, pl.ds(step * block, block)],
+            in_sem.at[step],
+        )
+        for step in range(steps)
+    ]
+    stores = [
+        pltpu.make_async_copy(
+            out_ref.at[:, pl.ds(step * pairs, pairs)],
+            out_hbm.at[:, pl.ds(step * pairs, pairs)],
+            out_sem.at[step],
+        )
+        for step in range(steps)
+    ]
+    fetch_table.start()
+    for fetch in fetches:
+        fetch.start()
+    fetch_table.wait()
     table = table_ref[...]
-    owners = out_ref.shape[0]
-    gates = echo_ref.shape[3]
-    for pair in range(echo_ref.shape[1] // 2):
-        even, odd = 2 * pair, 2 * pair + 1
-        samples = jnp.concatenate(
-            [
-                jnp.concatenate([echo_ref[0, even], echo_ref[0, odd]], axis=1),
-                jnp.concatenate([echo_ref[1, even], echo_ref[1, odd]], axis=1),
-            ],
-            axis=0,
-        )
-        bins = jnp.dot(table, samples, preferred_element_type=jnp.float32)
-        bins = bins.reshape(owners, bins.shape[0] // owners, 2 * gates)
-        rows = jnp.concatenate([bins[:, :, :gates], bins[:, :, gates:]], axis=1)
-        out_ref[:, pair] = rows.astype(jnp.bfloat16)
-
-
-def spectra(echoes, owners, block=8):
+    for step in range(steps):
+        fetches[step].wait()
+        for pair in range(step * pairs, (step + 1) * pairs):
+            even, odd = 2 * pair, 2 * pair + 1
+            samples = jnp.concatenate(
+                [
+                    jnp.concatenate([echo_ref[0, even], echo_ref[0, odd]], axis=1),
+                    jnp.concatenate([echo_ref[1, even], echo_ref[1, odd]], axis=1),
+                ],
+                axis=0,
+            )
+            bins = jnp.dot(table, samples, preferred_element_type=jnp.float32)
+            bins = bins.reshape(members, bins.shape[0] // members, 2 * gates)
+            rows = jnp.concatenate([bins[:, :, :gates], bins[:, :, gates:]], axis=1)
+            out_ref[:, pair] = rows.astype(jnp.bfloat16)
+        stores[step].start()
+    for store in stores:
+        store.wait()
+
+
+def spectra(half, echoes, devices, steps=STEPS):
     _, elements, pulses, gates = echoes.shape
-    devices = len(owners)
     bins = pulses // devices
+    members = devices // 2
     table = doppler_table(pulses)
-    table = table.transpose(2, 1, 0, 3).reshape(devices, bins, 2, 2 * pulses)[np.asarray(owners)]
-    table = table.transpose(0, 2, 1, 3).reshape(2 * pulses, 2 * pulses)
+    table = table.transpose(2, 1, 0, 3).reshape(devices, bins, 2, 2 * pulses)
+    table = table.transpose(0, 2, 1, 3).reshape(2, pulses, 2 * pulses)
+    shape = (members, elements // 2, 4 * bins, gates)
     return pl.pallas_call(
         spectra_body,
-        grid=(elements // block,),
-        in_specs=[
-            pl.BlockSpec((2 * pulses, 2 * pulses), lambda i: (0, 0)),
-            pl.BlockSpec((2, block, pulses, gates), lambda i: (0, i, 0, 0)),
+        in_specs=[pl.BlockSpec(memory_space=pltpu.SMEM)] + [pl.BlockSpec(memory_space=pl.ANY)] * 2,
+        out_specs=pl.BlockSpec(memory_space=pl.ANY),
+        out_shape=jax.ShapeDtypeStruct(shape, jnp.bfloat16),
+        scratch_shapes=[
+            pltpu.VMEM((pulses, 2 * pulses), jnp.bfloat16),
+            pltpu.VMEM(echoes.shape, jnp.bfloat16),
+            pltpu.VMEM(shape, jnp.bfloat16),
+            pltpu.SemaphoreType.DMA(()),
+            pltpu.SemaphoreType.DMA((steps,)),
+            pltpu.SemaphoreType.DMA((steps,)),
         ],
-        out_specs=pl.BlockSpec((devices, block // 2, 4 * bins, gates), lambda i: (0, i, 0, 0)),
-        out_shape=jax.ShapeDtypeStruct((devices, elements // 2, 4 * bins, gates), jnp.bfloat16),
         compiler_params=pltpu.CompilerParams(vmem_limit_bytes=SPECTRA_VMEM),
         name="spectra",
-    )(jnp.asarray(table), echoes)
+    )(half.reshape(1).astype(jnp.int32), jnp.asarray(table), echoes)
 
 
 def spread_body(weight_ref, out_ref, *, bins):
@@ -193,14 +228,13 @@
     )(beam_weights)
 
 
-def partial_body(half_ref, spectra_ref, spread_ref, out_ref, *, bins):
+def partial_body(spectra_ref, spread_ref, out_ref, *, bins):
     elems, ranges = spectra_ref.shape[:2]
-    rows = spectra_ref.shape[3] * spectra_ref.shape[4]
-    half = half_ref[0]
+    rows = spectra_ref.shape[2] * spectra_ref.shape[3]
     received = jnp.concatenate(
         [
             jnp.concatenate(
-                [spectra_ref[n, j, half].reshape(rows, spectra_ref.shape[5]) for n in range(elems)], axis=0
+                [spectra_ref[n, j].reshape(rows, spectra_ref.shape[4]) for n in range(elems)], axis=0
             )
             for j in range(ranges)
         ],
@@ -213,16 +247,16 @@
         out_ref[d] = jnp.dot(here, received, preferred_element_type=jnp.float32).astype(out_ref.dtype)
 
 
-def partial_sums(half, bound, spread_weights, bins, dtype):
-    shape = (bins, spread_weights.shape[0], bound.shape[1] * bound.shape[5])
+def partial_sums(bound, spread_weights, bins, dtype):
+    shape = (bins, spread_weights.shape[0], bound.shape[1] * bound.shape[4])
     return pl.pallas_call(
         functools.partial(partial_body, bins=bins),
-        in_specs=[pl.BlockSpec(memory_space=pltpu.SMEM)] + whole_vmem(2),
+        in_specs=whole_vmem(2),
         out_specs=whole_vmem(1)[0],
         out_shape=jax.ShapeDtypeStruct(shape, dtype),
         compiler_params=pltpu.CompilerParams(vmem_limit_bytes=BEAMS_VMEM),
         name="partial_sums",
-    )(half.reshape(1).astype(jnp.int32), bound, spread_weights)
+    )(bound, spread_weights)
 
 
 def split(value):
@@ -392,22 +426,18 @@
     side = lax.axis_index("range")
     half = lax.axis_index("elem") // (elems // 2)
     group = devices // 2
-    owners = [part * group + member for member in range(group) for part in range(2)]
-    sent = spectra(echoes, owners).reshape(group, 2, own_elements // 2, 4 * bins, gate_count)
-    bound = lax.all_to_all(
-        sent,
-        ("elem", "range"),
-        0,
-        0,
-        tiled=True,
-        axis_index_groups=[list(range(group)), list(range(group, devices))],
-    )
-    bound = bound.reshape(elems // 2, ranges, 2, own_elements // 2, 4 * bins, gate_count)
+    groups = [list(range(group)), list(range(group, devices))]
+
+    def gathered(owner_half):
+        sent = spectra(owner_half, echoes, devices)
+        bound = lax.all_to_all(sent, ("elem", "range"), 0, 0, tiled=True, axis_index_groups=groups)
+        return bound.reshape(elems // 2, ranges, own_elements // 2, 4 * bins, gate_count)
+
     here = lax.dynamic_slice_in_dim(beam_weights, half * (elements // 2), elements // 2, 2)
     spread_weights = spread(here, bins)
-    crossing = partial_sums(1 - half, bound, spread_weights, bins, jnp.bfloat16)
+    crossing = partial_sums(gathered(1 - half), spread_weights, bins, jnp.bfloat16)
     far = lax.ppermute(crossing, "elem", [(n, (n + elems // 2) % elems) for n in range(elems)])
-    near = partial_sums(half, bound, spread_weights, bins, jnp.float32)
+    near = partial_sums(gathered(half), spread_weights, bins, jnp.float32)
     pulse = pulse_kernel(replica, gates)[:, :, :gates]
     pulse = pulse.transpose(0, 2, 1, 3).reshape(2 * gates, 2 * gates)
     own_steering = lax.dynamic_slice_in_dim(steering, side * bins, bins, 1)

time: 64.9 us -> 60.3 us (0.929)
  waiting for transfers between devices: 35.4 us -> 28 us
  starting transfers between devices: 11.7 us -> 14.1 us
  Pallas kernels: 13.4 us -> 14.4 us
  other arithmetic: 1.63 us -> 0.79 us
    ppermute x1, waiting for transfers between devices: 9.58 us -> 0.01 us  [on_device_owned(): lax.ppermute(crossing, 'elem', [(n, (n + elems // 2) % elems) for n in ra...]
    all_to_all x1 -> x2, starting transfers between devices: 6.43 us -> 10 us  [gathered(): lax.all_to_all(sent, ('elem', 'range'), 0, 0, tiled=True, axis_index_grou...]
    all_to_all x1 -> x2, waiting for transfers between devices: 24.2 us -> 25.7 us  [gathered(): lax.all_to_all(sent, ('elem', 'range'), 0, 0, tiled=True, axis_index_grou...]
    ppermute x1, starting transfers between devices: 2.64 us -> 1.45 us  [on_device_owned(): return own + lax.ppermute(send, 'range', [(0, 1), (1, 0)])]
    pallas_call x3 -> x4, Pallas kernels: 6.51 us -> 7.61 us  [the longest x2 6.18 us: spectra(): pl.pallas_call(spectra_body, in_specs=[pl.BlockSpec(memory_space=pltpu.SM...]
    another operation x1, other arithmetic: 0.9 us -> 0.05 us  [pulse_kernel(): jnp.stack([jnp.stack([real_part, imag_part]), jnp.stack([-imag_part, real...]
  transfers between devices with their start and end apart: 3 -> 4, of which waited for: 3 -> 3; matrix products, arithmetic and copies ran while one was open for 5% -> 4% of each run, Pallas kernels for 2% -> 8%
where the time goes in v3:
time: 60.3 us; the launch traced here: 59.9 us
  waiting for transfers between devices  28 us (46%)
  Pallas kernels  14.4 us (24%)
  starting transfers between devices  14.1 us (23%)
  local copies, waits for them, and re-layouts  2.41 us (4%)
  other arithmetic  0.79 us (1%)
    all_to_all x2, waiting for transfers between devices, gathered(): lax.all_to_all(sent, ('elem', 'range'), 0, 0, tiled=True, axis_index_grou...  25.7 us
    all_to_all x2, starting transfers between devices, gathered(): lax.all_to_all(sent, ('elem', 'range'), 0, 0, tiled=True, axis_index_grou...  10 us
    pallas_call x1, Pallas kernels, on_device_owned(): pl.pallas_call(beams_body, in_specs=[pl.BlockSpec(memory_space=pltpu.SMEM...  6.56 us
    pallas_call x2, Pallas kernels, spectra(): pl.pallas_call(spectra_body, in_specs=[pl.BlockSpec(memory_space=pltpu.SM...  6.18 us
    ppermute x1, starting transfers between devices, on_device_owned(): lax.ppermute(crossing, 'elem', [(n, (n + elems // 2) % elems) for n in ra...  2.65 us
    ppermute x1, waiting for transfers between devices, on_device_owned(): return own + lax.ppermute(send, 'range', [(0, 1), (1, 0)])  2.21 us
    ppermute x1, starting transfers between devices, on_device_owned(): return own + lax.ppermute(send, 'range', [(0, 1), (1, 0)])  1.45 us
    pallas_call x2, Pallas kernels, partial_sums(): pl.pallas_call(functools.partial(partial_body, bins=bins), in_specs=whole...  1.43 us
  transfers between devices with their start and end apart: 4, of which 3 were waited for; matrix products, arithmetic and copies ran while one was open for 4% of the time, Pallas kernels for 8%

profile of v3, /device:TPU:0, one launch (start us, length us, event | category | flops | bytes accessed | tf_op | source)
XLA Modules:
  0.0 59.9 jit_solution(1375623817413089971)
XLA Ops:
  0.0 0.0 copy-start
  0.0 3.1 %spectra.3 = bf16[16,16,16,128]{3,2,1,0:T(8,128)(2,1)} custom-call(s32[1]{0:T(128)} %bitcast.3.half_ref, bf16[2,128,256]{2,1,0:T(8,128)(2,1)} %constant.37.clone.table_hbm, bf16[2,32,128,128]{3,2,1,0:T(8,128)(2,1)} %echo_hbm.3), custom_call_target="tpu_custom_call" | custom-call | tf_op jit(solution)/shard_map/spectra/pallas_call | solution.py:182
  3.1 6.3 %all-to-all-start.1 = ((bf16[16,16,16,128]{3,2,1,0:T(8,128)(2,1)}), bf16[16,16,16,128]{3,2,1,0:T(8,128)(2,1)S(1)}, u32[]{:S(2)}, u32[]{:S(2)}) async-start(bf16[16,16,16,128]{3,2,1,0:T(8,128)(2,1)} %spectra.3), calls=%async_computation.1 | async-start | bytes 2097152 | tf_op jit(solution)/shard_map/all_to_all | solution.py:433
  9.4 3.1 %spectra.2 = bf16[16,16,16,128]{3,2,1,0:T(8,128)(2,1)} custom-call(s32[1]{0:T(128)} %bitcast.1.half_ref, bf16[2,128,256]{2,1,0:T(8,128)(2,1)} %constant.37.clone.table_hbm, bf16[2,32,128,128]{3,2,1,0:T(8,128)(2,1)} %echo_hbm.3), custom_call_target="tpu_custom_call" | custom-call | tf_op jit(solution)/shard_map/spectra/pallas_call | solution.py:182
  12.5 0.0 copy-start.2
  12.5 11.7 %all-to-all-done.1 = bf16[16,16,16,128]{3,2,1,0:T(8,128)(2,1)S(1)} async-done(((bf16[16,16,16,128]{3,2,1,0:T(8,128)(2,1)}), bf16[16,16,16,128]{3,2,1,0:T(8,128)(2,1)S(1)}, u32[]{:S(2)}, u32[]{:S(2)}) %all-to-all-start.1) | async-done | bytes 1048608 | tf_op jit(solution)/shard_map/all_to_all | solution.py:433
  24.2 3.7 %all-to-all-start = ((bf16[16,16,16,128]{3,2,1,0:T(8,128)(2,1)}), bf16[16,16,16,128]{3,2,1,0:T(8,128)(2,1)S(1)}, u32[]{:S(2)}, u32[]{:S(2)}) async-start(bf16[16,16,16,128]{3,2,1,0:T(8,128)(2,1)} %spectra.2), calls=%async_computation | async-start | bytes 2097152 | tf_op jit(solution)/shard_map/all_to_all | solution.py:433
  28.0 0.0 copy-done
  28.0 0.3 spread.1.spread_ref
  28.3 0.0 copy-done.2
  28.3 0.3 tile.21
  28.6 0.4 reshape.33
  29.1 0.1 copy.9
  29.2 0.3 tile.9
  29.5 0.4 reshape.32
  29.9 0.1 copy.8
  30.1 0.1 maximum_bitcast_fusion
  30.2 0.7 %partial_sums.3 = bf16[4,128,256]{2,1,0:T(8,128)(2,1)S(1)} custom-call(bf16[8,2,16,16,128]{4,3,2,1,0:T(8,128)(2,1)S(1)} %bitcast.34, bf16[128,2048]{1,0:T(8,128)(2,1)S(1)} %spread.1.spread_ref), custom_call_target="tpu_custom_call" | custom-call | tf_op jit(solution)/shard_map/partial_sums/pallas_call | solution.py:252
  30.9 0.0 copy-start.1
  30.9 2.7 %collective-permute-start = (bf16[4,128,256]{2,1,0:T(8,128)(2,1)S(1)}, bf16[4,128,256]{2,1,0:T(8,128)(2,1)S(1)}, u32[]{:S(2)}, u32[]{:S(2)}) collective-permute-start(bf16[4,128,256]{2,1,0:T(8,128)(2,1)S(1)} %partial_sums.3), channel_id=1, source_target_pairs={{0,16},{2,18},{4,20},{6,22},{8,24},{10,26},{12,28},{14,30},{16,0},... | collective-permute-start | bytes 786440 | tf_op jit(solution)/shard_map/ppermute | solution.py:439
  33.6 0.5 copy.10
  34.1 0.1 copy.11
  34.2 0.0 copy-done.1
  34.3 0.1 pad_maximum_fusion.1.steer_ref
  34.3 14.0 %all-to-all-done = bf16[16,16,16,128]{3,2,1,0:T(8,128)(2,1)S(1)} async-done(((bf16[16,16,16,128]{3,2,1,0:T(8,128)(2,1)}), bf16[16,16,16,128]{3,2,1,0:T(8,128)(2,1)S(1)}, u32[]{:S(2)}, u32[]{:S(2)}) %all-to-all-start) | async-done | bytes 1048608 | tf_op jit(solution)/shard_map/all_to_all | solution.py:433
  48.4 0.7 %partial_sums.2.near_ref = f32[4,128,256]{2,1,0:T(8,128)S(1)} custom-call(bf16[8,2,16,16,128]{4,3,2,1,0:T(8,128)(2,1)S(1)} %bitcast.35, bf16[128,2048]{1,0:T(8,128)(2,1)S(1)} %spread.1.spread_ref), custom_call_target="tpu_custom_call" | custom-call | tf_op jit(solution)/shard_map/partial_sums/pallas_call | solution.py:252
  49.1 0.0 collective-permute-done.far_ref
  49.1 6.6 %beams.1 = (f32[2,8,128]{2,1,0:T(8,128)S(1)}, f32[2,8,128]{2,1,0:T(8,128)S(1)}) custom-call(s32[1]{0:T(128)} %bitcast.side_ref, f32[4,128,256]{2,1,0:T(8,128)S(1)} %partial_sums.2.near_ref, bf16[4,128,256]{2,1,0:T(8,128)(2,1)S(1)} %collective-permute-done.far_ref, bf16[512,512]{1,0:T(8,128)(2,1)S(1)} %bitcast.36, f32[4,128]{1,0:T(4,128)S(1)} %pad_maximum_fusion.1.steer_ref), custom_call_target="tpu_custom_call" | custom-call | tf_op jit(solution)/shard_map/beams/pallas_call | solution.py:446
  55.7 1.5 %collective-permute-start.1 = (f32[2,8,128]{2,1,0:T(8,128)S(1)}, f32[2,8,128]{2,1,0:T(8,128)S(1)}, u32[]{:S(2)}, u32[]{:S(2)}) collective-permute-start(f32[2,8,128]{2,1,0:T(8,128)S(1)} %get-tuple-element.8), channel_id=1, source_target_pairs={{0,1},{1,0},{2,3},{3,2},{4,5},{5,4},{6,7},{7,6},{8,9},{9,8},{10,11... | collective-permute-start | bytes 24584 | tf_op jit(solution)/shard_map/ppermute | solution.py:455
  57.1 2.2 %collective-permute-done.1 = f32[2,8,128]{2,1,0:T(8,128)S(1)} collective-permute-done((f32[2,8,128]{2,1,0:T(8,128)S(1)}, f32[2,8,128]{2,1,0:T(8,128)S(1)}, u32[]{:S(2)}, u32[]{:S(2)}) %collective-permute-start.1) | collective-permute-done | bytes 8224 | tf_op jit(solution)/shard_map/ppermute | solution.py:455
  59.3 0.6 %add.16 = f32[2,8,128]{2,1,0:T(8,128)} add(f32[2,8,128]{2,1,0:T(8,128)S(1)} %get-tuple-element.7, f32[2,8,128]{2,1,0:T(8,128)S(1)} %collective-permute-done.1) | non-fusion elementwise | flops 2048 | bytes 24576 | tf_op jit(solution)/shard_map/add | solution.py:455
  (9 shorter events, 0.1 us)
Async XLA Ops:
  0.0 28.0 %copy-start = (bf16[2,64,512]{2,1,0:T(8,128)(2,1)S(1)}, bf16[2,64,512]{2,1,0:T(8,128)(2,1)}, u32[]{:S(2)}) copy-start(bf16[2,64,512]{2,1,0:T(8,128)(2,1)} %param.8) | copy-start | bytes 393220
  3.1 21.1 %all-to-all-start.1 = ((bf16[16,16,16,128]{3,2,1,0:T(8,128)(2,1)}), bf16[16,16,16,128]{3,2,1,0:T(8,128)(2,1)S(1)}, u32[]{:S(2)}, u32[]{:S(2)}) async-start(bf16[16,16,16,128]{3,2,1,0:T(8,128)(2,1)} %spectra.3), calls=%async_computation.1 | async-start | bytes 2097152 | tf_op jit(solution)/shard_map/all_to_all | solution.py:433
  12.5 15.8 %copy-start.2 = (bf16[2,64]{1,0:T(2,128)(2,1)S(1)}, bf16[2,64]{1,0:T(2,128)(2,1)}, u32[]{:S(2)}) copy-start(bf16[2,64]{1,0:T(2,128)(2,1)} %param.7) | copy-start | bytes 772
  24.2 24.1 %all-to-all-start = ((bf16[16,16,16,128]{3,2,1,0:T(8,128)(2,1)}), bf16[16,16,16,128]{3,2,1,0:T(8,128)(2,1)S(1)}, u32[]{:S(2)}, u32[]{:S(2)}) async-start(bf16[16,16,16,128]{3,2,1,0:T(8,128)(2,1)} %spectra.2), calls=%async_computation | async-start | bytes 2097152 | tf_op jit(solution)/shard_map/all_to_all | solution.py:433
  30.9 3.4 %copy-start.1 = (f32[2,8,64]{2,1,0:T(8,128)S(1)}, f32[2,8,64]{2,1,0:T(8,128)}, u32[]{:S(2)}) copy-start(f32[2,8,64]{2,1,0:T(8,128)} %param.9) | copy-start | bytes 12292
  30.9 18.2 %collective-permute-start = (bf16[4,128,256]{2,1,0:T(8,128)(2,1)S(1)}, bf16[4,128,256]{2,1,0:T(8,128)(2,1)S(1)}, u32[]{:S(2)}, u32[]{:S(2)}) collective-permute-start(bf16[4,128,256]{2,1,0:T(8,128)(2,1)S(1)} %partial_sums.3), channel_id=1, source_target_pairs={{0,16},{2,18},{4,20},{6,22},{8,24},{10,26},{12,28},{14,30},{16,0},... | collective-permute-start | bytes 786440 | tf_op jit(solution)/shard_map/ppermute | solution.py:439
  55.7 3.7 %collective-permute-start.1 = (f32[2,8,128]{2,1,0:T(8,128)S(1)}, f32[2,8,128]{2,1,0:T(8,128)S(1)}, u32[]{:S(2)}, u32[]{:S(2)}) collective-permute-start(f32[2,8,128]{2,1,0:T(8,128)S(1)} %get-tuple-element.8), channel_id=1, source_target_pairs={{0,1},{1,0},{2,3},{3,2},{4,5},{5,4},{6,7},{7,6},{8,9},{9,8},{10,11... | collective-permute-start | bytes 24584 | tf_op jit(solution)/shard_map/ppermute | solution.py:455

commit v4 on v3

--- a/solution.py
+++ b/solution.py
@@ -11,7 +11,8 @@
 load_ratio = 0.1
 epsilon = 1e-06
 SPECTRA_VMEM = 56 << 20
-STEPS = 4
+STEPS = 2
+BLOCK = 16
 SMALL_VMEM = 14 << 20
 BEAMS_VMEM = 24 << 20
 
@@ -228,7 +229,7 @@
     )(beam_weights)
 
 
-def partial_body(spectra_ref, spread_ref, out_ref, *, bins):
+def beam_sums(spectra_ref, spread_ref, bins):
     elems, ranges = spectra_ref.shape[:2]
     rows = spectra_ref.shape[2] * spectra_ref.shape[3]
     received = jnp.concatenate(
@@ -242,15 +243,25 @@
     )
     weights = spread_ref[...]
     own = lax.broadcasted_iota(jnp.int32, weights.shape, 1) % bins
-    for d in range(bins):
-        here = jnp.where(own == d, weights, jnp.zeros_like(weights))
-        out_ref[d] = jnp.dot(here, received, preferred_element_type=jnp.float32).astype(out_ref.dtype)
+    return [
+        jnp.dot(
+            jnp.where(own == d, weights, jnp.zeros_like(weights)),
+            received,
+            preferred_element_type=jnp.float32,
+        )
+        for d in range(bins)
+    ]
+
+
+def partial_body(spectra_ref, spread_ref, out_ref):
+    for d, value in enumerate(beam_sums(spectra_ref, spread_ref, out_ref.shape[0])):
+        out_ref[d] = value.astype(out_ref.dtype)
 
 
 def partial_sums(bound, spread_weights, bins, dtype):
     shape = (bins, spread_weights.shape[0], bound.shape[1] * bound.shape[4])
     return pl.pallas_call(
-        functools.partial(partial_body, bins=bins),
+        partial_body,
         in_specs=whole_vmem(2),
         out_specs=whole_vmem(1)[0],
         out_shape=jax.ShapeDtypeStruct(shape, dtype),
@@ -314,27 +325,35 @@
     return inv
 
 
-def eliminate(rows, beams, lookahead=True):
+def turn(x):
+    half = x.shape[1] // 2
+    lane = lax.broadcasted_iota(jnp.int32, x.shape, 1)
+    y = pltpu.roll(x, half, 1)
+    return jnp.where(lane < half, -y, y)
+
+
+def sweep(rows, columns, updated):
     shape = rows[0].shape
+    beams = shape[1] // 2
     lane = lax.broadcasted_iota(jnp.int32, shape, 1)
     upper = lax.broadcasted_iota(jnp.int32, shape, 0) < 4
-    sign = jnp.where(lane < beams, -1.0, 1.0)
-    def turn(x): return pltpu.roll(x, beams, 1) * sign
-    def col(x, k): return jnp.broadcast_to(x[:, k:k+1], shape)
-    rows = list(rows)
-    for k in range(0, beams, 4):
+
+    def col(x, k):
+        return jnp.broadcast_to(x[:, k : k + 1], shape)
+
+    for step, k in enumerate(columns):
         inside = ((lane >= k) & (lane < k + 4)) | ((lane >= beams + k) & (lane < beams + k + 4))
-        r = []
-        for q in (k // 2, k // 2 + 1):
+        pivot = []
+        for q in (2 * step, 2 * step + 1):
             x = rows[q]
             y = pltpu.roll(x, 4, 0)
-            r += [jnp.where(upper, x, y), jnp.where(upper, y, x)]
-        e = [[None]*4 for _ in range(4)]
+            pivot += [jnp.where(upper, x, y), jnp.where(upper, y, x)]
+        entry = [[None] * 4 for _ in range(4)]
         for j in range(4):
             for l in range(j, 4):
-                e[j][l] = (col(r[j], k+l), col(r[j], beams+k+l) if l > j else None)
-        inv = inverse_four(e)
-        unit = [jnp.where(lane == k+l, 1.0, jnp.where(inside, 0.0, r[l])) for l in range(4)]
+                entry[j][l] = (col(pivot[j], k + l), col(pivot[j], beams + k + l) if l > j else None)
+        inv = inverse_four(entry)
+        unit = [jnp.where(lane == k + l, 1.0, jnp.where(inside, 0.0, pivot[l])) for l in range(4)]
         turned = [turn(x) for x in unit]
         b, bt = [], []
         for j in range(4):
@@ -345,20 +364,59 @@
                     tacc = tacc + (turned[l] * inv[j][l][0] - unit[l] * inv[j][l][1])
             b.append(acc)
             bt.append(tacc)
-        for i in range(k//2+2, beams//2+1):
-            x = rows[i]
+        for q in updated(step):
+            x = rows[q]
             acc = jnp.where(inside, 0.0, x)
             for l in range(4):
-                acc = acc - (col(x, k+l) * b[l] + col(x, beams+k+l) * bt[l])
-            rows[i] = acc
-    return rows[beams//2]
-
-
-def beams_body(side_ref, near_ref, far_ref, pulse_ref, steer_ref, own_ref, send_ref, rows_ref):
-    bins, total, gates = near_ref.shape
+                acc = acc - (col(x, k + l) * b[l] + col(x, beams + k + l) * bt[l])
+            rows[q] = acc
+        for q in (0, 1):
+            rows[2 * step + q] = jnp.where(upper, b[2 * q], b[2 * q + 1])
+    return rows
+
+
+def eliminate(systems, sources, rows_ref, size=BLOCK):
+    count = len(systems)
+    beams = systems[0].shape[0]
+    blocks = size // 2
+    rest = [
+        jnp.concatenate([systems[n], jnp.broadcast_to(sources[n], (8, 2 * beams))], axis=0) for n in range(count)
+    ]
+    for first in range(0, beams, size):
+        base = count * first
+        for n in range(count):
+            rows_ref[pl.ds(base + n, size, stride=count), :] = rest[n][:size]
+        rows = [rows_ref[base + 8 * q : base + 8 * q + 8] for q in range(blocks)]
+        columns = range(first, first + size, 4)
+        if first + size == beams:
+            bottoms = [value[size : size + 1] for value in rest]
+            rows.append(jnp.concatenate(bottoms + bottoms, axis=0))
+            return sweep(rows, columns, lambda step: range(2 * step + 2, blocks + 1))[blocks]
+        rows = sweep(rows, columns, lambda step: [q for q in range(blocks) if q // 2 != step])
+        for q in range(blocks):
+            rows_ref[base + 8 * q : base + 8 * q + 8] = rows[q]
+        for n in range(count):
+            top = rows_ref[pl.ds(base + n, size, stride=count), :]
+            before = [jnp.zeros((first, 2 * beams), jnp.float32)] * (first > 0)
+            after = [jnp.zeros((beams - first - size, 2 * beams), jnp.float32)]
+            high, low = split(jnp.concatenate(before + [top] + after + before + [turn(top)] + after, axis=0))
+            value = rest[n][size:]
+            v_high, v_low = split(value)
+            taken = jnp.dot(v_high, high, preferred_element_type=jnp.float32)
+            taken = taken + jnp.dot(v_high, low, preferred_element_type=jnp.float32)
+            taken = taken + jnp.dot(v_low, high, preferred_element_type=jnp.float32)
+            at = lax.broadcasted_iota(jnp.int32, value.shape, 1) % beams
+            rest[n] = jnp.where((at >= first) & (at < first + size), 0.0, value) - taken
+
+
+def beams_body(
+    side_ref, spectra_ref, spread_ref, far_ref, pulse_ref, steer_ref, own_ref, send_ref, rows_ref
+):
+    bins, total, gates = far_ref.shape
     beams = total // 2
     ranges = gates // own_ref.shape[2]
-    sums = [near_ref[d] + far_ref[d].astype(jnp.float32) for d in range(bins)]
+    near = beam_sums(spectra_ref, spread_ref, bins)
+    sums = [near[d] + far_ref[d].astype(jnp.float32) for d in range(bins)]
     wide = jnp.concatenate(
         [jnp.concatenate([value[:beams], value[beams:]], axis=1) for value in sums], axis=0
     )
@@ -369,7 +427,7 @@
     )
     sub = lax.broadcasted_iota(jnp.int32, (beams, 2 * beams), 0)
     lane = lax.broadcasted_iota(jnp.int32, (beams, 2 * beams), 1)
-    both = []
+    both, systems = [], []
     for d in range(bins):
         real = formed[d * beams : (d + 1) * beams, :gates]
         imag = formed[d * beams : (d + 1) * beams, gates:]
@@ -385,11 +443,10 @@
         trace = jnp.sum(jnp.where(on_diagonal, cov, 0.0), axis=(0, 1), keepdims=True)
         loading = load_ratio * trace / beams + epsilon
         cov = jnp.where(on_diagonal, cov + loading, cov)
-        rows_ref[pl.ds(d, beams, stride=bins), :] = cov
+        systems.append(cov)
     steer = steer_ref[...]
-    rows = [rows_ref[8 * q : 8 * q + 8] for q in range(beams // 2)]
-    rows.append(jnp.concatenate([steer, steer], axis=0))
-    conj = -eliminate(rows, beams)[:bins]
+    sources = [steer[d : d + 1] for d in range(bins)]
+    conj = -eliminate(systems, sources, rows_ref)[:bins]
     response = jnp.sum(conj * steer, axis=1, keepdims=True)
     weight = conj / response
     w_high, w_low = split(weight)
@@ -437,7 +494,7 @@
     spread_weights = spread(here, bins)
     crossing = partial_sums(gathered(1 - half), spread_weights, bins, jnp.bfloat16)
     far = lax.ppermute(crossing, "elem", [(n, (n + elems // 2) % elems) for n in range(elems)])
-    near = partial_sums(gathered(half), spread_weights, bins, jnp.float32)
+    near = gathered(half)
     pulse = pulse_kernel(replica, gates)[:, :, :gates]
     pulse = pulse.transpose(0, 2, 1, 3).reshape(2 * gates, 2 * gates)
     own_steering = lax.dynamic_slice_in_dim(steering, side * bins, bins, 1)
@@ -445,13 +502,13 @@
     shape = jax.ShapeDtypeStruct((2, 2 * bins, gate_count), jnp.float32)
     own, send = pl.pallas_call(
         beams_body,
-        in_specs=[pl.BlockSpec(memory_space=pltpu.SMEM)] + whole_vmem(4),
+        in_specs=[pl.BlockSpec(memory_space=pltpu.SMEM)] + whole_vmem(5),
         out_specs=whole_vmem(2),
         out_shape=[shape, shape],
         scratch_shapes=[pltpu.VMEM((bins * beam_weights.shape[1], 2 * beam_weights.shape[1]), jnp.float32)],
         compiler_params=pltpu.CompilerParams(vmem_limit_bytes=BEAMS_VMEM),
         name="beams",
-    )(side.reshape(1).astype(jnp.int32), near, far, pulse, steer_row)
+    )(side.reshape(1).astype(jnp.int32), near, spread_weights, far, pulse, steer_row)
     return own + lax.ppermute(send, "range", [(0, 1), (1, 0)])
 
 

time: 60.3 us -> 58.7 us (0.973)
  the two profiles are of different devices: /device:TPU:0 before, /device:TPU:8 now
where the time goes in v4:
time: 58.7 us; the launch traced here: 57.9 us
  waiting for transfers between devices  27.1 us (46%)
  starting transfers between devices  14.9 us (25%)
  Pallas kernels  12.5 us (21%)
  local copies, waits for them, and re-layouts  2.41 us (4%)
  other arithmetic  0.79 us (1%)
    all_to_all x2, waiting for transfers between devices, gathered(): lax.all_to_all(sent, ('elem', 'range'), 0, 0, tiled=True, axis_index_grou...  22 us
    all_to_all x2, starting transfers between devices, gathered(): lax.all_to_all(sent, ('elem', 'range'), 0, 0, tiled=True, axis_index_grou...  10.3 us
    pallas_call x1, Pallas kernels, on_device_owned(): pl.pallas_call(beams_body, in_specs=[pl.BlockSpec(memory_space=pltpu.SMEM...  6.03 us
    pallas_call x2, Pallas kernels, spectra(): pl.pallas_call(spectra_body, in_specs=[pl.BlockSpec(memory_space=pltpu.SM...  5.5 us
    ppermute x1, waiting for transfers between devices, on_device_owned(): lax.ppermute(crossing, 'elem', [(n, (n + elems // 2) % elems) for n in ra...  3.39 us
    ppermute x1, starting transfers between devices, on_device_owned(): lax.ppermute(crossing, 'elem', [(n, (n + elems // 2) % elems) for n in ra...  2.65 us
    ppermute x1, starting transfers between devices, on_device_owned(): return own + lax.ppermute(send, 'range', [(0, 1), (1, 0)])  2 us
    ppermute x1, waiting for transfers between devices, on_device_owned(): return own + lax.ppermute(send, 'range', [(0, 1), (1, 0)])  1.67 us
  transfers between devices with their start and end apart: 4, of which 4 were waited for; matrix products, arithmetic and copies ran while one was open for 4% of the time, Pallas kernels for 6%

profile of v4, /device:TPU:8, one launch (start us, length us, event | category | flops | bytes accessed | tf_op | source)
XLA Modules:
  0.0 57.9 jit_solution(11312076450120515277)
XLA Ops:
  0.0 0.0 copy-start
  0.0 2.8 %spectra.3 = bf16[16,16,16,128]{3,2,1,0:T(8,128)(2,1)} custom-call(s32[1]{0:T(128)} %bitcast.3.half_ref, bf16[2,128,256]{2,1,0:T(8,128)(2,1)} %constant.37.clone.table_hbm, bf16[2,32,128,128]{3,2,1,0:T(8,128)(2,1)} %echo_hbm.3), custom_call_target="tpu_custom_call" | custom-call | tf_op jit(solution)/shard_map/spectra/pallas_call | solution.py:183
  2.8 5.2 %all-to-all-start.1 = ((bf16[16,16,16,128]{3,2,1,0:T(8,128)(2,1)}), bf16[16,16,16,128]{3,2,1,0:T(8,128)(2,1)S(1)}, u32[]{:S(2)}, u32[]{:S(2)}) async-start(bf16[16,16,16,128]{3,2,1,0:T(8,128)(2,1)} %spectra.3), calls=%async_computation.1 | async-start | bytes 2097152 | tf_op jit(solution)/shard_map/all_to_all | solution.py:490
  8.0 2.7 %spectra.2 = bf16[16,16,16,128]{3,2,1,0:T(8,128)(2,1)} custom-call(s32[1]{0:T(128)} %bitcast.1.half_ref, bf16[2,128,256]{2,1,0:T(8,128)(2,1)} %constant.37.clone.table_hbm, bf16[2,32,128,128]{3,2,1,0:T(8,128)(2,1)} %echo_hbm.3), custom_call_target="tpu_custom_call" | custom-call | tf_op jit(solution)/shard_map/spectra/pallas_call | solution.py:183
  10.7 0.0 copy-start.2
  10.7 10.7 %all-to-all-done.1 = bf16[16,16,16,128]{3,2,1,0:T(8,128)(2,1)S(1)} async-done(((bf16[16,16,16,128]{3,2,1,0:T(8,128)(2,1)}), bf16[16,16,16,128]{3,2,1,0:T(8,128)(2,1)S(1)}, u32[]{:S(2)}, u32[]{:S(2)}) %all-to-all-start.1) | async-done | bytes 1048608 | tf_op jit(solution)/shard_map/all_to_all | solution.py:490
  21.5 5.1 %all-to-all-start = ((bf16[16,16,16,128]{3,2,1,0:T(8,128)(2,1)}), bf16[16,16,16,128]{3,2,1,0:T(8,128)(2,1)S(1)}, u32[]{:S(2)}, u32[]{:S(2)}) async-start(bf16[16,16,16,128]{3,2,1,0:T(8,128)(2,1)} %spectra.2), calls=%async_computation | async-start | bytes 2097152 | tf_op jit(solution)/shard_map/all_to_all | solution.py:490
  26.5 0.0 copy-done
  26.5 0.3 spread.1.spread_ref
  26.8 0.0 copy-done.2
  26.9 0.3 tile.21
  27.1 0.4 reshape.33
  27.6 0.1 copy.9
  27.8 0.3 tile.9
  28.0 0.4 reshape.32
  28.5 0.1 copy.8
  28.7 0.1 maximum_bitcast_fusion
  28.7 0.7 %partial_sums.1 = bf16[4,128,256]{2,1,0:T(8,128)(2,1)S(1)} custom-call(bf16[8,2,16,16,128]{4,3,2,1,0:T(8,128)(2,1)S(1)} %bitcast.34, bf16[128,2048]{1,0:T(8,128)(2,1)S(1)} %spread.1.spread_ref), custom_call_target="tpu_custom_call" | custom-call | tf_op jit(solution)/shard_map/partial_sums/pallas_call | solution.py:263
  29.4 0.0 copy-start.1
  29.5 2.7 %collective-permute-start = (bf16[4,128,256]{2,1,0:T(8,128)(2,1)S(1)}, bf16[4,128,256]{2,1,0:T(8,128)(2,1)S(1)}, u32[]{:S(2)}, u32[]{:S(2)}) collective-permute-start(bf16[4,128,256]{2,1,0:T(8,128)(2,1)S(1)} %partial_sums.1), channel_id=1, source_target_pairs={{0,16},{2,18},{4,20},{6,22},{8,24},{10,26},{12,28},{14,30},{16,0},... | collective-permute-start | bytes 786440 | tf_op jit(solution)/shard_map/ppermute | solution.py:496
  32.1 0.5 copy.10
  32.7 0.1 copy.11
  32.8 0.0 copy-done.1
  32.8 0.1 pad_maximum_fusion.1.steer_ref
  32.9 11.3 %all-to-all-done = bf16[16,16,16,128]{3,2,1,0:T(8,128)(2,1)S(1)} async-done(((bf16[16,16,16,128]{3,2,1,0:T(8,128)(2,1)}), bf16[16,16,16,128]{3,2,1,0:T(8,128)(2,1)S(1)}, u32[]{:S(2)}, u32[]{:S(2)}) %all-to-all-start) | async-done | bytes 1048608 | tf_op jit(solution)/shard_map/all_to_all | solution.py:490
  44.2 3.4 %collective-permute-done.far_ref = bf16[4,128,256]{2,1,0:T(8,128)(2,1)S(1)} collective-permute-done((bf16[4,128,256]{2,1,0:T(8,128)(2,1)S(1)}, bf16[4,128,256]{2,1,0:T(8,128)(2,1)S(1)}, u32[]{:S(2)}, u32[]{:S(2)}) %collective-permute-start) | collective-permute-done | bytes 262176 | tf_op jit(solution)/shard_map/ppermute | solution.py:496
  47.6 6.0 %beams.1 = (f32[2,8,128]{2,1,0:T(8,128)S(1)}, f32[2,8,128]{2,1,0:T(8,128)S(1)}) custom-call(s32[1]{0:T(128)} %bitcast.side_ref, bf16[8,2,16,16,128]{4,3,2,1,0:T(8,128)(2,1)S(1)} %bitcast.35, bf16[128,2048]{1,0:T(8,128)(2,1)S(1)} %spread.1.spread_ref, bf16[4,128,256]{2,1,0:T(8,128)(2,1)S(1)} %collective-permute-done.far_ref, bf16[512,512]{1,0:T(8,128)(2,1)S(1)} %bitcast.36, ...), custom_call_target="tpu_custom_call" | custom-call | tf_op jit(solution)/shard_map/beams/pallas_call | solution.py:503
  53.6 2.0 %collective-permute-start.1 = (f32[2,8,128]{2,1,0:T(8,128)S(1)}, f32[2,8,128]{2,1,0:T(8,128)S(1)}, u32[]{:S(2)}, u32[]{:S(2)}) collective-permute-start(f32[2,8,128]{2,1,0:T(8,128)S(1)} %get-tuple-element.8), channel_id=1, source_target_pairs={{0,1},{1,0},{2,3},{3,2},{4,5},{5,4},{6,7},{7,6},{8,9},{9,8},{10,11... | collective-permute-start | bytes 24584 | tf_op jit(solution)/shard_map/ppermute | solution.py:512
  55.6 1.7 %collective-permute-done.1 = f32[2,8,128]{2,1,0:T(8,128)S(1)} collective-permute-done((f32[2,8,128]{2,1,0:T(8,128)S(1)}, f32[2,8,128]{2,1,0:T(8,128)S(1)}, u32[]{:S(2)}, u32[]{:S(2)}) %collective-permute-start.1) | collective-permute-done | bytes 8224 | tf_op jit(solution)/shard_map/ppermute | solution.py:512
  57.3 0.6 %add.16 = f32[2,8,128]{2,1,0:T(8,128)} add(f32[2,8,128]{2,1,0:T(8,128)S(1)} %get-tuple-element.7, f32[2,8,128]{2,1,0:T(8,128)S(1)} %collective-permute-done.1) | non-fusion elementwise | flops 2048 | bytes 24576 | tf_op jit(solution)/shard_map/add | solution.py:512
  (9 shorter events, 0.1 us)
Async XLA Ops:
  0.0 26.5 %copy-start = (bf16[2,64,512]{2,1,0:T(8,128)(2,1)S(1)}, bf16[2,64,512]{2,1,0:T(8,128)(2,1)}, u32[]{:S(2)}) copy-start(bf16[2,64,512]{2,1,0:T(8,128)(2,1)} %param.8) | copy-start | bytes 393220
  2.8 18.7 %all-to-all-start.1 = ((bf16[16,16,16,128]{3,2,1,0:T(8,128)(2,1)}), bf16[16,16,16,128]{3,2,1,0:T(8,128)(2,1)S(1)}, u32[]{:S(2)}, u32[]{:S(2)}) async-start(bf16[16,16,16,128]{3,2,1,0:T(8,128)(2,1)} %spectra.3), calls=%async_computation.1 | async-start | bytes 2097152 | tf_op jit(solution)/shard_map/all_to_all | solution.py:490
  10.7 16.1 %copy-start.2 = (bf16[2,64]{1,0:T(2,128)(2,1)S(1)}, bf16[2,64]{1,0:T(2,128)(2,1)}, u32[]{:S(2)}) copy-start(bf16[2,64]{1,0:T(2,128)(2,1)} %param.7) | copy-start | bytes 772
  21.5 22.8 %all-to-all-start = ((bf16[16,16,16,128]{3,2,1,0:T(8,128)(2,1)}), bf16[16,16,16,128]{3,2,1,0:T(8,128)(2,1)S(1)}, u32[]{:S(2)}, u32[]{:S(2)}) async-start(bf16[16,16,16,128]{3,2,1,0:T(8,128)(2,1)} %spectra.2), calls=%async_computation | async-start | bytes 2097152 | tf_op jit(solution)/shard_map/all_to_all | solution.py:490
  29.4 3.3 %copy-start.1 = (f32[2,8,64]{2,1,0:T(8,128)S(1)}, f32[2,8,64]{2,1,0:T(8,128)}, u32[]{:S(2)}) copy-start(f32[2,8,64]{2,1,0:T(8,128)} %param.9) | copy-start | bytes 12292
  29.5 18.2 %collective-permute-start = (bf16[4,128,256]{2,1,0:T(8,128)(2,1)S(1)}, bf16[4,128,256]{2,1,0:T(8,128)(2,1)S(1)}, u32[]{:S(2)}, u32[]{:S(2)}) collective-permute-start(bf16[4,128,256]{2,1,0:T(8,128)(2,1)S(1)} %partial_sums.1), channel_id=1, source_target_pairs={{0,16},{2,18},{4,20},{6,22},{8,24},{10,26},{12,28},{14,30},{16,0},... | collective-permute-start | bytes 786440 | tf_op jit(solution)/shard_map/ppermute | solution.py:496
  53.6 3.7 %collective-permute-start.1 = (f32[2,8,128]{2,1,0:T(8,128)S(1)}, f32[2,8,128]{2,1,0:T(8,128)S(1)}, u32[]{:S(2)}, u32[]{:S(2)}) collective-permute-start(f32[2,8,128]{2,1,0:T(8,128)S(1)} %get-tuple-element.8), channel_id=1, source_target_pairs={{0,1},{1,0},{2,3},{3,2},{4,5},{5,4},{6,7},{7,6},{8,9},{9,8},{10,11... | collective-permute-start | bytes 24584 | tf_op jit(solution)/shard_map/ppermute | solution.py:512

commit v5 on v4

--- a/solution.py
+++ b/solution.py
@@ -395,18 +395,31 @@
         rows = sweep(rows, columns, lambda step: [q for q in range(blocks) if q // 2 != step])
         for q in range(blocks):
             rows_ref[base + 8 * q : base + 8 * q + 8] = rows[q]
+        at = (lax.broadcasted_iota(jnp.int32, rest[0][size:].shape, 1) - first) % beams
         for n in range(count):
             top = rows_ref[pl.ds(base + n, size, stride=count), :]
-            before = [jnp.zeros((first, 2 * beams), jnp.float32)] * (first > 0)
-            after = [jnp.zeros((beams - first - size, 2 * beams), jnp.float32)]
-            high, low = split(jnp.concatenate(before + [top] + after + before + [turn(top)] + after, axis=0))
             value = rest[n][size:]
-            v_high, v_low = split(value)
-            taken = jnp.dot(v_high, high, preferred_element_type=jnp.float32)
-            taken = taken + jnp.dot(v_high, low, preferred_element_type=jnp.float32)
-            taken = taken + jnp.dot(v_low, high, preferred_element_type=jnp.float32)
-            at = lax.broadcasted_iota(jnp.int32, value.shape, 1) % beams
-            rest[n] = jnp.where((at >= first) & (at < first + size), 0.0, value) - taken
+            taken = jnp.dot(
+                packed_left(value, at, size), packed_right(top, first), preferred_element_type=jnp.float32
+            )
+            rest[n] = jnp.where(at < size, 0.0, value) - taken
+
+
+def packed_left(value, at, size):
+    high, low = (part.astype(jnp.float32) for part in split(value))
+    again = jnp.where(at < 2 * size, pltpu.roll(low, size, 1), pltpu.roll(high, 2 * size, 1))
+    return jnp.where(at < size, high, again).astype(jnp.bfloat16)
+
+
+def packed_right(top, first):
+    size, width = top.shape
+    count = width // size
+    pieces = [jnp.zeros(top.shape, jnp.bfloat16)] * count
+    for start, rows in ((first, top), (first + width // 2, turn(top))):
+        high, low = split(rows)
+        for step, piece in enumerate((high, high, low)):
+            pieces[(start // size + step) % count] = piece
+    return jnp.concatenate(pieces, axis=0)
 
 
 def beams_body(
@@ -417,54 +430,81 @@
     ranges = gates // own_ref.shape[2]
     near = beam_sums(spectra_ref, spread_ref, bins)
     sums = [near[d] + far_ref[d].astype(jnp.float32) for d in range(bins)]
-    wide = jnp.concatenate(
-        [jnp.concatenate([value[:beams], value[beams:]], axis=1) for value in sums], axis=0
-    )
-    high, low = split(wide)
-    pulse = pulse_ref[...]
-    formed = jnp.dot(high, pulse, preferred_element_type=jnp.float32) + jnp.dot(
-        low, pulse, preferred_element_type=jnp.float32
-    )
+    half = gates // ranges
+    high, low = split(
+        jnp.concatenate(
+            [
+                jnp.concatenate(
+                    [
+                        value[part * beams : (part + 1) * beams, block * half : (block + 1) * half]
+                        for block in range(ranges)
+                        for part in range(2)
+                    ],
+                    axis=1,
+                )
+                for value in sums
+            ],
+            axis=0,
+        )
+    )
+    formed = [0.0] * ranges
+    for block in range(ranges):
+        into = slice(block * 2 * half, (block + 1) * 2 * half)
+        pulse = pulse_ref[block * 2 * half :, into]
+        for piece in (high, low):
+            formed[block] = formed[block] + jnp.dot(
+                piece[:, block * 2 * half :], pulse, preferred_element_type=jnp.float32
+            )
     sub = lax.broadcasted_iota(jnp.int32, (beams, 2 * beams), 0)
     lane = lax.broadcasted_iota(jnp.int32, (beams, 2 * beams), 1)
     both, systems = [], []
     for d in range(bins):
-        real = formed[d * beams : (d + 1) * beams, :gates]
-        imag = formed[d * beams : (d + 1) * beams, gates:]
+        mine = slice(d * beams, (d + 1) * beams)
+        real = jnp.concatenate([value[mine, :half] for value in formed], axis=1)
+        imag = jnp.concatenate([value[mine, half:] for value in formed], axis=1)
         top = jnp.concatenate([real, imag], axis=1)
-        whole = jnp.concatenate([top, jnp.concatenate([-imag, real], axis=1)], axis=0)
-        g_high, g_low = split(whole)
-        both.append((g_high, g_low))
-        cov = lax.dot_general(g_high[:beams], g_high, NT, preferred_element_type=jnp.float32)
-        cov = cov + lax.dot_general(g_high[:beams], g_low, NT, preferred_element_type=jnp.float32)
-        cov = cov + lax.dot_general(g_low[:beams], g_high, NT, preferred_element_type=jnp.float32)
+        t_high, t_low = split(top)
+        u_high, u_low = split(jnp.concatenate([-imag, real], axis=1))
+        left = jnp.concatenate([t_high, t_low], axis=0)
+        both.append(left)
+        products = lax.dot_general(
+            left, jnp.concatenate([t_high, u_high, t_low, u_low], axis=0), NT, preferred_element_type=jnp.float32
+        )
+        cov = (
+            products[:beams, : 2 * beams] + products[:beams, 2 * beams :] + products[beams:, : 2 * beams]
+        )
         cov = cov * (1.0 / gates)
         on_diagonal = sub == lane
         trace = jnp.sum(jnp.where(on_diagonal, cov, 0.0), axis=(0, 1), keepdims=True)
         loading = load_ratio * trace / beams + epsilon
-        cov = jnp.where(on_diagonal, cov + loading, cov)
+        cov = jnp.where(on_diagonal, cov + loading, cov) * (1.0 / loading)
         systems.append(cov)
     steer = steer_ref[...]
     sources = [steer[d : d + 1] for d in range(bins)]
     conj = -eliminate(systems, sources, rows_ref)[:bins]
     response = jnp.sum(conj * steer, axis=1, keepdims=True)
     weight = conj / response
-    w_high, w_low = split(weight)
+    part_of = lax.broadcasted_iota(jnp.int32, weight.shape, 1) < beams
+    other = pltpu.roll(weight, beams, 1)
+    pieces = []
+    for twice in (jnp.where(part_of, weight, other), jnp.where(part_of, other, weight)):
+        w_high, w_low = split(twice)
+        pieces += [w_high, jnp.where(part_of, w_low, jnp.zeros_like(w_low))]
+    left = jnp.concatenate(pieces, axis=0)
     first_side = side_ref[0] == 0
-    half = gates // ranges
-    row = lax.broadcasted_iota(jnp.int32, (bins, half), 0)
-    outs = [jnp.zeros((bins, half), jnp.float32)] * (2 * ranges)
+    row = lax.broadcasted_iota(jnp.int32, (bins, 2 * gates), 0)
+    by_real = by_imag = jnp.zeros((bins, 2 * gates), jnp.float32)
     for d in range(bins):
-        g_high, g_low = both[d]
-        out = jnp.dot(w_high, g_high, preferred_element_type=jnp.float32)
-        out = out + jnp.dot(w_high, g_low, preferred_element_type=jnp.float32)
-        out = out + jnp.dot(w_low, g_high, preferred_element_type=jnp.float32)
-        outs = [
-            jnp.where(row == d, out[:, n * half : (n + 1) * half], kept) for n, kept in enumerate(outs)
-        ]
+        out = jnp.dot(left, both[d], preferred_element_type=jnp.float32)
+        by_real = jnp.where(row == d, out[:bins] + out[bins : 2 * bins], by_real)
+        by_imag = jnp.where(row == d, out[2 * bins : 3 * bins] + out[3 * bins :], by_imag)
+    joined = (
+        by_real[:, :gates] - by_imag[:, gates:],
+        by_real[:, gates:] + by_imag[:, :gates],
+    )
     nothing = jnp.zeros((bins, half), jnp.float32)
     for part in range(2):
-        first, second = outs[2 * part : 2 * part + 2]
+        first, second = joined[part][:, :half], joined[part][:, half:]
         own_ref[part] = jnp.concatenate(
             [jnp.where(first_side, first, nothing), jnp.where(first_side, nothing, second)], axis=0
         )
@@ -496,7 +536,8 @@
     far = lax.ppermute(crossing, "elem", [(n, (n + elems // 2) % elems) for n in range(elems)])
     near = gathered(half)
     pulse = pulse_kernel(replica, gates)[:, :, :gates]
-    pulse = pulse.transpose(0, 2, 1, 3).reshape(2 * gates, 2 * gates)
+    pulse = pulse.reshape(2, 2, ranges, gate_count, ranges, gate_count)
+    pulse = pulse.transpose(2, 0, 3, 4, 1, 5).reshape(2 * gates, 2 * gates)
     own_steering = lax.dynamic_slice_in_dim(steering, side * bins, bins, 1)
     steer_row = jnp.concatenate([own_steering[0], -own_steering[1]], axis=1)
     shape = jax.ShapeDtypeStruct((2, 2 * bins, gate_count), jnp.float32)

time: 58.7 us -> 58.6 us (level)
  waiting for transfers between devices: 27.1 us -> 24.7 us
  local copies, waits for them, and re-layouts: 2.41 us -> 4.67 us
    all_to_all x2, waiting for transfers between devices: 22 us -> 19.7 us  [gathered(): lax.all_to_all(sent, ('elem', 'range'), 0, 0, tiled=True, axis_index_grou...]
    reshape x0 -> x2, local copies, waits for them, and re-layouts: none -> 1.36 us  [the longest x1 1.24 us: on_device_owned(): pulse = pulse.transpose(2, 0, 3, 4, 1, 5).reshape(2 * gates, 2 * gates)]
    transpose x2 -> x1, local copies, waits for them, and re-layouts: 0.67 us -> 1.8 us  [on_device_owned(): pulse = pulse.transpose(2, 0, 3, 4, 1, 5).reshape(2 * gates, 2 * gates)]
  transfers between devices with their start and end apart: 4 -> 4, of which waited for: 4 -> 4; matrix products, arithmetic and copies ran while one was open for 4% -> 9% of each run, Pallas kernels for 6% -> 6%
where the time goes in v5:
time: 58.6 us; the launch traced here: 57.7 us
  waiting for transfers between devices  24.7 us (42%)
  starting transfers between devices  15 us (26%)
  Pallas kernels  12.2 us (21%)
  local copies, waits for them, and re-layouts  4.67 us (8%)
  other arithmetic  0.89 us (2%)
    all_to_all x2, waiting for transfers between devices, gathered(): lax.all_to_all(sent, ('elem', 'range'), 0, 0, tiled=True, axis_index_grou...  19.7 us
    all_to_all x2, starting transfers between devices, gathered(): lax.all_to_all(sent, ('elem', 'range'), 0, 0, tiled=True, axis_index_grou...  10.3 us
    pallas_call x1, Pallas kernels, on_device_owned(): pl.pallas_call(beams_body, in_specs=[pl.BlockSpec(memory_space=pltpu.SMEM...  5.74 us
    pallas_call x2, Pallas kernels, spectra(): pl.pallas_call(spectra_body, in_specs=[pl.BlockSpec(memory_space=pltpu.SM...  5.5 us
    ppermute x1, waiting for transfers between devices, on_device_owned(): lax.ppermute(crossing, 'elem', [(n, (n + elems // 2) % elems) for n in ra...  3.39 us
    ppermute x1, starting transfers between devices, on_device_owned(): lax.ppermute(crossing, 'elem', [(n, (n + elems // 2) % elems) for n in ra...  2.66 us
    ppermute x1, starting transfers between devices, on_device_owned(): return own + lax.ppermute(send, 'range', [(0, 1), (1, 0)])  2.06 us
    transpose x1, local copies, waits for them, and re-layouts, on_device_owned(): pulse = pulse.transpose(2, 0, 3, 4, 1, 5).reshape(2 * gates, 2 * gates)  1.8 us
  transfers between devices with their start and end apart: 4, of which 4 were waited for; matrix products, arithmetic and copies ran while one was open for 9% of the time, Pallas kernels for 6%

profile of v5, /device:TPU:8, one launch (start us, length us, event | category | flops | bytes accessed | tf_op | source)
XLA Modules:
  0.0 57.7 jit_solution(8319836359644308668)
XLA Ops:
  0.0 0.0 copy-start
  0.0 2.8 %spectra.3 = bf16[16,16,16,128]{3,2,1,0:T(8,128)(2,1)} custom-call(s32[1]{0:T(128)} %bitcast.3.half_ref, bf16[2,128,256]{2,1,0:T(8,128)(2,1)} %constant.37.clone.table_hbm, bf16[2,32,128,128]{3,2,1,0:T(8,128)(2,1)} %echo_hbm.3), custom_call_target="tpu_custom_call" | custom-call | tf_op jit(solution)/shard_map/spectra/pallas_call | solution.py:183
  2.8 5.2 %all-to-all-start.1 = ((bf16[16,16,16,128]{3,2,1,0:T(8,128)(2,1)}), bf16[16,16,16,128]{3,2,1,0:T(8,128)(2,1)S(1)}, u32[]{:S(2)}, u32[]{:S(2)}) async-start(bf16[16,16,16,128]{3,2,1,0:T(8,128)(2,1)} %spectra.3), calls=%async_computation.1 | async-start | bytes 2097152 | tf_op jit(solution)/shard_map/all_to_all | solution.py:530
  8.0 2.7 %spectra.2 = bf16[16,16,16,128]{3,2,1,0:T(8,128)(2,1)} custom-call(s32[1]{0:T(128)} %bitcast.1.half_ref, bf16[2,128,256]{2,1,0:T(8,128)(2,1)} %constant.37.clone.table_hbm, bf16[2,32,128,128]{3,2,1,0:T(8,128)(2,1)} %echo_hbm.3), custom_call_target="tpu_custom_call" | custom-call | tf_op jit(solution)/shard_map/spectra/pallas_call | solution.py:183
  10.7 0.0 copy-start.2
  10.7 10.7 %all-to-all-done.1 = bf16[16,16,16,128]{3,2,1,0:T(8,128)(2,1)S(1)} async-done(((bf16[16,16,16,128]{3,2,1,0:T(8,128)(2,1)}), bf16[16,16,16,128]{3,2,1,0:T(8,128)(2,1)S(1)}, u32[]{:S(2)}, u32[]{:S(2)}) %all-to-all-start.1) | async-done | bytes 1048608 | tf_op jit(solution)/shard_map/all_to_all | solution.py:530
  21.5 5.1 %all-to-all-start = ((bf16[16,16,16,128]{3,2,1,0:T(8,128)(2,1)}), bf16[16,16,16,128]{3,2,1,0:T(8,128)(2,1)S(1)}, u32[]{:S(2)}, u32[]{:S(2)}) async-start(bf16[16,16,16,128]{3,2,1,0:T(8,128)(2,1)} %spectra.2), calls=%async_computation | async-start | bytes 2097152 | tf_op jit(solution)/shard_map/all_to_all | solution.py:530
  26.5 0.0 copy-done
  26.5 0.3 spread.1.spread_ref
  26.8 0.0 copy-done.2
  26.9 0.3 tile.21
  27.2 0.4 reshape.36
  27.7 0.3 tile.9
  27.9 0.4 reshape.35
  28.4 0.1 maximum_bitcast_fusion
  28.6 0.7 %partial_sums.1 = bf16[4,128,256]{2,1,0:T(8,128)(2,1)S(1)} custom-call(bf16[8,2,16,16,128]{4,3,2,1,0:T(8,128)(2,1)S(1)} %bitcast.36, bf16[128,2048]{1,0:T(8,128)(2,1)S(1)} %spread.1.spread_ref), custom_call_target="tpu_custom_call" | custom-call | tf_op jit(solution)/shard_map/partial_sums/pallas_call | solution.py:263
  29.3 2.7 %collective-permute-start = (bf16[4,128,256]{2,1,0:T(8,128)(2,1)S(1)}, bf16[4,128,256]{2,1,0:T(8,128)(2,1)S(1)}, u32[]{:S(2)}, u32[]{:S(2)}) collective-permute-start(bf16[4,128,256]{2,1,0:T(8,128)(2,1)S(1)} %partial_sums.1), channel_id=1, source_target_pairs={{0,16},{2,18},{4,20},{6,22},{8,24},{10,26},{12,28},{14,30},{16,0},... | collective-permute-start | bytes 786440 | tf_op jit(solution)/shard_map/ppermute | solution.py:536
  31.9 0.0 copy-start.1
  32.0 0.1 reshape.39
  32.1 1.8 %copy.8 = bf16[2,2,128,2,2,128]{5,4,3,2,1,0:T(2,128)(2,1)} copy(bf16[2,2,128,2,2,128]{2,0,5,3,4,1:T(2,128)(2,1)S(1)} %bitcast.38) | data formatting | bytes 1048576 | tf_op jit(solution)/shard_map/transpose | solution.py:540
  33.9 1.2 %reshape.38.pulse_ref = bf16[512,512]{1,0:T(8,128)(2,1)S(1)} reshape(bf16[2,2,128,2,2,128]{5,4,3,2,1,0:T(2,128)(2,1)} %copy.8) | data formatting | bytes 1048576 | tf_op jit(solution)/shard_map/reshape | solution.py:540
  35.2 0.0 copy-done.1
  35.2 0.1 pad_maximum_fusion.1.steer_ref
  35.3 9.0 %all-to-all-done = bf16[16,16,16,128]{3,2,1,0:T(8,128)(2,1)S(1)} async-done(((bf16[16,16,16,128]{3,2,1,0:T(8,128)(2,1)}), bf16[16,16,16,128]{3,2,1,0:T(8,128)(2,1)S(1)}, u32[]{:S(2)}, u32[]{:S(2)}) %all-to-all-start) | async-done | bytes 1048608 | tf_op jit(solution)/shard_map/all_to_all | solution.py:530
  44.2 3.4 %collective-permute-done.far_ref = bf16[4,128,256]{2,1,0:T(8,128)(2,1)S(1)} collective-permute-done((bf16[4,128,256]{2,1,0:T(8,128)(2,1)S(1)}, bf16[4,128,256]{2,1,0:T(8,128)(2,1)S(1)}, u32[]{:S(2)}, u32[]{:S(2)}) %collective-permute-start) | collective-permute-done | bytes 262176 | tf_op jit(solution)/shard_map/ppermute | solution.py:536
  47.6 5.7 %beams.1 = (f32[2,8,128]{2,1,0:T(8,128)S(1)}, f32[2,8,128]{2,1,0:T(8,128)S(1)}) custom-call(s32[1]{0:T(128)} %bitcast.side_ref, bf16[8,2,16,16,128]{4,3,2,1,0:T(8,128)(2,1)S(1)} %bitcast.37, bf16[128,2048]{1,0:T(8,128)(2,1)S(1)} %spread.1.spread_ref, bf16[4,128,256]{2,1,0:T(8,128)(2,1)S(1)} %collective-permute-done.far_ref, ...), custom_call_target="tpu_custom_call" | custom-call | tf_op jit(solution)/shard_map/beams/pallas_call | solution.py:544
  53.4 2.1 %collective-permute-start.1 = (f32[2,8,128]{2,1,0:T(8,128)S(1)}, f32[2,8,128]{2,1,0:T(8,128)S(1)}, u32[]{:S(2)}, u32[]{:S(2)}) collective-permute-start(f32[2,8,128]{2,1,0:T(8,128)S(1)} %get-tuple-element.8), channel_id=1, source_target_pairs={{0,1},{1,0},{2,3},{3,2},{4,5},{5,4},{6,7},{7,6},{8,9},{9,8},{10,11... | collective-permute-start | bytes 24584 | tf_op jit(solution)/shard_map/ppermute | solution.py:553
  55.4 1.7 %collective-permute-done.1 = f32[2,8,128]{2,1,0:T(8,128)S(1)} collective-permute-done((f32[2,8,128]{2,1,0:T(8,128)S(1)}, f32[2,8,128]{2,1,0:T(8,128)S(1)}, u32[]{:S(2)}, u32[]{:S(2)}) %collective-permute-start.1) | collective-permute-done | bytes 8224 | tf_op jit(solution)/shard_map/ppermute | solution.py:553
  57.1 0.6 %add.16 = f32[2,8,128]{2,1,0:T(8,128)} add(f32[2,8,128]{2,1,0:T(8,128)S(1)} %get-tuple-element.7, f32[2,8,128]{2,1,0:T(8,128)S(1)} %collective-permute-done.1) | non-fusion elementwise | flops 2048 | bytes 24576 | tf_op jit(solution)/shard_map/add | solution.py:553
  (9 shorter events, 0.1 us)
Async XLA Ops:
  0.0 26.5 %copy-start = (bf16[2,64,512]{2,1,0:T(8,128)(2,1)S(1)}, bf16[2,64,512]{2,1,0:T(8,128)(2,1)}, u32[]{:S(2)}) copy-start(bf16[2,64,512]{2,1,0:T(8,128)(2,1)} %param.8) | copy-start | bytes 393220
  2.8 18.7 %all-to-all-start.1 = ((bf16[16,16,16,128]{3,2,1,0:T(8,128)(2,1)}), bf16[16,16,16,128]{3,2,1,0:T(8,128)(2,1)S(1)}, u32[]{:S(2)}, u32[]{:S(2)}) async-start(bf16[16,16,16,128]{3,2,1,0:T(8,128)(2,1)} %spectra.3), calls=%async_computation.1 | async-start | bytes 2097152 | tf_op jit(solution)/shard_map/all_to_all | solution.py:530
  10.7 16.1 %copy-start.2 = (bf16[2,64]{1,0:T(2,128)(2,1)S(1)}, bf16[2,64]{1,0:T(2,128)(2,1)}, u32[]{:S(2)}) copy-start(bf16[2,64]{1,0:T(2,128)(2,1)} %param.7) | copy-start | bytes 772
  21.5 22.8 %all-to-all-start = ((bf16[16,16,16,128]{3,2,1,0:T(8,128)(2,1)}), bf16[16,16,16,128]{3,2,1,0:T(8,128)(2,1)S(1)}, u32[]{:S(2)}, u32[]{:S(2)}) async-start(bf16[16,16,16,128]{3,2,1,0:T(8,128)(2,1)} %spectra.2), calls=%async_computation | async-start | bytes 2097152 | tf_op jit(solution)/shard_map/all_to_all | solution.py:530
  29.3 18.3 %collective-permute-start = (bf16[4,128,256]{2,1,0:T(8,128)(2,1)S(1)}, bf16[4,128,256]{2,1,0:T(8,128)(2,1)S(1)}, u32[]{:S(2)}, u32[]{:S(2)}) collective-permute-start(bf16[4,128,256]{2,1,0:T(8,128)(2,1)S(1)} %partial_sums.1), channel_id=1, source_target_pairs={{0,16},{2,18},{4,20},{6,22},{8,24},{10,26},{12,28},{14,30},{16,0},... | collective-permute-start | bytes 786440 | tf_op jit(solution)/shard_map/ppermute | solution.py:536
  31.9 3.2 %copy-start.1 = (f32[2,8,64]{2,1,0:T(8,128)S(1)}, f32[2,8,64]{2,1,0:T(8,128)}, u32[]{:S(2)}) copy-start(f32[2,8,64]{2,1,0:T(8,128)} %param.9) | copy-start | bytes 12292
  53.4 3.7 %collective-permute-start.1 = (f32[2,8,128]{2,1,0:T(8,128)S(1)}, f32[2,8,128]{2,1,0:T(8,128)S(1)}, u32[]{:S(2)}, u32[]{:S(2)}) collective-permute-start(f32[2,8,128]{2,1,0:T(8,128)S(1)} %get-tuple-element.8), channel_id=1, source_target_pairs={{0,1},{1,0},{2,3},{3,2},{4,5},{5,4},{6,7},{7,6},{8,9},{9,8},{10,11... | collective-permute-start | bytes 24584 | tf_op jit(solution)/shard_map/ppermute | solution.py:553

commit v6 on v5

--- a/solution.py
+++ b/solution.py
@@ -253,21 +253,25 @@
     ]
 
 
-def partial_body(spectra_ref, spread_ref, out_ref):
-    for d, value in enumerate(beam_sums(spectra_ref, spread_ref, out_ref.shape[0])):
-        out_ref[d] = value.astype(out_ref.dtype)
-
-
-def partial_sums(bound, spread_weights, bins, dtype):
-    shape = (bins, spread_weights.shape[0], bound.shape[1] * bound.shape[4])
+def crossing_body(side_ref, spectra_ref, spread_ref, same_ref, other_ref):
+    bins, _, gates = same_ref.shape
+    first_side = side_ref[0] == 0
+    for d, value in enumerate(beam_sums(spectra_ref, spread_ref, bins)):
+        first, second = value[:, :gates], value[:, gates:]
+        same_ref[d] = jnp.where(first_side, first, second).astype(same_ref.dtype)
+        other_ref[d] = jnp.where(first_side, second, first).astype(other_ref.dtype)
+
+
+def crossing_sums(side, bound, spread_weights, bins):
+    shape = jax.ShapeDtypeStruct((bins, spread_weights.shape[0], bound.shape[4]), jnp.bfloat16)
     return pl.pallas_call(
-        partial_body,
-        in_specs=whole_vmem(2),
-        out_specs=whole_vmem(1)[0],
-        out_shape=jax.ShapeDtypeStruct(shape, dtype),
+        crossing_body,
+        in_specs=[pl.BlockSpec(memory_space=pltpu.SMEM)] + whole_vmem(2),
+        out_specs=whole_vmem(2),
+        out_shape=[shape, shape],
         compiler_params=pltpu.CompilerParams(vmem_limit_bytes=BEAMS_VMEM),
-        name="partial_sums",
-    )(bound, spread_weights)
+        name="crossing_sums",
+    )(side, bound, spread_weights)
 
 
 def split(value):
@@ -423,14 +427,19 @@
 
 
 def beams_body(
-    side_ref, spectra_ref, spread_ref, far_ref, pulse_ref, steer_ref, own_ref, send_ref, rows_ref
+    side_ref, spectra_ref, spread_ref, same_ref, other_ref, pulse_ref, steer_ref, own_ref, send_ref, rows_ref
 ):
-    bins, total, gates = far_ref.shape
+    bins, total, half = same_ref.shape
     beams = total // 2
-    ranges = gates // own_ref.shape[2]
+    ranges = spectra_ref.shape[1]
+    gates = ranges * half
+    first_side = side_ref[0] == 0
     near = beam_sums(spectra_ref, spread_ref, bins)
-    sums = [near[d] + far_ref[d].astype(jnp.float32) for d in range(bins)]
-    half = gates // ranges
+    sums = []
+    for d in range(bins):
+        same, other = same_ref[d].astype(jnp.float32), other_ref[d].astype(jnp.float32)
+        far = [jnp.where(first_side, same, other), jnp.where(first_side, other, same)]
+        sums.append(near[d] + jnp.concatenate(far, axis=1))
     high, low = split(
         jnp.concatenate(
             [
@@ -491,7 +500,6 @@
         w_high, w_low = split(twice)
         pieces += [w_high, jnp.where(part_of, w_low, jnp.zeros_like(w_low))]
     left = jnp.concatenate(pieces, axis=0)
-    first_side = side_ref[0] == 0
     row = lax.broadcasted_iota(jnp.int32, (bins, 2 * gates), 0)
     by_real = by_imag = jnp.zeros((bins, 2 * gates), jnp.float32)
     for d in range(bins):
@@ -523,18 +531,21 @@
     side = lax.axis_index("range")
     half = lax.axis_index("elem") // (elems // 2)
     group = devices // 2
-    groups = [list(range(group)), list(range(group, devices))]
-
-    def gathered(owner_half):
-        sent = spectra(owner_half, echoes, devices)
-        bound = lax.all_to_all(sent, ("elem", "range"), 0, 0, tiled=True, axis_index_groups=groups)
-        return bound.reshape(elems // 2, ranges, own_elements // 2, 4 * bins, gate_count)
-
+    seat = side.reshape(1).astype(jnp.int32)
     here = lax.dynamic_slice_in_dim(beam_weights, half * (elements // 2), elements // 2, 2)
     spread_weights = spread(here, bins)
-    crossing = partial_sums(gathered(1 - half), spread_weights, bins, jnp.bfloat16)
-    far = lax.ppermute(crossing, "elem", [(n, (n + elems // 2) % elems) for n in range(elems)])
-    near = gathered(half)
+
+    def exchanged(owner_half, axes, size):
+        groups = [list(range(size)), list(range(size, 2 * size))]
+        sent = spectra(owner_half, echoes, devices)
+        bound = lax.all_to_all(sent, axes, 0, 0, tiled=True, axis_index_groups=groups)
+        return bound.reshape(elems // 2, ranges, own_elements // 2, 4 * bins, gate_count)
+
+    same, other = crossing_sums(seat, exchanged(1 - half, "elem", elems // 2), spread_weights, bins)
+    across = [(n + group) % devices for n in range(devices)]
+    same = lax.ppermute(same, ("elem", "range"), list(enumerate(across)))
+    other = lax.ppermute(other, ("elem", "range"), [(n, to ^ 1) for n, to in enumerate(across)])
+    near = exchanged(half, ("elem", "range"), group)
     pulse = pulse_kernel(replica, gates)[:, :, :gates]
     pulse = pulse.reshape(2, 2, ranges, gate_count, ranges, gate_count)
     pulse = pulse.transpose(2, 0, 3, 4, 1, 5).reshape(2 * gates, 2 * gates)
@@ -543,13 +554,13 @@
     shape = jax.ShapeDtypeStruct((2, 2 * bins, gate_count), jnp.float32)
     own, send = pl.pallas_call(
         beams_body,
-        in_specs=[pl.BlockSpec(memory_space=pltpu.SMEM)] + whole_vmem(5),
+        in_specs=[pl.BlockSpec(memory_space=pltpu.SMEM)] + whole_vmem(6),
         out_specs=whole_vmem(2),
         out_shape=[shape, shape],
         scratch_shapes=[pltpu.VMEM((bins * beam_weights.shape[1], 2 * beam_weights.shape[1]), jnp.float32)],
         compiler_params=pltpu.CompilerParams(vmem_limit_bytes=BEAMS_VMEM),
         name="beams",
-    )(side.reshape(1).astype(jnp.int32), near, spread_weights, far, pulse, steer_row)
+    )(seat, near, spread_weights, same, other, pulse, steer_row)
     return own + lax.ppermute(send, "range", [(0, 1), (1, 0)])
 
 

time: 58.6 us -> 58.1 us (level); the launches traced: 57.7 us -> 57.8 us
  waiting for transfers between devices: 24.7 us -> 29.2 us
  starting transfers between devices: 15 us -> 12.5 us
  local copies, waits for them, and re-layouts: 4.67 us -> 2.81 us
    ppermute x1 -> x2, waiting for transfers between devices: 3.39 us -> 14.4 us  [the longest x1 10.6 us: on_device_owned(): same = lax.ppermute(same, ('elem', 'range'), list(enumerate(across)))]
    all_to_all x2, waiting for transfers between devices: 19.7 us -> 11.1 us  [exchanged(): lax.all_to_all(sent, axes, 0, 0, tiled=True, axis_index_groups=groups)]
    ppermute x1, waiting for transfers between devices: 1.66 us -> 3.62 us  [on_device_owned(): return own + lax.ppermute(send, 'range', [(0, 1), (1, 0)])]
    ppermute x1, starting transfers between devices: 2.06 us -> 0.1 us  [on_device_owned(): return own + lax.ppermute(send, 'range', [(0, 1), (1, 0)])]
    all_to_all x2, starting transfers between devices: 10.3 us -> 8.51 us  [exchanged(): lax.all_to_all(sent, axes, 0, 0, tiled=True, axis_index_groups=groups)]
    ppermute x1 -> x2, starting transfers between devices: 2.66 us -> 3.88 us  [the longest x1 2.65 us: on_device_owned(): same = lax.ppermute(same, ('elem', 'range'), list(enumerate(across)))]
    reshape x1, local copies, waits for them, and re-layouts: 1.24 us -> 0.2 us  [on_device_owned(): pulse = pulse.transpose(2, 0, 3, 4, 1, 5).reshape(2 * gates, 2 * gates)]
    transpose x1, local copies, waits for them, and re-layouts: 1.8 us -> 0.97 us  [on_device_owned(): pulse = pulse.transpose(2, 0, 3, 4, 1, 5).reshape(2 * gates, 2 * gates)]
  transfers between devices with their start and end apart: 4 -> 5, of which waited for: 4 -> 4; matrix products, arithmetic and copies ran while one was open for 9% -> 5% of each run, Pallas kernels for 6% -> 6%
where the time goes in v6:
time: 58.1 us; the launch traced here: 57.8 us
  waiting for transfers between devices  29.2 us (50%)
  starting transfers between devices  12.5 us (22%)
  Pallas kernels  12.2 us (21%)
  local copies, waits for them, and re-layouts  2.81 us (5%)
  other arithmetic  0.89 us (2%)
    all_to_all x2, waiting for transfers between devices, exchanged(): lax.all_to_all(sent, axes, 0, 0, tiled=True, axis_index_groups=groups)  11.1 us
    ppermute x1, waiting for transfers between devices, on_device_owned(): same = lax.ppermute(same, ('elem', 'range'), list(enumerate(across)))  10.6 us
    all_to_all x2, starting transfers between devices, exchanged(): lax.all_to_all(sent, axes, 0, 0, tiled=True, axis_index_groups=groups)  8.51 us
    pallas_call x1, Pallas kernels, on_device_owned(): pl.pallas_call(beams_body, in_specs=[pl.BlockSpec(memory_space=pltpu.SMEM...  5.74 us
    pallas_call x2, Pallas kernels, spectra(): pl.pallas_call(spectra_body, in_specs=[pl.BlockSpec(memory_space=pltpu.SM...  5.51 us
    ppermute x1, waiting for transfers between devices, on_device_owned(): lax.ppermute(other, ('elem', 'range'), [(n, to ^ 1) for n, to in enumerat...  3.77 us
    ppermute x1, waiting for transfers between devices, on_device_owned(): return own + lax.ppermute(send, 'range', [(0, 1), (1, 0)])  3.62 us
    ppermute x1, starting transfers between devices, on_device_owned(): same = lax.ppermute(same, ('elem', 'range'), list(enumerate(across)))  2.65 us
  transfers between devices with their start and end apart: 5, of which 4 were waited for; matrix products, arithmetic and copies ran while one was open for 5% of the time, Pallas kernels for 6%

profile of v6, /device:TPU:8, one launch (start us, length us, event | category | flops | bytes accessed | tf_op | source)
XLA Modules:
  0.0 57.8 jit_solution(4602946267552877669)
XLA Ops:
  0.0 0.0 copy-start
  0.0 2.8 %spectra.3 = bf16[16,16,16,128]{3,2,1,0:T(8,128)(2,1)} custom-call(s32[1]{0:T(128)} %bitcast.3.half_ref, bf16[2,128,256]{2,1,0:T(8,128)(2,1)} %constant.37.clone.table_hbm, bf16[2,32,128,128]{3,2,1,0:T(8,128)(2,1)} %echo_hbm.3), custom_call_target="tpu_custom_call" | custom-call | tf_op jit(solution)/shard_map/spectra/pallas_call | solution.py:183
  2.8 4.3 %all-to-all-start.1 = ((bf16[16,16,16,128]{3,2,1,0:T(8,128)(2,1)}), bf16[16,16,16,128]{3,2,1,0:T(8,128)(2,1)S(1)}, u32[]{:S(2)}, u32[]{:S(2)}) async-start(bf16[16,16,16,128]{3,2,1,0:T(8,128)(2,1)} %spectra.3), calls=%async_computation.1 | async-start | bytes 2097152 | tf_op jit(solution)/shard_map/all_to_all | solution.py:541
  7.0 2.7 %spectra.2 = bf16[16,16,16,128]{3,2,1,0:T(8,128)(2,1)} custom-call(s32[1]{0:T(128)} %bitcast.1.half_ref, bf16[2,128,256]{2,1,0:T(8,128)(2,1)} %constant.37.clone.table_hbm, bf16[2,32,128,128]{3,2,1,0:T(8,128)(2,1)} %echo_hbm.3), custom_call_target="tpu_custom_call" | custom-call | tf_op jit(solution)/shard_map/spectra/pallas_call | solution.py:183
  9.8 0.0 copy-start.2
  9.8 11.1 %all-to-all-done.1 = bf16[16,16,16,128]{3,2,1,0:T(8,128)(2,1)S(1)} async-done(((bf16[16,16,16,128]{3,2,1,0:T(8,128)(2,1)}), bf16[16,16,16,128]{3,2,1,0:T(8,128)(2,1)S(1)}, u32[]{:S(2)}, u32[]{:S(2)}) %all-to-all-start.1) | async-done | bytes 1048608 | tf_op jit(solution)/shard_map/all_to_all | solution.py:541
  20.9 4.2 %all-to-all-start = ((bf16[16,16,16,128]{3,2,1,0:T(8,128)(2,1)}), bf16[16,16,16,128]{3,2,1,0:T(8,128)(2,1)S(1)}, u32[]{:S(2)}, u32[]{:S(2)}) async-start(bf16[16,16,16,128]{3,2,1,0:T(8,128)(2,1)} %spectra.2), calls=%async_computation | async-start | bytes 2097152 | tf_op jit(solution)/shard_map/all_to_all | solution.py:541
  25.2 0.0 copy-done
  25.2 0.3 spread.1.spread_ref
  25.5 0.0 copy-done.2
  25.6 0.3 tile.21
  25.8 0.4 reshape.36
  26.3 0.3 tile.9
  26.6 0.4 reshape.35
  27.1 0.0 copy-start.1
  27.1 0.1 maximum_bitcast_fusion
  27.3 0.7 %crossing_sums.1 = (bf16[4,128,128]{2,1,0:T(8,128)(2,1)S(1)}, bf16[4,128,128]{2,1,0:T(8,128)(2,1)S(1)}) custom-call(s32[1]{0:T(128)} %bitcast.side_ref, bf16[8,2,16,16,128]{4,3,2,1,0:T(8,128)(2,1)S(1)} %bitcast.37, bf16[128,2048]{1,0:T(8,128)(2,1)S(1)} %spread.1.spread_ref), custom_call_target="tpu_custom_call" | custom-call | tf_op jit(solution)/shard_map/crossing_sums/pallas_call | solution.py:267
  28.0 2.6 %collective-permute-start = (bf16[4,128,128]{2,1,0:T(8,128)(2,1)S(1)}, bf16[4,128,128]{2,1,0:T(8,128)(2,1)S(1)}, u32[]{:S(2)}, u32[]{:S(2)}) collective-permute-start(bf16[4,128,128]{2,1,0:T(8,128)(2,1)S(1)} %get-tuple-element.9), channel_id=1, source_target_pairs={{0,16},{1,17},{2,18},{3,19},{4,20},{5,21},{6,22},{7,23},{8,24},{9,... | collective-permute-start | bytes 393224 | tf_op jit(solution)/shard_map/ppermute | solution.py:546
  30.7 1.2 %collective-permute-start.1 = (bf16[4,128,128]{2,1,0:T(8,128)(2,1)S(1)}, bf16[4,128,128]{2,1,0:T(8,128)(2,1)S(1)}, u32[]{:S(2)}, u32[]{:S(2)}) collective-permute-start(bf16[4,128,128]{2,1,0:T(8,128)(2,1)S(1)} %get-tuple-element.10), channel_id=1, source_target_pairs={{0,17},{1,16},{2,19},{3,18},{4,21},{5,20},{6,23},{7,22},{8,25},{9,... | collective-permute-start | bytes 393224 | tf_op jit(solution)/shard_map/ppermute | solution.py:547
  31.9 0.0 copy-done.1
  31.9 0.1 reshape.39
  32.0 1.0 %copy.8 = bf16[2,2,128,2,2,128]{5,4,3,2,1,0:T(2,128)(2,1)S(1)} copy(bf16[2,2,128,2,2,128]{2,0,5,3,4,1:T(2,128)(2,1)S(1)} %bitcast.38) | data formatting | bytes 1048576 | tf_op jit(solution)/shard_map/transpose | solution.py:551
  33.0 0.2 reshape.38.pulse_ref
  33.2 0.1 pad_maximum_fusion.1.steer_ref
  33.3 10.6 %collective-permute-done.same_ref = bf16[4,128,128]{2,1,0:T(8,128)(2,1)S(1)} collective-permute-done((bf16[4,128,128]{2,1,0:T(8,128)(2,1)S(1)}, bf16[4,128,128]{2,1,0:T(8,128)(2,1)S(1)}, u32[]{:S(2)}, u32[]{:S(2)}) %collective-permute-start) | collective-permute-done | bytes 131104 | tf_op jit(solution)/shard_map/ppermute | solution.py:546
  43.9 3.8 %collective-permute-done.1.other_ref = bf16[4,128,128]{2,1,0:T(8,128)(2,1)S(1)} collective-permute-done((bf16[4,128,128]{2,1,0:T(8,128)(2,1)S(1)}, bf16[4,128,128]{2,1,0:T(8,128)(2,1)S(1)}, u32[]{:S(2)}, u32[]{:S(2)}) %collective-permute-start.1) | collective-permute-done | bytes 131104 | tf_op jit(solution)/shard_map/ppermute | solution.py:547
  47.7 0.0 all-to-all-done
  47.7 5.7 %beams.1 = (f32[2,8,128]{2,1,0:T(8,128)S(1)}, f32[2,8,128]{2,1,0:T(8,128)S(1)}) custom-call(s32[1]{0:T(128)} %bitcast.side_ref, bf16[8,2,16,16,128]{4,3,2,1,0:T(8,128)(2,1)S(1)} %bitcast.36, bf16[128,2048]{1,0:T(8,128)(2,1)S(1)} %spread.1.spread_ref, bf16[4,128,128]{2,1,0:T(8,128)(2,1)S(1)} %collective-permute-done.same_ref, ...), custom_call_target="tpu_custom_call" | custom-call | tf_op jit(solution)/shard_map/beams/pallas_call | solution.py:555
  53.5 0.1 collective-permute-start.2
  53.6 3.6 %collective-permute-done.2 = f32[2,8,128]{2,1,0:T(8,128)S(1)} collective-permute-done((f32[2,8,128]{2,1,0:T(8,128)S(1)}, f32[2,8,128]{2,1,0:T(8,128)S(1)}, u32[]{:S(2)}, u32[]{:S(2)}) %collective-permute-start.2) | collective-permute-done | bytes 8224 | tf_op jit(solution)/shard_map/ppermute | solution.py:564
  57.2 0.6 %add.16 = f32[2,8,128]{2,1,0:T(8,128)} add(f32[2,8,128]{2,1,0:T(8,128)S(1)} %get-tuple-element.11, f32[2,8,128]{2,1,0:T(8,128)S(1)} %collective-permute-done.2) | non-fusion elementwise | flops 2048 | bytes 24576 | tf_op jit(solution)/shard_map/add | solution.py:564
  (9 shorter events, 0.1 us)
Async XLA Ops:
  0.0 25.2 %copy-start = (bf16[2,64,512]{2,1,0:T(8,128)(2,1)S(1)}, bf16[2,64,512]{2,1,0:T(8,128)(2,1)}, u32[]{:S(2)}) copy-start(bf16[2,64,512]{2,1,0:T(8,128)(2,1)} %param.8) | copy-start | bytes 393220
  2.8 18.2 %all-to-all-start.1 = ((bf16[16,16,16,128]{3,2,1,0:T(8,128)(2,1)}), bf16[16,16,16,128]{3,2,1,0:T(8,128)(2,1)S(1)}, u32[]{:S(2)}, u32[]{:S(2)}) async-start(bf16[16,16,16,128]{3,2,1,0:T(8,128)(2,1)} %spectra.3), calls=%async_computation.1 | async-start | bytes 2097152 | tf_op jit(solution)/shard_map/all_to_all | solution.py:541
  9.8 15.7 %copy-start.2 = (bf16[2,64]{1,0:T(2,128)(2,1)S(1)}, bf16[2,64]{1,0:T(2,128)(2,1)}, u32[]{:S(2)}) copy-start(bf16[2,64]{1,0:T(2,128)(2,1)} %param.7) | copy-start | bytes 772
  20.9 26.8 %all-to-all-start = ((bf16[16,16,16,128]{3,2,1,0:T(8,128)(2,1)}), bf16[16,16,16,128]{3,2,1,0:T(8,128)(2,1)S(1)}, u32[]{:S(2)}, u32[]{:S(2)}) async-start(bf16[16,16,16,128]{3,2,1,0:T(8,128)(2,1)} %spectra.2), calls=%async_computation | async-start | bytes 2097152 | tf_op jit(solution)/shard_map/all_to_all | solution.py:541
  27.1 4.8 %copy-start.1 = (f32[2,8,64]{2,1,0:T(8,128)S(1)}, f32[2,8,64]{2,1,0:T(8,128)}, u32[]{:S(2)}) copy-start(f32[2,8,64]{2,1,0:T(8,128)} %param.9) | copy-start | bytes 12292
  28.0 15.9 %collective-permute-start = (bf16[4,128,128]{2,1,0:T(8,128)(2,1)S(1)}, bf16[4,128,128]{2,1,0:T(8,128)(2,1)S(1)}, u32[]{:S(2)}, u32[]{:S(2)}) collective-permute-start(bf16[4,128,128]{2,1,0:T(8,128)(2,1)S(1)} %get-tuple-element.9), channel_id=1, source_target_pairs={{0,16},{1,17},{2,18},{3,19},{4,20},{5,21},{6,22},{7,23},{8,24},{9,... | collective-permute-start | bytes 393224 | tf_op jit(solution)/shard_map/ppermute | solution.py:546
  30.7 17.1 %collective-permute-start.1 = (bf16[4,128,128]{2,1,0:T(8,128)(2,1)S(1)}, bf16[4,128,128]{2,1,0:T(8,128)(2,1)S(1)}, u32[]{:S(2)}, u32[]{:S(2)}) collective-permute-start(bf16[4,128,128]{2,1,0:T(8,128)(2,1)S(1)} %get-tuple-element.10), channel_id=1, source_target_pairs={{0,17},{1,16},{2,19},{3,18},{4,21},{5,20},{6,23},{7,22},{8,25},{9,... | collective-permute-start | bytes 393224 | tf_op jit(solution)/shard_map/ppermute | solution.py:547
  53.5 3.7 %collective-permute-start.2 = (f32[2,8,128]{2,1,0:T(8,128)S(1)}, f32[2,8,128]{2,1,0:T(8,128)S(1)}, u32[]{:S(2)}, u32[]{:S(2)}) collective-permute-start(f32[2,8,128]{2,1,0:T(8,128)S(1)} %get-tuple-element.12), channel_id=1, source_target_pairs={{0,1},{1,0},{2,3},{3,2},{4,5},{5,4},{6,7},{7,6},{8,9},{9,8},{10,11... | collective-permute-start | bytes 24584 | tf_op jit(solution)/shard_map/ppermute | solution.py:564

commit v7 on v6

--- a/solution.py
+++ b/solution.py
@@ -124,8 +124,9 @@
     return [pl.BlockSpec(memory_space=pltpu.VMEM)] * count
 
 
-def spectra_body(half_ref, table_hbm, echo_hbm, out_hbm, table_ref, echo_ref, out_ref, table_sem, in_sem, out_sem):
-    members = out_ref.shape[0]
+def spectra_body(half_ref, place_ref, table_hbm, echo_hbm, *refs, apart):
+    *out_hbm, table_ref, echo_ref, out_ref, table_sem, in_sem, out_sem = refs
+    members = table_ref.shape[0]
     gates = echo_ref.shape[3]
     steps = in_sem.shape[0]
     block = echo_ref.shape[1] // steps
@@ -139,19 +140,26 @@
         )
         for step in range(steps)
     ]
-    stores = [
-        pltpu.make_async_copy(
-            out_ref.at[:, pl.ds(step * pairs, pairs)],
-            out_hbm.at[:, pl.ds(step * pairs, pairs)],
-            out_sem.at[step],
-        )
-        for step in range(steps)
-    ]
+    if apart:
+        stores = [
+            pltpu.make_async_copy(out_ref.at[n], out_hbm[n], out_sem.at[n]) for n in range(members)
+        ]
+    else:
+        stores = [
+            pltpu.make_async_copy(
+                out_ref.at[:, :, pl.ds(step * pairs, pairs)],
+                out_hbm[0].at[:, :, pl.ds(step * pairs, pairs)],
+                out_sem.at[step],
+            )
+            for step in range(steps)
+        ]
     fetch_table.start()
     for fetch in fetches:
         fetch.start()
     fetch_table.wait()
-    table = table_ref[...]
+    place = place_ref[0]
+    table = jnp.concatenate([table_ref[place ^ n if apart else n] for n in range(members)], axis=0)
+    sides = out_ref.shape[1]
     for step in range(steps):
         fetches[step].wait()
         for pair in range(step * pairs, (step + 1) * pairs):
@@ -164,43 +172,51 @@
                 axis=0,
             )
             bins = jnp.dot(table, samples, preferred_element_type=jnp.float32)
-            bins = bins.reshape(members, bins.shape[0] // members, 2 * gates)
-            rows = jnp.concatenate([bins[:, :, :gates], bins[:, :, gates:]], axis=1)
-            out_ref[:, pair] = rows.astype(jnp.bfloat16)
-        stores[step].start()
+            bins = bins.reshape(members, sides, bins.shape[0] // (members * sides), 2 * gates)
+            rows = jnp.concatenate([bins[..., :gates], bins[..., gates:]], axis=2)
+            out_ref[:, :, pair] = rows.astype(jnp.bfloat16)
+        if not apart:
+            stores[step].start()
+    if apart:
+        for store in stores:
+            store.start()
     for store in stores:
         store.wait()
 
 
-def spectra(half, echoes, devices, steps=STEPS):
+def spectra(half, place, echoes, members, sides, apart, steps=STEPS):
     _, elements, pulses, gates = echoes.shape
+    devices = 2 * members * sides
     bins = pulses // devices
-    members = devices // 2
     table = doppler_table(pulses)
     table = table.transpose(2, 1, 0, 3).reshape(devices, bins, 2, 2 * pulses)
-    table = table.transpose(0, 2, 1, 3).reshape(2, pulses, 2 * pulses)
-    shape = (members, elements // 2, 4 * bins, gates)
+    table = table.transpose(0, 2, 1, 3).reshape(2, members, sides * 2 * bins, 2 * pulses)
+    block = (sides, elements // 2, 4 * bins, gates)
+    anywhere = pl.BlockSpec(memory_space=pl.ANY)
+    count = members if apart else 1
+    shape = jax.ShapeDtypeStruct(block if apart else (members, *block), jnp.bfloat16)
     return pl.pallas_call(
-        spectra_body,
-        in_specs=[pl.BlockSpec(memory_space=pltpu.SMEM)] + [pl.BlockSpec(memory_space=pl.ANY)] * 2,
-        out_specs=pl.BlockSpec(memory_space=pl.ANY),
-        out_shape=jax.ShapeDtypeStruct(shape, jnp.bfloat16),
+        functools.partial(spectra_body, apart=apart),
+        in_specs=[pl.BlockSpec(memory_space=pltpu.SMEM)] * 2 + [anywhere, anywhere],
+        out_specs=[anywhere] * count,
+        out_shape=[shape] * count,
         scratch_shapes=[
-            pltpu.VMEM((pulses, 2 * pulses), jnp.bfloat16),
+            pltpu.VMEM(table.shape[1:], jnp.bfloat16),
             pltpu.VMEM(echoes.shape, jnp.bfloat16),
-            pltpu.VMEM(shape, jnp.bfloat16),
+            pltpu.VMEM((members, *block), jnp.bfloat16),
             pltpu.SemaphoreType.DMA(()),
             pltpu.SemaphoreType.DMA((steps,)),
-            pltpu.SemaphoreType.DMA((steps,)),
+            pltpu.SemaphoreType.DMA((members if apart else steps,)),
         ],
         compiler_params=pltpu.CompilerParams(vmem_limit_bytes=SPECTRA_VMEM),
         name="spectra",
-    )(half.reshape(1).astype(jnp.int32), jnp.asarray(table), echoes)
+    )(half, place, jnp.asarray(table), echoes)
 
 
 def spread_body(weight_ref, out_ref, *, bins):
     beams = weight_ref.shape[1]
     elements = weight_ref.shape[2]
+    own = out_ref.shape[2]
     group = 128
     width = group * 2 * bins
     lane = lax.broadcasted_iota(jnp.int32, (group, width), 1)
@@ -210,38 +226,36 @@
     is_real = (col // bins) % 2 == 0
     for at in range(elements // group):
         span = slice(at * group, (at + 1) * group)
-        here = slice(at * width, (at + 1) * width)
         real = jnp.dot(weight_ref[0, :, span], repeat, preferred_element_type=jnp.float32)
         imag = jnp.dot(weight_ref[1, :, span], repeat, preferred_element_type=jnp.float32)
-        out_ref[:beams, here] = jnp.where(is_real, real, -imag).astype(jnp.bfloat16)
-        out_ref[beams:, here] = jnp.where(is_real, imag, real).astype(jnp.bfloat16)
-
-
-def spread(beam_weights, bins):
+        to_real = jnp.where(is_real, real, -imag).astype(jnp.bfloat16)
+        to_imag = jnp.where(is_real, imag, real).astype(jnp.bfloat16)
+        for n in range(width // own):
+            out_ref[at * (width // own) + n, :beams] = to_real[:, n * own : (n + 1) * own]
+            out_ref[at * (width // own) + n, beams:] = to_imag[:, n * own : (n + 1) * own]
+
+
+def spread(beam_weights, bins, members):
     _, beams, elements = beam_weights.shape
     return pl.pallas_call(
         functools.partial(spread_body, bins=bins),
         in_specs=whole_vmem(1),
         out_specs=whole_vmem(1)[0],
-        out_shape=jax.ShapeDtypeStruct((2 * beams, elements * 2 * bins), jnp.bfloat16),
+        out_shape=jax.ShapeDtypeStruct((members, 2 * beams, elements // members * 2 * bins), jnp.bfloat16),
         compiler_params=pltpu.CompilerParams(vmem_limit_bytes=SMALL_VMEM),
         name="spread",
     )(beam_weights)
 
 
-def beam_sums(spectra_ref, spread_ref, bins):
-    elems, ranges = spectra_ref.shape[:2]
-    rows = spectra_ref.shape[2] * spectra_ref.shape[3]
+def beam_sums(blocks, weights, bins):
     received = jnp.concatenate(
         [
-            jnp.concatenate(
-                [spectra_ref[n, j].reshape(rows, spectra_ref.shape[4]) for n in range(elems)], axis=0
-            )
-            for j in range(ranges)
+            jnp.concatenate([block[j].reshape(-1, block.shape[3]) for block in blocks], axis=0)
+            for j in range(blocks[0].shape[0])
         ],
         axis=1,
     )
-    weights = spread_ref[...]
+    weights = jnp.concatenate(weights, axis=1)
     own = lax.broadcasted_iota(jnp.int32, weights.shape, 1) % bins
     return [
         jnp.dot(
@@ -253,25 +267,27 @@
     ]
 
 
-def crossing_body(side_ref, spectra_ref, spread_ref, same_ref, other_ref):
+def crossing_body(place_ref, side_ref, spread_ref, *refs):
+    *block_refs, same_ref, other_ref = refs
     bins, _, gates = same_ref.shape
-    first_side = side_ref[0] == 0
-    for d, value in enumerate(beam_sums(spectra_ref, spread_ref, bins)):
+    place, first_side = place_ref[0], side_ref[0] == 0
+    weights = [spread_ref[place ^ n] for n in range(len(block_refs))]
+    for d, value in enumerate(beam_sums([ref[...] for ref in block_refs], weights, bins)):
         first, second = value[:, :gates], value[:, gates:]
         same_ref[d] = jnp.where(first_side, first, second).astype(same_ref.dtype)
         other_ref[d] = jnp.where(first_side, second, first).astype(other_ref.dtype)
 
 
-def crossing_sums(side, bound, spread_weights, bins):
-    shape = jax.ShapeDtypeStruct((bins, spread_weights.shape[0], bound.shape[4]), jnp.bfloat16)
+def crossing_sums(place, side, blocks, spread_weights, bins):
+    shape = jax.ShapeDtypeStruct((bins, spread_weights.shape[1], blocks[0].shape[3]), jnp.bfloat16)
     return pl.pallas_call(
         crossing_body,
-        in_specs=[pl.BlockSpec(memory_space=pltpu.SMEM)] + whole_vmem(2),
+        in_specs=[pl.BlockSpec(memory_space=pltpu.SMEM)] * 2 + whole_vmem(1 + len(blocks)),
         out_specs=whole_vmem(2),
         out_shape=[shape, shape],
         compiler_params=pltpu.CompilerParams(vmem_limit_bytes=BEAMS_VMEM),
         name="crossing_sums",
-    )(side, bound, spread_weights)
+    )(place, side, spread_weights, *blocks)
 
 
 def split(value):
@@ -434,7 +450,8 @@
     ranges = spectra_ref.shape[1]
     gates = ranges * half
     first_side = side_ref[0] == 0
-    near = beam_sums(spectra_ref, spread_ref, bins)
+    members = range(spectra_ref.shape[0])
+    near = beam_sums([spectra_ref[n] for n in members], [spread_ref[n] for n in members], bins)
     sums = []
     for d in range(bins):
         same, other = same_ref[d].astype(jnp.float32), other_ref[d].astype(jnp.float32)
@@ -531,21 +548,32 @@
     side = lax.axis_index("range")
     half = lax.axis_index("elem") // (elems // 2)
     group = devices // 2
-    seat = side.reshape(1).astype(jnp.int32)
+    members = elems // 2
+    place, far_half, near_half, seat = (
+        value.reshape(1).astype(jnp.int32)
+        for value in (lax.axis_index("elem") % members, 1 - half, half, side)
+    )
     here = lax.dynamic_slice_in_dim(beam_weights, half * (elements // 2), elements // 2, 2)
-    spread_weights = spread(here, bins)
-
-    def exchanged(owner_half, axes, size):
-        groups = [list(range(size)), list(range(size, 2 * size))]
-        sent = spectra(owner_half, echoes, devices)
-        bound = lax.all_to_all(sent, axes, 0, 0, tiled=True, axis_index_groups=groups)
-        return bound.reshape(elems // 2, ranges, own_elements // 2, 4 * bins, gate_count)
-
-    same, other = crossing_sums(seat, exchanged(1 - half, "elem", elems // 2), spread_weights, bins)
+    spread_weights = spread(here, bins, members)
+    blocks = spectra(far_half, place, echoes, members, ranges, True)
+    blocks = [blocks[0]] + [
+        lax.ppermute(blocks[n], "elem", [(m, m ^ n) for m in range(elems)]) for n in range(1, members)
+    ]
+    (sent,) = spectra(near_half, place, echoes, members, ranges, False)
+    sent, *blocks[1:] = lax.optimization_barrier((sent, *blocks[1:]))
+    same, other = crossing_sums(place, seat, blocks, spread_weights, bins)
     across = [(n + group) % devices for n in range(devices)]
     same = lax.ppermute(same, ("elem", "range"), list(enumerate(across)))
     other = lax.ppermute(other, ("elem", "range"), [(n, to ^ 1) for n, to in enumerate(across)])
-    near = exchanged(half, ("elem", "range"), group)
+    near = lax.all_to_all(
+        sent.reshape(group, *sent.shape[2:]),
+        ("elem", "range"),
+        0,
+        0,
+        tiled=True,
+        axis_index_groups=[list(range(group)), list(range(group, devices))],
+    )
+    near = near.reshape(members, ranges, own_elements // 2, 4 * bins, gate_count)
     pulse = pulse_kernel(replica, gates)[:, :, :gates]
     pulse = pulse.reshape(2, 2, ranges, gate_count, ranges, gate_count)
     pulse = pulse.transpose(2, 0, 3, 4, 1, 5).reshape(2 * gates, 2 * gates)
@@ -574,6 +602,8 @@
         and gate_count % 128 == 0
         and beams == 64
         and elems % 2 == 0
+        and elems & (elems - 1) == 0
+        and 128 % echoes.shape[1] == 0
         and elements % 256 == 0
         and echoes.shape[1] % 8 == 0
         and replica.shape[1] <= gate_count

time: 58.1 us -> 56.8 us (0.978)
  waiting for transfers between devices: 29.2 us -> 26.7 us
  starting transfers between devices: 12.5 us -> 13.5 us
    all_to_all x2 -> x1, waiting for transfers between devices: 11.1 us -> 0.01 us  [on_device_owned(): lax.all_to_all(sent.reshape(group, *sent.shape[2:]), ('elem', 'range'), 0...]
    ppermute x0 -> x7, waiting for transfers between devices: none -> 8.71 us  [on_device_owned(): lax.ppermute(blocks[n], 'elem', [(m, m ^ n) for m in range(elems)])]
    ppermute x0 -> x7, starting transfers between devices: none -> 5.25 us  [on_device_owned(): lax.ppermute(blocks[n], 'elem', [(m, m ^ n) for m in range(elems)])]
    all_to_all x2 -> x1, starting transfers between devices: 8.51 us -> 4.28 us  [on_device_owned(): lax.all_to_all(sent.reshape(group, *sent.shape[2:]), ('elem', 'range'), 0...]
  transfers between devices with their start and end apart: 5 -> 11, of which waited for: 4 -> 7; matrix products, arithmetic and copies ran while one was open for 5% -> 5% of each run, Pallas kernels for 6% -> 7%
where the time goes in v7:
time: 56.8 us; the launch traced here: 56.5 us
  waiting for transfers between devices  26.7 us (47%)
  starting transfers between devices  13.5 us (24%)
  Pallas kernels  12.4 us (22%)
  local copies, waits for them, and re-layouts  2.81 us (5%)
  other arithmetic  0.89 us (2%)
    ppermute x1, waiting for transfers between devices, on_device_owned(): same = lax.ppermute(same, ('elem', 'range'), list(enumerate(across)))  10.6 us
    ppermute x7, waiting for transfers between devices, on_device_owned(): lax.ppermute(blocks[n], 'elem', [(m, m ^ n) for m in range(elems)])  8.71 us
    pallas_call x1, Pallas kernels, on_device_owned(): pl.pallas_call(beams_body, in_specs=[pl.BlockSpec(memory_space=pltpu.SMEM...  5.74 us
    pallas_call x2, Pallas kernels, spectra(): pl.pallas_call(functools.partial(spectra_body, apart=apart), in_specs=[pl...  5.65 us
    ppermute x7, starting transfers between devices, on_device_owned(): lax.ppermute(blocks[n], 'elem', [(m, m ^ n) for m in range(elems)])  5.25 us
    all_to_all x1, starting transfers between devices, on_device_owned(): lax.all_to_all(sent.reshape(group, *sent.shape[2:]), ('elem', 'range'), 0...  4.28 us
    ppermute x1, waiting for transfers between devices, on_device_owned(): lax.ppermute(other, ('elem', 'range'), [(n, to ^ 1) for n, to in enumerat...  3.77 us
    ppermute x1, waiting for transfers between devices, on_device_owned(): return own + lax.ppermute(send, 'range', [(0, 1), (1, 0)])  3.62 us
  transfers between devices with their start and end apart: 11, of which 7 were waited for; matrix products, arithmetic and copies ran while one was open for 5% of the time, Pallas kernels for 7%

profile of v7, /device:TPU:8, one launch (start us, length us, event | category | flops | bytes accessed | tf_op | source)
XLA Modules:
  0.0 56.5 jit_solution(8228110778604806399)
XLA Ops:
  0.0 3.0 %spectra.3 = (bf16[2,16,16,128]{3,2,1,0:T(8,128)(2,1)}, bf16[2,16,16,128]{3,2,1,0:T(8,128)(2,1)}, bf16[2,16,16,128]{3,2,1,0:T(8,128)(2,1)}, bf16[2,16,16,128]{3,...) custom-call(s32[1]{0:T(128)} %bitcast.3.half_ref, ...), custom_call_target="tpu_custom_call" | custom-call | tf_op jit(solution)/shard_map/spectra/pallas_call | solution.py:198
  3.0 1.6 %collective-permute-start.1 = (bf16[2,16,16,128]{3,2,1,0:T(8,128)(2,1)}, bf16[2,16,16,128]{3,2,1,0:T(8,128)(2,1)S(1)}, u32[]{:S(2)}, u32[]{:S(2)}) collective-permute-start(bf16[2,16,16,128]{3,2,1,0:T(8,128)(2,1)} %get-tuple-element.26), channel_id=1, source_target_pairs={{0,4},{2,6},{4,0},{6,2},{8,12},{10,14},{12,8},{14,10},{16,20},{18,... | collective-permute-start | bytes 393224 | tf_op jit(solution)/shard_map/ppermute | solution.py:560
  4.6 0.3 collective-permute-start.2
  4.9 0.2 collective-permute-start.3
  5.2 1.5 %collective-permute-start.4 = (bf16[2,16,16,128]{3,2,1,0:T(8,128)(2,1)}, bf16[2,16,16,128]{3,2,1,0:T(8,128)(2,1)S(1)}, u32[]{:S(2)}, u32[]{:S(2)}) collective-permute-start(bf16[2,16,16,128]{3,2,1,0:T(8,128)(2,1)} %get-tuple-element.29), channel_id=1, source_target_pairs={{0,10},{2,8},{4,14},{6,12},{8,2},{10,0},{12,6},{14,4},{16,26},{18,... | collective-permute-start | bytes 393224 | tf_op jit(solution)/shard_map/ppermute | solution.py:560
  6.6 1.4 %collective-permute-start.5 = (bf16[2,16,16,128]{3,2,1,0:T(8,128)(2,1)}, bf16[2,16,16,128]{3,2,1,0:T(8,128)(2,1)S(1)}, u32[]{:S(2)}, u32[]{:S(2)}) collective-permute-start(bf16[2,16,16,128]{3,2,1,0:T(8,128)(2,1)} %get-tuple-element.30), channel_id=1, source_target_pairs={{0,12},{2,14},{4,8},{6,10},{8,4},{10,6},{12,0},{14,2},{16,28},{18,... | collective-permute-start | bytes 393224 | tf_op jit(solution)/shard_map/ppermute | solution.py:560
  8.0 1.6 %collective-permute-done.1.refs_2_ = bf16[2,16,16,128]{3,2,1,0:T(8,128)(2,1)S(1)} collective-permute-done((bf16[2,16,16,128]{3,2,1,0:T(8,128)(2,1)}, bf16[2,16,16,128]{3,2,1,0:T(8,128)(2,1)S(1)}, u32[]{:S(2)}, u32[]{:S(2)}) %collective-permute-start.1) | collective-permute-done | bytes 131104 | tf_op jit(solution)/shard_map/ppermute | solution.py:560
  9.6 0.2 collective-permute-start.6
  9.8 2.7 %spectra.2 = bf16[8,2,16,16,128]{4,3,2,1,0:T(8,128)(2,1)} custom-call(s32[1]{0:T(128)} %bitcast.1.half_ref, s32[1]{0:T(128)} %bitcast.2.place_ref, bf16[2,8,16,256]{3,2,1,0:T(8,128)(2,1)} %constant.46.clone.table_hbm, bf16[2,32,128,128]{3,2,1,0:T(8,128)(2,1)} %echo_hbm.3), custom_call_target="tpu_custom_call" | custom-call | tf_op jit(solution)/shard_map/spectra/pallas_call | solution.py:198
  12.6 0.5 collective-permute-done.4.refs_5_
  13.1 4.9 %collective-permute-done.5.refs_6_ = bf16[2,16,16,128]{3,2,1,0:T(8,128)(2,1)S(1)} collective-permute-done((bf16[2,16,16,128]{3,2,1,0:T(8,128)(2,1)}, bf16[2,16,16,128]{3,2,1,0:T(8,128)(2,1)S(1)}, u32[]{:S(2)}, u32[]{:S(2)}) %collective-permute-start.5) | collective-permute-done | bytes 131104 | tf_op jit(solution)/shard_map/ppermute | solution.py:560
  18.0 1.7 %collective-permute-done.6.refs_7_ = bf16[2,16,16,128]{3,2,1,0:T(8,128)(2,1)S(1)} collective-permute-done((bf16[2,16,16,128]{3,2,1,0:T(8,128)(2,1)}, bf16[2,16,16,128]{3,2,1,0:T(8,128)(2,1)S(1)}, u32[]{:S(2)}, u32[]{:S(2)}) %collective-permute-start.6) | collective-permute-done | bytes 131104 | tf_op jit(solution)/shard_map/ppermute | solution.py:560
  19.7 4.3 %all-to-all-start = ((bf16[16,16,16,128]{3,2,1,0:T(8,128)(2,1)}), bf16[16,16,16,128]{3,2,1,0:T(8,128)(2,1)S(1)}, u32[]{:S(2)}, u32[]{:S(2)}) async-start(bf16[16,16,16,128]{3,2,1,0:T(8,128)(2,1)} %bitcast.38), calls=%async_computation | async-start | bytes 2097152 | tf_op jit(solution)/shard_map/all_to_all | solution.py:568
  24.0 0.3 spread.1.spread_ref
  24.3 0.3 tile.21
  24.6 0.4 reshape.40
  25.1 0.3 tile.9
  25.4 0.4 reshape.39
  25.9 0.1 maximum_bitcast_fusion
  26.1 0.7 %crossing_sums.1 = (bf16[4,128,128]{2,1,0:T(8,128)(2,1)S(1)}, bf16[4,128,128]{2,1,0:T(8,128)(2,1)S(1)}) custom-call(s32[1]{0:T(128)} %bitcast.2.place_ref, s32[1]{0:T(128)} %bitcast.side_ref, bf16[8,128,256]{2,1,0:T(8,128)(2,1)S(1)} %spread.1.spread_ref, bf16[2,16,16,128]{3,2,1,0:T(8,128)(2,1)S(1)} %copy-done.1, ...), custom_call_target="tpu_custom_call" | custom-call | tf_op jit(solution)/shard_map/crossing_sums/pallas_call | solution.py:283
  26.8 2.7 %collective-permute-start.7 = (bf16[4,128,128]{2,1,0:T(8,128)(2,1)S(1)}, bf16[4,128,128]{2,1,0:T(8,128)(2,1)S(1)}, u32[]{:S(2)}, u32[]{:S(2)}) collective-permute-start(bf16[4,128,128]{2,1,0:T(8,128)(2,1)S(1)} %get-tuple-element.41), channel_id=1, source_target_pairs={{0,16},{1,17},{2,18},{3,19},{4,20},{5,21},{6,22},{7,23},{8,24},{9,... | collective-permute-start | bytes 393224 | tf_op jit(solution)/shard_map/ppermute | solution.py:566
  29.5 1.2 %collective-permute-start.8 = (bf16[4,128,128]{2,1,0:T(8,128)(2,1)S(1)}, bf16[4,128,128]{2,1,0:T(8,128)(2,1)S(1)}, u32[]{:S(2)}, u32[]{:S(2)}) collective-permute-start(bf16[4,128,128]{2,1,0:T(8,128)(2,1)S(1)} %get-tuple-element.42), channel_id=1, source_target_pairs={{0,17},{1,16},{2,19},{3,18},{4,21},{5,20},{6,23},{7,22},{8,25},{9,... | collective-permute-start | bytes 393224 | tf_op jit(solution)/shard_map/ppermute | solution.py:567
  30.7 0.1 reshape.43
  30.8 1.0 %copy.8 = bf16[2,2,128,2,2,128]{5,4,3,2,1,0:T(2,128)(2,1)S(1)} copy(bf16[2,2,128,2,2,128]{2,0,5,3,4,1:T(2,128)(2,1)S(1)} %bitcast.39) | data formatting | bytes 1048576 | tf_op jit(solution)/shard_map/transpose | solution.py:579
  31.8 0.2 reshape.42.pulse_ref
  32.0 0.1 pad_maximum_fusion.1.steer_ref
  32.1 10.6 %collective-permute-done.7.same_ref = bf16[4,128,128]{2,1,0:T(8,128)(2,1)S(1)} collective-permute-done((bf16[4,128,128]{2,1,0:T(8,128)(2,1)S(1)}, bf16[4,128,128]{2,1,0:T(8,128)(2,1)S(1)}, u32[]{:S(2)}, u32[]{:S(2)}) %collective-permute-start.7) | collective-permute-done | bytes 131104 | tf_op jit(solution)/shard_map/ppermute | solution.py:566
  42.7 3.8 %collective-permute-done.8.other_ref = bf16[4,128,128]{2,1,0:T(8,128)(2,1)S(1)} collective-permute-done((bf16[4,128,128]{2,1,0:T(8,128)(2,1)S(1)}, bf16[4,128,128]{2,1,0:T(8,128)(2,1)S(1)}, u32[]{:S(2)}, u32[]{:S(2)}) %collective-permute-start.8) | collective-permute-done | bytes 131104 | tf_op jit(solution)/shard_map/ppermute | solution.py:567
  46.5 5.7 %beams.1 = (f32[2,8,128]{2,1,0:T(8,128)S(1)}, f32[2,8,128]{2,1,0:T(8,128)S(1)}) custom-call(s32[1]{0:T(128)} %bitcast.side_ref, bf16[8,2,16,16,128]{4,3,2,1,0:T(8,128)(2,1)S(1)} %bitcast.37, bf16[8,128,256]{2,1,0:T(8,128)(2,1)S(1)} %spread.1.spread_ref, bf16[4,128,128]{2,1,0:T(8,128)(2,1)S(1)} %collective-permute-done.7.same_ref, ...), custom_call_target="tpu_custom_call" | custom-call | tf_op jit(solution)/shard_map/beams/pallas_call | solution.py:583
  52.2 0.1 collective-permute-start.9
  52.3 3.6 %collective-permute-done.9 = f32[2,8,128]{2,1,0:T(8,128)S(1)} collective-permute-done((f32[2,8,128]{2,1,0:T(8,128)S(1)}, f32[2,8,128]{2,1,0:T(8,128)S(1)}, u32[]{:S(2)}, u32[]{:S(2)}) %collective-permute-start.9) | collective-permute-done | bytes 8224 | tf_op jit(solution)/shard_map/ppermute | solution.py:592
  55.9 0.6 %add.21 = f32[2,8,128]{2,1,0:T(8,128)} add(f32[2,8,128]{2,1,0:T(8,128)S(1)} %get-tuple-element.43, f32[2,8,128]{2,1,0:T(8,128)S(1)} %collective-permute-done.9) | non-fusion elementwise | flops 2048 | bytes 24576 | tf_op jit(solution)/shard_map/add | solution.py:592
  (22 shorter events, 0.2 us)
Async XLA Ops:
  0.0 24.0 %copy-start = (bf16[2,64,512]{2,1,0:T(8,128)(2,1)S(1)}, bf16[2,64,512]{2,1,0:T(8,128)(2,1)}, u32[]{:S(2)}) copy-start(bf16[2,64,512]{2,1,0:T(8,128)(2,1)} %param.8) | copy-start | bytes 393220
  3.0 3.6 %collective-permute-start = (bf16[2,16,16,128]{3,2,1,0:T(8,128)(2,1)}, bf16[2,16,16,128]{3,2,1,0:T(8,128)(2,1)S(1)}, u32[]{:S(2)}, u32[]{:S(2)}) collective-permute-start(bf16[2,16,16,128]{3,2,1,0:T(8,128)(2,1)} %get-tuple-element.25), channel_id=1, source_target_pairs={{0,2},{2,0},{4,6},{6,4},{8,10},{10,8},{12,14},{14,12},{16,18},{18,... | collective-permute-start | bytes 393224 | tf_op jit(solution)/shard_map/ppermute | solution.py:560
  3.0 6.6 %collective-permute-start.1 = (bf16[2,16,16,128]{3,2,1,0:T(8,128)(2,1)}, bf16[2,16,16,128]{3,2,1,0:T(8,128)(2,1)S(1)}, u32[]{:S(2)}, u32[]{:S(2)}) collective-permute-start(bf16[2,16,16,128]{3,2,1,0:T(8,128)(2,1)} %get-tuple-element.26), channel_id=1, source_target_pairs={{0,4},{2,6},{4,0},{6,2},{8,12},{10,14},{12,8},{14,10},{16,20},{18,... | collective-permute-start | bytes 393224 | tf_op jit(solution)/shard_map/ppermute | solution.py:560
  4.6 7.9 %collective-permute-start.2 = (bf16[2,16,16,128]{3,2,1,0:T(8,128)(2,1)}, bf16[2,16,16,128]{3,2,1,0:T(8,128)(2,1)S(1)}, u32[]{:S(2)}, u32[]{:S(2)}) collective-permute-start(bf16[2,16,16,128]{3,2,1,0:T(8,128)(2,1)} %get-tuple-element.27), channel_id=1, source_target_pairs={{0,6},{2,4},{4,2},{6,0},{8,14},{10,12},{12,10},{14,8},{16,22},{18,... | collective-permute-start | bytes 393224 | tf_op jit(solution)/shard_map/ppermute | solution.py:560
  4.9 7.7 %collective-permute-start.3 = (bf16[2,16,16,128]{3,2,1,0:T(8,128)(2,1)}, bf16[2,16,16,128]{3,2,1,0:T(8,128)(2,1)S(1)}, u32[]{:S(2)}, u32[]{:S(2)}) collective-permute-start(bf16[2,16,16,128]{3,2,1,0:T(8,128)(2,1)} %get-tuple-element.28), channel_id=1, source_target_pairs={{0,8},{2,10},{4,12},{6,14},{8,0},{10,2},{12,4},{14,6},{16,24},{18,... | collective-permute-start | bytes 393224 | tf_op jit(solution)/shard_map/ppermute | solution.py:560
  5.2 7.9 %collective-permute-start.4 = (bf16[2,16,16,128]{3,2,1,0:T(8,128)(2,1)}, bf16[2,16,16,128]{3,2,1,0:T(8,128)(2,1)S(1)}, u32[]{:S(2)}, u32[]{:S(2)}) collective-permute-start(bf16[2,16,16,128]{3,2,1,0:T(8,128)(2,1)} %get-tuple-element.29), channel_id=1, source_target_pairs={{0,10},{2,8},{4,14},{6,12},{8,2},{10,0},{12,6},{14,4},{16,26},{18,... | collective-permute-start | bytes 393224 | tf_op jit(solution)/shard_map/ppermute | solution.py:560
  6.6 11.4 %collective-permute-start.5 = (bf16[2,16,16,128]{3,2,1,0:T(8,128)(2,1)}, bf16[2,16,16,128]{3,2,1,0:T(8,128)(2,1)S(1)}, u32[]{:S(2)}, u32[]{:S(2)}) collective-permute-start(bf16[2,16,16,128]{3,2,1,0:T(8,128)(2,1)} %get-tuple-element.30), channel_id=1, source_target_pairs={{0,12},{2,14},{4,8},{6,10},{8,4},{10,6},{12,0},{14,2},{16,28},{18,... | collective-permute-start | bytes 393224 | tf_op jit(solution)/shard_map/ppermute | solution.py:560
  9.6 10.1 %collective-permute-start.6 = (bf16[2,16,16,128]{3,2,1,0:T(8,128)(2,1)}, bf16[2,16,16,128]{3,2,1,0:T(8,128)(2,1)S(1)}, u32[]{:S(2)}, u32[]{:S(2)}) collective-permute-start(bf16[2,16,16,128]{3,2,1,0:T(8,128)(2,1)} %get-tuple-element.31), channel_id=1, source_target_pairs={{0,14},{2,12},{4,10},{6,8},{8,6},{10,4},{12,2},{14,0},{16,30},{18,... | collective-permute-start | bytes 393224 | tf_op jit(solution)/shard_map/ppermute | solution.py:560
  12.5 11.7 %copy-start.3 = (bf16[2,64]{1,0:T(2,128)(2,1)S(1)}, bf16[2,64]{1,0:T(2,128)(2,1)}, u32[]{:S(2)}) copy-start(bf16[2,64]{1,0:T(2,128)(2,1)} %param.7) | copy-start | bytes 772
  19.7 26.8 %all-to-all-start = ((bf16[16,16,16,128]{3,2,1,0:T(8,128)(2,1)}), bf16[16,16,16,128]{3,2,1,0:T(8,128)(2,1)S(1)}, u32[]{:S(2)}, u32[]{:S(2)}) async-start(bf16[16,16,16,128]{3,2,1,0:T(8,128)(2,1)} %bitcast.38), calls=%async_computation | async-start | bytes 2097152 | tf_op jit(solution)/shard_map/all_to_all | solution.py:568
  25.0 1.0 %copy-start.1 = (bf16[2,16,16,128]{3,2,1,0:T(8,128)(2,1)S(1)}, bf16[2,16,16,128]{3,2,1,0:T(8,128)(2,1)}, u32[]{:S(2)}) copy-start(bf16[2,16,16,128]{3,2,1,0:T(8,128)(2,1)} %get-tuple-element.33.refs_0_) | copy-start | bytes 393220
  25.8 4.8 %copy-start.2 = (f32[2,8,64]{2,1,0:T(8,128)S(1)}, f32[2,8,64]{2,1,0:T(8,128)}, u32[]{:S(2)}) copy-start(f32[2,8,64]{2,1,0:T(8,128)} %param.9) | copy-start | bytes 12292
  26.8 15.9 %collective-permute-start.7 = (bf16[4,128,128]{2,1,0:T(8,128)(2,1)S(1)}, bf16[4,128,128]{2,1,0:T(8,128)(2,1)S(1)}, u32[]{:S(2)}, u32[]{:S(2)}) collective-permute-start(bf16[4,128,128]{2,1,0:T(8,128)(2,1)S(1)} %get-tuple-element.41), channel_id=1, source_target_pairs={{0,16},{1,17},{2,18},{3,19},{4,20},{5,21},{6,22},{7,23},{8,24},{9,... | collective-permute-start | bytes 393224 | tf_op jit(solution)/shard_map/ppermute | solution.py:566
  29.5 17.0 %collective-permute-start.8 = (bf16[4,128,128]{2,1,0:T(8,128)(2,1)S(1)}, bf16[4,128,128]{2,1,0:T(8,128)(2,1)S(1)}, u32[]{:S(2)}, u32[]{:S(2)}) collective-permute-start(bf16[4,128,128]{2,1,0:T(8,128)(2,1)S(1)} %get-tuple-element.42), channel_id=1, source_target_pairs={{0,17},{1,16},{2,19},{3,18},{4,21},{5,20},{6,23},{7,22},{8,25},{9,... | collective-permute-start | bytes 393224 | tf_op jit(solution)/shard_map/ppermute | solution.py:567
  52.2 3.7 %collective-permute-start.9 = (f32[2,8,128]{2,1,0:T(8,128)S(1)}, f32[2,8,128]{2,1,0:T(8,128)S(1)}, u32[]{:S(2)}, u32[]{:S(2)}) collective-permute-start(f32[2,8,128]{2,1,0:T(8,128)S(1)} %get-tuple-element.44), channel_id=1, source_target_pairs={{0,1},{1,0},{2,3},{3,2},{4,5},{5,4},{6,7},{7,6},{8,9},{9,8},{10,11... | collective-permute-start | bytes 24584 | tf_op jit(solution)/shard_map/ppermute | solution.py:592

commit v8 on v7

--- a/solution.py
+++ b/solution.py
@@ -122,6 +122,10 @@
 
 def whole_vmem(count):
     return [pl.BlockSpec(memory_space=pltpu.VMEM)] * count
+
+
+def far_first(members):
+    return [0] + sorted(range(1, members), key=lambda n: (-(n >> 1).bit_count(), n))
 
 
 def spectra_body(half_ref, place_ref, table_hbm, echo_hbm, *refs, apart):
@@ -158,7 +162,7 @@
         fetch.start()
     fetch_table.wait()
     place = place_ref[0]
-    table = jnp.concatenate([table_ref[place ^ n if apart else n] for n in range(members)], axis=0)
+    table = jnp.concatenate([table_ref[place ^ n if apart else n] for n in (far_first(members) if apart else range(members))], axis=0)
     sides = out_ref.shape[1]
     for step in range(steps):
         fetches[step].wait()
@@ -271,7 +275,7 @@
     *block_refs, same_ref, other_ref = refs
     bins, _, gates = same_ref.shape
     place, first_side = place_ref[0], side_ref[0] == 0
-    weights = [spread_ref[place ^ n] for n in range(len(block_refs))]
+    weights = [spread_ref[place ^ n] for n in far_first(len(block_refs))]
     for d, value in enumerate(beam_sums([ref[...] for ref in block_refs], weights, bins)):
         first, second = value[:, :gates], value[:, gates:]
         same_ref[d] = jnp.where(first_side, first, second).astype(same_ref.dtype)
@@ -556,8 +560,9 @@
     here = lax.dynamic_slice_in_dim(beam_weights, half * (elements // 2), elements // 2, 2)
     spread_weights = spread(here, bins, members)
     blocks = spectra(far_half, place, echoes, members, ranges, True)
-    blocks = [blocks[0]] + [
-        lax.ppermute(blocks[n], "elem", [(m, m ^ n) for m in range(elems)]) for n in range(1, members)
+    blocks = [
+        block if n == 0 else lax.ppermute(block, "elem", [(m, m ^ n) for m in range(elems)])
+        for n, block in zip(far_first(members), blocks)
     ]
     (sent,) = spectra(near_half, place, echoes, members, ranges, False)
     sent, *blocks[1:] = lax.optimization_barrier((sent, *blocks[1:]))

time: 56.8 us -> 55.9 us (0.984)
  waiting for transfers between devices: 26.7 us -> 23.9 us
  starting transfers between devices: 13.5 us -> 15.4 us
    ppermute x7, waiting for transfers between devices: 8.71 us -> 5.89 us  [on_device_owned(): lax.ppermute(block, 'elem', [(m, m ^ n) for m in range(elems)])]
    ppermute x7, starting transfers between devices: 5.25 us -> 6.23 us  [on_device_owned(): lax.ppermute(block, 'elem', [(m, m ^ n) for m in range(elems)])]
    all_to_all x1, starting transfers between devices: 4.28 us -> 5.21 us  [on_device_owned(): lax.all_to_all(sent.reshape(group, *sent.shape[2:]), ('elem', 'range'), 0...]
  transfers between devices with their start and end apart: 11 -> 11, of which waited for: 7 -> 6; matrix products, arithmetic and copies ran while one was open for 5% -> 6% of each run, Pallas kernels for 7% -> 7%
where the time goes in v8:
time: 55.9 us; the launch traced here: 55.6 us
  waiting for transfers between devices  23.9 us (43%)
  starting transfers between devices  15.4 us (28%)
  Pallas kernels  12.4 us (22%)
  local copies, waits for them, and re-layouts  2.81 us (5%)
  other arithmetic  0.89 us (2%)
    ppermute x1, waiting for transfers between devices, on_device_owned(): same = lax.ppermute(same, ('elem', 'range'), list(enumerate(across)))  10.6 us
    ppermute x7, starting transfers between devices, on_device_owned(): lax.ppermute(block, 'elem', [(m, m ^ n) for m in range(elems)])  6.23 us
    ppermute x7, waiting for transfers between devices, on_device_owned(): lax.ppermute(block, 'elem', [(m, m ^ n) for m in range(elems)])  5.89 us
    pallas_call x1, Pallas kernels, on_device_owned(): pl.pallas_call(beams_body, in_specs=[pl.BlockSpec(memory_space=pltpu.SMEM...  5.74 us
    pallas_call x2, Pallas kernels, spectra(): pl.pallas_call(functools.partial(spectra_body, apart=apart), in_specs=[pl...  5.65 us
    all_to_all x1, starting transfers between devices, on_device_owned(): lax.all_to_all(sent.reshape(group, *sent.shape[2:]), ('elem', 'range'), 0...  5.21 us
    ppermute x1, waiting for transfers between devices, on_device_owned(): lax.ppermute(other, ('elem', 'range'), [(n, to ^ 1) for n, to in enumerat...  3.77 us
    ppermute x1, waiting for transfers between devices, on_device_owned(): return own + lax.ppermute(send, 'range', [(0, 1), (1, 0)])  3.61 us
  transfers between devices with their start and end apart: 11, of which 6 were waited for; matrix products, arithmetic and copies ran while one was open for 6% of the time, Pallas kernels for 7%

profile of v8, /device:TPU:8, one launch (start us, length us, event | category | flops | bytes accessed | tf_op | source)
XLA Modules:
  0.0 55.6 jit_solution(1599719175553503761)
XLA Ops:
  0.0 3.0 %spectra.3 = (bf16[2,16,16,128]{3,2,1,0:T(8,128)(2,1)}, bf16[2,16,16,128]{3,2,1,0:T(8,128)(2,1)}, bf16[2,16,16,128]{3,2,1,0:T(8,128)(2,1)}, bf16[2,16,16,128]{3,...) custom-call(s32[1]{0:T(128)} %bitcast.3.half_ref, ...), custom_call_target="tpu_custom_call" | custom-call | tf_op jit(solution)/shard_map/spectra/pallas_call | solution.py:202
  3.0 1.5 %collective-permute-start = (bf16[2,16,16,128]{3,2,1,0:T(8,128)(2,1)}, bf16[2,16,16,128]{3,2,1,0:T(8,128)(2,1)S(1)}, u32[]{:S(2)}, u32[]{:S(2)}) collective-permute-start(bf16[2,16,16,128]{3,2,1,0:T(8,128)(2,1)} %get-tuple-element.25), channel_id=1, source_target_pairs={{0,12},{2,14},{4,8},{6,10},{8,4},{10,6},{12,0},{14,2},{16,28},{18,... | collective-permute-start | bytes 393224 | tf_op jit(solution)/shard_map/ppermute | solution.py:564
  4.4 0.7 %collective-permute-start.1 = (bf16[2,16,16,128]{3,2,1,0:T(8,128)(2,1)}, bf16[2,16,16,128]{3,2,1,0:T(8,128)(2,1)S(1)}, u32[]{:S(2)}, u32[]{:S(2)}) collective-permute-start(bf16[2,16,16,128]{3,2,1,0:T(8,128)(2,1)} %get-tuple-element.26), channel_id=1, source_target_pairs={{0,14},{2,12},{4,10},{6,8},{8,6},{10,4},{12,2},{14,0},{16,30},{18,... | collective-permute-start | bytes 393224 | tf_op jit(solution)/shard_map/ppermute | solution.py:564
  5.1 1.5 %collective-permute-start.2 = (bf16[2,16,16,128]{3,2,1,0:T(8,128)(2,1)}, bf16[2,16,16,128]{3,2,1,0:T(8,128)(2,1)S(1)}, u32[]{:S(2)}, u32[]{:S(2)}) collective-permute-start(bf16[2,16,16,128]{3,2,1,0:T(8,128)(2,1)} %get-tuple-element.27), channel_id=1, source_target_pairs={{0,4},{2,6},{4,0},{6,2},{8,12},{10,14},{12,8},{14,10},{16,20},{18,... | collective-permute-start | bytes 393224 | tf_op jit(solution)/shard_map/ppermute | solution.py:564
  6.6 0.8 %collective-permute-start.3 = (bf16[2,16,16,128]{3,2,1,0:T(8,128)(2,1)}, bf16[2,16,16,128]{3,2,1,0:T(8,128)(2,1)S(1)}, u32[]{:S(2)}, u32[]{:S(2)}) collective-permute-start(bf16[2,16,16,128]{3,2,1,0:T(8,128)(2,1)} %get-tuple-element.28), channel_id=1, source_target_pairs={{0,6},{2,4},{4,2},{6,0},{8,14},{10,12},{12,10},{14,8},{16,22},{18,... | collective-permute-start | bytes 393224 | tf_op jit(solution)/shard_map/ppermute | solution.py:564
  7.4 0.3 collective-permute-start.4
  7.7 2.7 %collective-permute-done.refs_1_ = bf16[2,16,16,128]{3,2,1,0:T(8,128)(2,1)S(1)} collective-permute-done((bf16[2,16,16,128]{3,2,1,0:T(8,128)(2,1)}, bf16[2,16,16,128]{3,2,1,0:T(8,128)(2,1)S(1)}, u32[]{:S(2)}, u32[]{:S(2)}) %collective-permute-start) | collective-permute-done | bytes 131104 | tf_op jit(solution)/shard_map/ppermute | solution.py:564
  10.4 1.1 %collective-permute-done.1.refs_2_ = bf16[2,16,16,128]{3,2,1,0:T(8,128)(2,1)S(1)} collective-permute-done((bf16[2,16,16,128]{3,2,1,0:T(8,128)(2,1)}, bf16[2,16,16,128]{3,2,1,0:T(8,128)(2,1)S(1)}, u32[]{:S(2)}, u32[]{:S(2)}) %collective-permute-start.1) | collective-permute-done | bytes 131104 | tf_op jit(solution)/shard_map/ppermute | solution.py:564
  11.4 1.5 %collective-permute-start.6 = (bf16[2,16,16,128]{3,2,1,0:T(8,128)(2,1)}, bf16[2,16,16,128]{3,2,1,0:T(8,128)(2,1)S(1)}, u32[]{:S(2)}, u32[]{:S(2)}) collective-permute-start(bf16[2,16,16,128]{3,2,1,0:T(8,128)(2,1)} %get-tuple-element.31), channel_id=1, source_target_pairs={{0,2},{2,0},{4,6},{6,4},{8,10},{10,8},{12,14},{14,12},{16,18},{18,... | collective-permute-start | bytes 393224 | tf_op jit(solution)/shard_map/ppermute | solution.py:564
  12.9 2.7 %spectra.2 = bf16[8,2,16,16,128]{4,3,2,1,0:T(8,128)(2,1)} custom-call(s32[1]{0:T(128)} %bitcast.1.half_ref, s32[1]{0:T(128)} %bitcast.2.place_ref, bf16[2,8,16,256]{3,2,1,0:T(8,128)(2,1)} %constant.46.clone.table_hbm, bf16[2,32,128,128]{3,2,1,0:T(8,128)(2,1)} %echo_hbm.3), custom_call_target="tpu_custom_call" | custom-call | tf_op jit(solution)/shard_map/spectra/pallas_call | solution.py:202
  15.6 0.0 copy-start.3
  15.7 2.2 %collective-permute-done.3.refs_4_ = bf16[2,16,16,128]{3,2,1,0:T(8,128)(2,1)S(1)} collective-permute-done((bf16[2,16,16,128]{3,2,1,0:T(8,128)(2,1)}, bf16[2,16,16,128]{3,2,1,0:T(8,128)(2,1)S(1)}, u32[]{:S(2)}, u32[]{:S(2)}) %collective-permute-start.3) | collective-permute-done | bytes 131104 | tf_op jit(solution)/shard_map/ppermute | solution.py:564
  17.8 5.2 %all-to-all-start = ((bf16[16,16,16,128]{3,2,1,0:T(8,128)(2,1)}), bf16[16,16,16,128]{3,2,1,0:T(8,128)(2,1)S(1)}, u32[]{:S(2)}, u32[]{:S(2)}) async-start(bf16[16,16,16,128]{3,2,1,0:T(8,128)(2,1)} %bitcast.38), calls=%async_computation | async-start | bytes 2097152 | tf_op jit(solution)/shard_map/all_to_all | solution.py:573
  23.1 0.3 spread.1.spread_ref
  23.4 0.3 tile.21
  23.7 0.4 reshape.40
  24.2 0.3 tile.9
  24.4 0.4 reshape.39
  24.9 0.1 maximum_bitcast_fusion
  25.1 0.7 %crossing_sums.1 = (bf16[4,128,128]{2,1,0:T(8,128)(2,1)S(1)}, bf16[4,128,128]{2,1,0:T(8,128)(2,1)S(1)}) custom-call(s32[1]{0:T(128)} %bitcast.2.place_ref, s32[1]{0:T(128)} %bitcast.side_ref, bf16[8,128,256]{2,1,0:T(8,128)(2,1)S(1)} %spread.1.spread_ref, bf16[2,16,16,128]{3,2,1,0:T(8,128)(2,1)S(1)} %copy-done.1, ...), custom_call_target="tpu_custom_call" | custom-call | tf_op jit(solution)/shard_map/crossing_sums/pallas_call | solution.py:287
  25.9 2.7 %collective-permute-start.7 = (bf16[4,128,128]{2,1,0:T(8,128)(2,1)S(1)}, bf16[4,128,128]{2,1,0:T(8,128)(2,1)S(1)}, u32[]{:S(2)}, u32[]{:S(2)}) collective-permute-start(bf16[4,128,128]{2,1,0:T(8,128)(2,1)S(1)} %get-tuple-element.41), channel_id=1, source_target_pairs={{0,16},{1,17},{2,18},{3,19},{4,20},{5,21},{6,22},{7,23},{8,24},{9,... | collective-permute-start | bytes 393224 | tf_op jit(solution)/shard_map/ppermute | solution.py:571
  28.5 1.2 %collective-permute-start.8 = (bf16[4,128,128]{2,1,0:T(8,128)(2,1)S(1)}, bf16[4,128,128]{2,1,0:T(8,128)(2,1)S(1)}, u32[]{:S(2)}, u32[]{:S(2)}) collective-permute-start(bf16[4,128,128]{2,1,0:T(8,128)(2,1)S(1)} %get-tuple-element.42), channel_id=1, source_target_pairs={{0,17},{1,16},{2,19},{3,18},{4,21},{5,20},{6,23},{7,22},{8,25},{9,... | collective-permute-start | bytes 393224 | tf_op jit(solution)/shard_map/ppermute | solution.py:572
  29.8 0.1 reshape.43
  29.9 1.0 %copy.8 = bf16[2,2,128,2,2,128]{5,4,3,2,1,0:T(2,128)(2,1)S(1)} copy(bf16[2,2,128,2,2,128]{2,0,5,3,4,1:T(2,128)(2,1)S(1)} %bitcast.39) | data formatting | bytes 1048576 | tf_op jit(solution)/shard_map/transpose | solution.py:584
  30.9 0.2 reshape.42.pulse_ref
  31.1 0.1 pad_maximum_fusion.1.steer_ref
  31.2 10.6 %collective-permute-done.7.same_ref = bf16[4,128,128]{2,1,0:T(8,128)(2,1)S(1)} collective-permute-done((bf16[4,128,128]{2,1,0:T(8,128)(2,1)S(1)}, bf16[4,128,128]{2,1,0:T(8,128)(2,1)S(1)}, u32[]{:S(2)}, u32[]{:S(2)}) %collective-permute-start.7) | collective-permute-done | bytes 131104 | tf_op jit(solution)/shard_map/ppermute | solution.py:571
  41.8 3.8 %collective-permute-done.8.other_ref = bf16[4,128,128]{2,1,0:T(8,128)(2,1)S(1)} collective-permute-done((bf16[4,128,128]{2,1,0:T(8,128)(2,1)S(1)}, bf16[4,128,128]{2,1,0:T(8,128)(2,1)S(1)}, u32[]{:S(2)}, u32[]{:S(2)}) %collective-permute-start.8) | collective-permute-done | bytes 131104 | tf_op jit(solution)/shard_map/ppermute | solution.py:572
  45.6 5.7 %beams.1 = (f32[2,8,128]{2,1,0:T(8,128)S(1)}, f32[2,8,128]{2,1,0:T(8,128)S(1)}) custom-call(s32[1]{0:T(128)} %bitcast.side_ref, bf16[8,2,16,16,128]{4,3,2,1,0:T(8,128)(2,1)S(1)} %bitcast.37, bf16[8,128,256]{2,1,0:T(8,128)(2,1)S(1)} %spread.1.spread_ref, bf16[4,128,128]{2,1,0:T(8,128)(2,1)S(1)} %collective-permute-done.7.same_ref, ...), custom_call_target="tpu_custom_call" | custom-call | tf_op jit(solution)/shard_map/beams/pallas_call | solution.py:588
  51.3 0.1 collective-permute-start.9
  51.4 3.6 %collective-permute-done.9 = f32[2,8,128]{2,1,0:T(8,128)S(1)} collective-permute-done((f32[2,8,128]{2,1,0:T(8,128)S(1)}, f32[2,8,128]{2,1,0:T(8,128)S(1)}, u32[]{:S(2)}, u32[]{:S(2)}) %collective-permute-start.9) | collective-permute-done | bytes 8224 | tf_op jit(solution)/shard_map/ppermute | solution.py:597
  55.0 0.6 %add.21 = f32[2,8,128]{2,1,0:T(8,128)} add(f32[2,8,128]{2,1,0:T(8,128)S(1)} %get-tuple-element.43, f32[2,8,128]{2,1,0:T(8,128)S(1)} %collective-permute-done.9) | non-fusion elementwise | flops 2048 | bytes 24576 | tf_op jit(solution)/shard_map/add | solution.py:597
  (22 shorter events, 0.2 us)
Async XLA Ops:
  0.0 23.0 %copy-start = (bf16[2,64,512]{2,1,0:T(8,128)(2,1)S(1)}, bf16[2,64,512]{2,1,0:T(8,128)(2,1)}, u32[]{:S(2)}) copy-start(bf16[2,64,512]{2,1,0:T(8,128)(2,1)} %param.8) | copy-start | bytes 393220
  3.0 7.4 %collective-permute-start = (bf16[2,16,16,128]{3,2,1,0:T(8,128)(2,1)}, bf16[2,16,16,128]{3,2,1,0:T(8,128)(2,1)S(1)}, u32[]{:S(2)}, u32[]{:S(2)}) collective-permute-start(bf16[2,16,16,128]{3,2,1,0:T(8,128)(2,1)} %get-tuple-element.25), channel_id=1, source_target_pairs={{0,12},{2,14},{4,8},{6,10},{8,4},{10,6},{12,0},{14,2},{16,28},{18,... | collective-permute-start | bytes 393224 | tf_op jit(solution)/shard_map/ppermute | solution.py:564
  4.4 7.0 %collective-permute-start.1 = (bf16[2,16,16,128]{3,2,1,0:T(8,128)(2,1)}, bf16[2,16,16,128]{3,2,1,0:T(8,128)(2,1)S(1)}, u32[]{:S(2)}, u32[]{:S(2)}) collective-permute-start(bf16[2,16,16,128]{3,2,1,0:T(8,128)(2,1)} %get-tuple-element.26), channel_id=1, source_target_pairs={{0,14},{2,12},{4,10},{6,8},{8,6},{10,4},{12,2},{14,0},{16,30},{18,... | collective-permute-start | bytes 393224 | tf_op jit(solution)/shard_map/ppermute | solution.py:564
  5.1 10.5 %collective-permute-start.2 = (bf16[2,16,16,128]{3,2,1,0:T(8,128)(2,1)}, bf16[2,16,16,128]{3,2,1,0:T(8,128)(2,1)S(1)}, u32[]{:S(2)}, u32[]{:S(2)}) collective-permute-start(bf16[2,16,16,128]{3,2,1,0:T(8,128)(2,1)} %get-tuple-element.27), channel_id=1, source_target_pairs={{0,4},{2,6},{4,0},{6,2},{8,12},{10,14},{12,8},{14,10},{16,20},{18,... | collective-permute-start | bytes 393224 | tf_op jit(solution)/shard_map/ppermute | solution.py:564
  6.6 11.2 %collective-permute-start.3 = (bf16[2,16,16,128]{3,2,1,0:T(8,128)(2,1)}, bf16[2,16,16,128]{3,2,1,0:T(8,128)(2,1)S(1)}, u32[]{:S(2)}, u32[]{:S(2)}) collective-permute-start(bf16[2,16,16,128]{3,2,1,0:T(8,128)(2,1)} %get-tuple-element.28), channel_id=1, source_target_pairs={{0,6},{2,4},{4,2},{6,0},{8,14},{10,12},{12,10},{14,8},{16,22},{18,... | collective-permute-start | bytes 393224 | tf_op jit(solution)/shard_map/ppermute | solution.py:564
  7.4 10.4 %collective-permute-start.4 = (bf16[2,16,16,128]{3,2,1,0:T(8,128)(2,1)}, bf16[2,16,16,128]{3,2,1,0:T(8,128)(2,1)S(1)}, u32[]{:S(2)}, u32[]{:S(2)}) collective-permute-start(bf16[2,16,16,128]{3,2,1,0:T(8,128)(2,1)} %get-tuple-element.29), channel_id=1, source_target_pairs={{0,8},{2,10},{4,12},{6,14},{8,0},{10,2},{12,4},{14,6},{16,24},{18,... | collective-permute-start | bytes 393224 | tf_op jit(solution)/shard_map/ppermute | solution.py:564
  10.4 7.5 %collective-permute-start.5 = (bf16[2,16,16,128]{3,2,1,0:T(8,128)(2,1)}, bf16[2,16,16,128]{3,2,1,0:T(8,128)(2,1)S(1)}, u32[]{:S(2)}, u32[]{:S(2)}) collective-permute-start(bf16[2,16,16,128]{3,2,1,0:T(8,128)(2,1)} %get-tuple-element.30), channel_id=1, source_target_pairs={{0,10},{2,8},{4,14},{6,12},{8,2},{10,0},{12,6},{14,4},{16,26},{18,... | collective-permute-start | bytes 393224 | tf_op jit(solution)/shard_map/ppermute | solution.py:564
  11.4 6.4 %collective-permute-start.6 = (bf16[2,16,16,128]{3,2,1,0:T(8,128)(2,1)}, bf16[2,16,16,128]{3,2,1,0:T(8,128)(2,1)S(1)}, u32[]{:S(2)}, u32[]{:S(2)}) collective-permute-start(bf16[2,16,16,128]{3,2,1,0:T(8,128)(2,1)} %get-tuple-element.31), channel_id=1, source_target_pairs={{0,2},{2,0},{4,6},{6,4},{8,10},{10,8},{12,14},{14,12},{16,18},{18,... | collective-permute-start | bytes 393224 | tf_op jit(solution)/shard_map/ppermute | solution.py:564
  15.6 7.7 %copy-start.3 = (bf16[2,64]{1,0:T(2,128)(2,1)S(1)}, bf16[2,64]{1,0:T(2,128)(2,1)}, u32[]{:S(2)}) copy-start(bf16[2,64]{1,0:T(2,128)(2,1)} %param.7) | copy-start | bytes 772
  17.8 27.7 %all-to-all-start = ((bf16[16,16,16,128]{3,2,1,0:T(8,128)(2,1)}), bf16[16,16,16,128]{3,2,1,0:T(8,128)(2,1)S(1)}, u32[]{:S(2)}, u32[]{:S(2)}) async-start(bf16[16,16,16,128]{3,2,1,0:T(8,128)(2,1)} %bitcast.38), calls=%async_computation | async-start | bytes 2097152 | tf_op jit(solution)/shard_map/all_to_all | solution.py:573
  24.1 1.0 %copy-start.1 = (bf16[2,16,16,128]{3,2,1,0:T(8,128)(2,1)S(1)}, bf16[2,16,16,128]{3,2,1,0:T(8,128)(2,1)}, u32[]{:S(2)}) copy-start(bf16[2,16,16,128]{3,2,1,0:T(8,128)(2,1)} %get-tuple-element.33.refs_0_) | copy-start | bytes 393220
  24.9 4.8 %copy-start.2 = (f32[2,8,64]{2,1,0:T(8,128)S(1)}, f32[2,8,64]{2,1,0:T(8,128)}, u32[]{:S(2)}) copy-start(f32[2,8,64]{2,1,0:T(8,128)} %param.9) | copy-start | bytes 12292
  25.9 15.9 %collective-permute-start.7 = (bf16[4,128,128]{2,1,0:T(8,128)(2,1)S(1)}, bf16[4,128,128]{2,1,0:T(8,128)(2,1)S(1)}, u32[]{:S(2)}, u32[]{:S(2)}) collective-permute-start(bf16[4,128,128]{2,1,0:T(8,128)(2,1)S(1)} %get-tuple-element.41), channel_id=1, source_target_pairs={{0,16},{1,17},{2,18},{3,19},{4,20},{5,21},{6,22},{7,23},{8,24},{9,... | collective-permute-start | bytes 393224 | tf_op jit(solution)/shard_map/ppermute | solution.py:571
  28.5 17.0 %collective-permute-start.8 = (bf16[4,128,128]{2,1,0:T(8,128)(2,1)S(1)}, bf16[4,128,128]{2,1,0:T(8,128)(2,1)S(1)}, u32[]{:S(2)}, u32[]{:S(2)}) collective-permute-start(bf16[4,128,128]{2,1,0:T(8,128)(2,1)S(1)} %get-tuple-element.42), channel_id=1, source_target_pairs={{0,17},{1,16},{2,19},{3,18},{4,21},{5,20},{6,23},{7,22},{8,25},{9,... | collective-permute-start | bytes 393224 | tf_op jit(solution)/shard_map/ppermute | solution.py:572
  51.3 3.7 %collective-permute-start.9 = (f32[2,8,128]{2,1,0:T(8,128)S(1)}, f32[2,8,128]{2,1,0:T(8,128)S(1)}, u32[]{:S(2)}, u32[]{:S(2)}) collective-permute-start(f32[2,8,128]{2,1,0:T(8,128)S(1)} %get-tuple-element.44), channel_id=1, source_target_pairs={{0,1},{1,0},{2,3},{3,2},{4,5},{5,4},{6,7},{7,6},{8,9},{9,8},{10,11... | collective-permute-start | bytes 24584 | tf_op jit(solution)/shard_map/ppermute | solution.py:597

commit v9 on v8

--- a/solution.py
+++ b/solution.py
@@ -125,7 +125,7 @@
 
 
 def far_first(members):
-    return [0] + sorted(range(1, members), key=lambda n: (-(n >> 1).bit_count(), n))
+    return [0] + sorted(range(1, members), key=lambda n: (-(n >> 1).bit_count(), n & 1, -n))
 
 
 def spectra_body(half_ref, place_ref, table_hbm, echo_hbm, *refs, apart):
@@ -365,6 +365,12 @@
     def col(x, k):
         return jnp.broadcast_to(x[:, k : k + 1], shape)
 
+    first = lane < beams
+    base = jnp.where(first, 0, beams)
+
+    def pick(x, k):
+        return jnp.take_along_axis(x, base + k, axis=1, mode="promise_in_bounds")
+
     for step, k in enumerate(columns):
         inside = ((lane >= k) & (lane < k + 4)) | ((lane >= beams + k) & (lane < beams + k + 4))
         pivot = []
@@ -388,12 +394,20 @@
                     tacc = tacc + (turned[l] * inv[j][l][0] - unit[l] * inv[j][l][1])
             b.append(acc)
             bt.append(tacc)
-        for q in updated(step):
+        same = [jnp.where(first, b[l], bt[l]) for l in range(4)]
+        cross = [-jnp.where(first, bt[l], b[l]) for l in range(4)]
+        for q in sorted(updated(step), key=lambda q: q // 2 != step + 1):
             x = rows[q]
-            acc = jnp.where(inside, 0.0, x)
-            for l in range(4):
-                acc = acc - (col(x, k + l) * b[l] + col(x, beams + k + l) * bt[l])
-            rows[q] = acc
+            kept = jnp.where(inside, 0.0, x)
+            if q // 2 == step + 1:
+                for l in range(4):
+                    kept = kept - (col(x, k + l) * b[l] + col(x, beams + k + l) * bt[l])
+                rows[q] = kept
+            else:
+                both = [pick(x, k + l) for l in range(4)]
+                straight = (both[0] * same[0] + both[1] * same[1]) + (both[2] * same[2] + both[3] * same[3])
+                swapped = (both[0] * cross[0] + both[1] * cross[1]) + (both[2] * cross[2] + both[3] * cross[3])
+                rows[q] = (kept - straight) - pltpu.roll(swapped, beams, 1)
         for q in (0, 1):
             rows[2 * step + q] = jnp.where(upper, b[2 * q], b[2 * q + 1])
     return rows

time: 55.9 us -> 55.6 us (level)
  starting transfers between devices: 15.4 us -> 16.5 us
  waiting for transfers between devices: 23.9 us -> 22.8 us
    ppermute x7, waiting for transfers between devices: 5.89 us -> 4.82 us  [on_device_owned(): lax.ppermute(block, 'elem', [(m, m ^ n) for m in range(elems)])]
    ppermute x7, starting transfers between devices: 6.23 us -> 7.21 us  [on_device_owned(): lax.ppermute(block, 'elem', [(m, m ^ n) for m in range(elems)])]
  transfers between devices with their start and end apart: 11 -> 11, of which waited for: 6 -> 8; matrix products, arithmetic and copies ran while one was open for 6% -> 6% of each run, Pallas kernels for 7% -> 7%
where the time goes in v9:
time: 55.6 us; the launch traced here: 55.4 us
  waiting for transfers between devices  22.8 us (41%)
  starting transfers between devices  16.5 us (30%)
  Pallas kernels  12.2 us (22%)
  local copies, waits for them, and re-layouts  2.81 us (5%)
  other arithmetic  0.89 us (2%)
    ppermute x1, waiting for transfers between devices, on_device_owned(): same = lax.ppermute(same, ('elem', 'range'), list(enumerate(across)))  10.6 us
    ppermute x7, starting transfers between devices, on_device_owned(): lax.ppermute(block, 'elem', [(m, m ^ n) for m in range(elems)])  7.21 us
    pallas_call x2, Pallas kernels, spectra(): pl.pallas_call(functools.partial(spectra_body, apart=apart), in_specs=[pl...  5.65 us
    pallas_call x1, Pallas kernels, on_device_owned(): pl.pallas_call(beams_body, in_specs=[pl.BlockSpec(memory_space=pltpu.SMEM...  5.55 us
    all_to_all x1, starting transfers between devices, on_device_owned(): lax.all_to_all(sent.reshape(group, *sent.shape[2:]), ('elem', 'range'), 0...  5.26 us
    ppermute x7, waiting for transfers between devices, on_device_owned(): lax.ppermute(block, 'elem', [(m, m ^ n) for m in range(elems)])  4.82 us
    ppermute x1, waiting for transfers between devices, on_device_owned(): lax.ppermute(other, ('elem', 'range'), [(n, to ^ 1) for n, to in enumerat...  3.77 us
    ppermute x1, waiting for transfers between devices, on_device_owned(): return own + lax.ppermute(send, 'range', [(0, 1), (1, 0)])  3.61 us
  transfers between devices with their start and end apart: 11, of which 8 were waited for; matrix products, arithmetic and copies ran while one was open for 6% of the time, Pallas kernels for 7%

profile of v9, /device:TPU:8, one launch (start us, length us, event | category | flops | bytes accessed | tf_op | source)
XLA Modules:
  0.0 55.4 jit_solution(18130739434298939917)
XLA Ops:
  0.0 3.0 %spectra.3 = (bf16[2,16,16,128]{3,2,1,0:T(8,128)(2,1)}, bf16[2,16,16,128]{3,2,1,0:T(8,128)(2,1)}, bf16[2,16,16,128]{3,2,1,0:T(8,128)(2,1)}, bf16[2,16,16,128]{3,...) custom-call(s32[1]{0:T(128)} %bitcast.3.half_ref, ...), custom_call_target="tpu_custom_call" | custom-call | tf_op jit(solution)/shard_map/spectra/pallas_call | solution.py:202
  3.0 1.5 %collective-permute-start = (bf16[2,16,16,128]{3,2,1,0:T(8,128)(2,1)}, bf16[2,16,16,128]{3,2,1,0:T(8,128)(2,1)S(1)}, u32[]{:S(2)}, u32[]{:S(2)}) collective-permute-start(bf16[2,16,16,128]{3,2,1,0:T(8,128)(2,1)} %get-tuple-element.25), channel_id=1, source_target_pairs={{0,12},{2,14},{4,8},{6,10},{8,4},{10,6},{12,0},{14,2},{16,28},{18,... | collective-permute-start | bytes 393224 | tf_op jit(solution)/shard_map/ppermute | solution.py:578
  4.4 0.7 %collective-permute-start.1 = (bf16[2,16,16,128]{3,2,1,0:T(8,128)(2,1)}, bf16[2,16,16,128]{3,2,1,0:T(8,128)(2,1)S(1)}, u32[]{:S(2)}, u32[]{:S(2)}) collective-permute-start(bf16[2,16,16,128]{3,2,1,0:T(8,128)(2,1)} %get-tuple-element.26), channel_id=1, source_target_pairs={{0,14},{2,12},{4,10},{6,8},{8,6},{10,4},{12,2},{14,0},{16,30},{18,... | collective-permute-start | bytes 393224 | tf_op jit(solution)/shard_map/ppermute | solution.py:578
  5.1 0.9 %collective-permute-start.2 = (bf16[2,16,16,128]{3,2,1,0:T(8,128)(2,1)}, bf16[2,16,16,128]{3,2,1,0:T(8,128)(2,1)S(1)}, u32[]{:S(2)}, u32[]{:S(2)}) collective-permute-start(bf16[2,16,16,128]{3,2,1,0:T(8,128)(2,1)} %get-tuple-element.27), channel_id=1, source_target_pairs={{0,8},{2,10},{4,12},{6,14},{8,0},{10,2},{12,4},{14,6},{16,24},{18,... | collective-permute-start | bytes 393224 | tf_op jit(solution)/shard_map/ppermute | solution.py:578
  6.0 1.1 %collective-permute-start.3 = (bf16[2,16,16,128]{3,2,1,0:T(8,128)(2,1)}, bf16[2,16,16,128]{3,2,1,0:T(8,128)(2,1)S(1)}, u32[]{:S(2)}, u32[]{:S(2)}) collective-permute-start(bf16[2,16,16,128]{3,2,1,0:T(8,128)(2,1)} %get-tuple-element.28), channel_id=1, source_target_pairs={{0,4},{2,6},{4,0},{6,2},{8,12},{10,14},{12,8},{14,10},{16,20},{18,... | collective-permute-start | bytes 393224 | tf_op jit(solution)/shard_map/ppermute | solution.py:578
  7.1 1.6 %collective-permute-start.4 = (bf16[2,16,16,128]{3,2,1,0:T(8,128)(2,1)}, bf16[2,16,16,128]{3,2,1,0:T(8,128)(2,1)S(1)}, u32[]{:S(2)}, u32[]{:S(2)}) collective-permute-start(bf16[2,16,16,128]{3,2,1,0:T(8,128)(2,1)} %get-tuple-element.29), channel_id=1, source_target_pairs={{0,10},{2,8},{4,14},{6,12},{8,2},{10,0},{12,6},{14,4},{16,26},{18,... | collective-permute-start | bytes 393224 | tf_op jit(solution)/shard_map/ppermute | solution.py:578
  8.7 1.7 %collective-permute-done.refs_1_ = bf16[2,16,16,128]{3,2,1,0:T(8,128)(2,1)S(1)} collective-permute-done((bf16[2,16,16,128]{3,2,1,0:T(8,128)(2,1)}, bf16[2,16,16,128]{3,2,1,0:T(8,128)(2,1)S(1)}, u32[]{:S(2)}, u32[]{:S(2)}) %collective-permute-start) | collective-permute-done | bytes 131104 | tf_op jit(solution)/shard_map/ppermute | solution.py:578
  10.4 1.1 %collective-permute-done.1.refs_2_ = bf16[2,16,16,128]{3,2,1,0:T(8,128)(2,1)S(1)} collective-permute-done((bf16[2,16,16,128]{3,2,1,0:T(8,128)(2,1)}, bf16[2,16,16,128]{3,2,1,0:T(8,128)(2,1)S(1)}, u32[]{:S(2)}, u32[]{:S(2)}) %collective-permute-start.1) | collective-permute-done | bytes 131104 | tf_op jit(solution)/shard_map/ppermute | solution.py:578
  11.4 1.5 %collective-permute-start.6 = (bf16[2,16,16,128]{3,2,1,0:T(8,128)(2,1)}, bf16[2,16,16,128]{3,2,1,0:T(8,128)(2,1)S(1)}, u32[]{:S(2)}, u32[]{:S(2)}) collective-permute-start(bf16[2,16,16,128]{3,2,1,0:T(8,128)(2,1)} %get-tuple-element.31), channel_id=1, source_target_pairs={{0,2},{2,0},{4,6},{6,4},{8,10},{10,8},{12,14},{14,12},{16,18},{18,... | collective-permute-start | bytes 393224 | tf_op jit(solution)/shard_map/ppermute | solution.py:578
  12.9 2.7 %spectra.2 = bf16[8,2,16,16,128]{4,3,2,1,0:T(8,128)(2,1)} custom-call(s32[1]{0:T(128)} %bitcast.1.half_ref, s32[1]{0:T(128)} %bitcast.2.place_ref, bf16[2,8,16,256]{3,2,1,0:T(8,128)(2,1)} %constant.46.clone.table_hbm, bf16[2,32,128,128]{3,2,1,0:T(8,128)(2,1)} %echo_hbm.3), custom_call_target="tpu_custom_call" | custom-call | tf_op jit(solution)/shard_map/spectra/pallas_call | solution.py:202
  15.6 0.6 %collective-permute-done.2.refs_3_ = bf16[2,16,16,128]{3,2,1,0:T(8,128)(2,1)S(1)} collective-permute-done((bf16[2,16,16,128]{3,2,1,0:T(8,128)(2,1)}, bf16[2,16,16,128]{3,2,1,0:T(8,128)(2,1)S(1)}, u32[]{:S(2)}, u32[]{:S(2)}) %collective-permute-start.2) | collective-permute-done | bytes 131104 | tf_op jit(solution)/shard_map/ppermute | solution.py:578
  16.2 0.5 collective-permute-done.4.refs_5_
  16.8 1.0 %collective-permute-done.5.refs_6_ = bf16[2,16,16,128]{3,2,1,0:T(8,128)(2,1)S(1)} collective-permute-done((bf16[2,16,16,128]{3,2,1,0:T(8,128)(2,1)}, bf16[2,16,16,128]{3,2,1,0:T(8,128)(2,1)S(1)}, u32[]{:S(2)}, u32[]{:S(2)}) %collective-permute-start.5) | collective-permute-done | bytes 131104 | tf_op jit(solution)/shard_map/ppermute | solution.py:578
  17.7 5.3 %all-to-all-start = ((bf16[16,16,16,128]{3,2,1,0:T(8,128)(2,1)}), bf16[16,16,16,128]{3,2,1,0:T(8,128)(2,1)S(1)}, u32[]{:S(2)}, u32[]{:S(2)}) async-start(bf16[16,16,16,128]{3,2,1,0:T(8,128)(2,1)} %bitcast.38), calls=%async_computation | async-start | bytes 2097152 | tf_op jit(solution)/shard_map/all_to_all | solution.py:587
  23.0 0.3 spread.1.spread_ref
  23.4 0.3 tile.21
  23.6 0.4 reshape.40
  24.1 0.3 tile.9
  24.4 0.4 reshape.39
  24.9 0.1 maximum_bitcast_fusion
  25.1 0.7 %crossing_sums.1 = (bf16[4,128,128]{2,1,0:T(8,128)(2,1)S(1)}, bf16[4,128,128]{2,1,0:T(8,128)(2,1)S(1)}) custom-call(s32[1]{0:T(128)} %bitcast.2.place_ref, s32[1]{0:T(128)} %bitcast.side_ref, bf16[8,128,256]{2,1,0:T(8,128)(2,1)S(1)} %spread.1.spread_ref, bf16[2,16,16,128]{3,2,1,0:T(8,128)(2,1)S(1)} %copy-done.1, ...), custom_call_target="tpu_custom_call" | custom-call | tf_op jit(solution)/shard_map/crossing_sums/pallas_call | solution.py:287
  25.8 2.7 %collective-permute-start.7 = (bf16[4,128,128]{2,1,0:T(8,128)(2,1)S(1)}, bf16[4,128,128]{2,1,0:T(8,128)(2,1)S(1)}, u32[]{:S(2)}, u32[]{:S(2)}) collective-permute-start(bf16[4,128,128]{2,1,0:T(8,128)(2,1)S(1)} %get-tuple-element.41), channel_id=1, source_target_pairs={{0,16},{1,17},{2,18},{3,19},{4,20},{5,21},{6,22},{7,23},{8,24},{9,... | collective-permute-start | bytes 393224 | tf_op jit(solution)/shard_map/ppermute | solution.py:585
  28.5 1.2 %collective-permute-start.8 = (bf16[4,128,128]{2,1,0:T(8,128)(2,1)S(1)}, bf16[4,128,128]{2,1,0:T(8,128)(2,1)S(1)}, u32[]{:S(2)}, u32[]{:S(2)}) collective-permute-start(bf16[4,128,128]{2,1,0:T(8,128)(2,1)S(1)} %get-tuple-element.42), channel_id=1, source_target_pairs={{0,17},{1,16},{2,19},{3,18},{4,21},{5,20},{6,23},{7,22},{8,25},{9,... | collective-permute-start | bytes 393224 | tf_op jit(solution)/shard_map/ppermute | solution.py:586
  29.7 0.1 reshape.43
  29.9 1.0 %copy.8 = bf16[2,2,128,2,2,128]{5,4,3,2,1,0:T(2,128)(2,1)S(1)} copy(bf16[2,2,128,2,2,128]{2,0,5,3,4,1:T(2,128)(2,1)S(1)} %bitcast.39) | data formatting | bytes 1048576 | tf_op jit(solution)/shard_map/transpose | solution.py:598
  30.8 0.2 reshape.42.pulse_ref
  31.1 10.6 %collective-permute-done.7.same_ref = bf16[4,128,128]{2,1,0:T(8,128)(2,1)S(1)} collective-permute-done((bf16[4,128,128]{2,1,0:T(8,128)(2,1)S(1)}, bf16[4,128,128]{2,1,0:T(8,128)(2,1)S(1)}, u32[]{:S(2)}, u32[]{:S(2)}) %collective-permute-start.7) | collective-permute-done | bytes 131104 | tf_op jit(solution)/shard_map/ppermute | solution.py:585
  41.7 3.8 %collective-permute-done.8.other_ref = bf16[4,128,128]{2,1,0:T(8,128)(2,1)S(1)} collective-permute-done((bf16[4,128,128]{2,1,0:T(8,128)(2,1)S(1)}, bf16[4,128,128]{2,1,0:T(8,128)(2,1)S(1)}, u32[]{:S(2)}, u32[]{:S(2)}) %collective-permute-start.8) | collective-permute-done | bytes 131104 | tf_op jit(solution)/shard_map/ppermute | solution.py:586
  45.5 5.5 %beams.1 = (f32[2,8,128]{2,1,0:T(8,128)S(1)}, f32[2,8,128]{2,1,0:T(8,128)S(1)}) custom-call(s32[1]{0:T(128)} %bitcast.side_ref, bf16[8,2,16,16,128]{4,3,2,1,0:T(8,128)(2,1)S(1)} %bitcast.37, bf16[8,128,256]{2,1,0:T(8,128)(2,1)S(1)} %spread.1.spread_ref, bf16[4,128,128]{2,1,0:T(8,128)(2,1)S(1)} %collective-permute-done.7.same_ref, ...), custom_call_target="tpu_custom_call" | custom-call | tf_op jit(solution)/shard_map/beams/pallas_call | solution.py:602
  51.1 0.1 collective-permute-start.9
  51.2 3.6 %collective-permute-done.9 = f32[2,8,128]{2,1,0:T(8,128)S(1)} collective-permute-done((f32[2,8,128]{2,1,0:T(8,128)S(1)}, f32[2,8,128]{2,1,0:T(8,128)S(1)}, u32[]{:S(2)}, u32[]{:S(2)}) %collective-permute-start.9) | collective-permute-done | bytes 8224 | tf_op jit(solution)/shard_map/ppermute | solution.py:611
  54.8 0.6 %add.21 = f32[2,8,128]{2,1,0:T(8,128)} add(f32[2,8,128]{2,1,0:T(8,128)S(1)} %get-tuple-element.43, f32[2,8,128]{2,1,0:T(8,128)S(1)} %collective-permute-done.9) | non-fusion elementwise | flops 2048 | bytes 24576 | tf_op jit(solution)/shard_map/add | solution.py:611
  (22 shorter events, 0.2 us)
Async XLA Ops:
  0.0 23.0 %copy-start = (bf16[2,64,512]{2,1,0:T(8,128)(2,1)S(1)}, bf16[2,64,512]{2,1,0:T(8,128)(2,1)}, u32[]{:S(2)}) copy-start(bf16[2,64,512]{2,1,0:T(8,128)(2,1)} %param.8) | copy-start | bytes 393220
  3.0 7.4 %collective-permute-start = (bf16[2,16,16,128]{3,2,1,0:T(8,128)(2,1)}, bf16[2,16,16,128]{3,2,1,0:T(8,128)(2,1)S(1)}, u32[]{:S(2)}, u32[]{:S(2)}) collective-permute-start(bf16[2,16,16,128]{3,2,1,0:T(8,128)(2,1)} %get-tuple-element.25), channel_id=1, source_target_pairs={{0,12},{2,14},{4,8},{6,10},{8,4},{10,6},{12,0},{14,2},{16,28},{18,... | collective-permute-start | bytes 393224 | tf_op jit(solution)/shard_map/ppermute | solution.py:578
  4.4 7.0 %collective-permute-start.1 = (bf16[2,16,16,128]{3,2,1,0:T(8,128)(2,1)}, bf16[2,16,16,128]{3,2,1,0:T(8,128)(2,1)S(1)}, u32[]{:S(2)}, u32[]{:S(2)}) collective-permute-start(bf16[2,16,16,128]{3,2,1,0:T(8,128)(2,1)} %get-tuple-element.26), channel_id=1, source_target_pairs={{0,14},{2,12},{4,10},{6,8},{8,6},{10,4},{12,2},{14,0},{16,30},{18,... | collective-permute-start | bytes 393224 | tf_op jit(solution)/shard_map/ppermute | solution.py:578
  5.1 11.1 %collective-permute-start.2 = (bf16[2,16,16,128]{3,2,1,0:T(8,128)(2,1)}, bf16[2,16,16,128]{3,2,1,0:T(8,128)(2,1)S(1)}, u32[]{:S(2)}, u32[]{:S(2)}) collective-permute-start(bf16[2,16,16,128]{3,2,1,0:T(8,128)(2,1)} %get-tuple-element.27), channel_id=1, source_target_pairs={{0,8},{2,10},{4,12},{6,14},{8,0},{10,2},{12,4},{14,6},{16,24},{18,... | collective-permute-start | bytes 393224 | tf_op jit(solution)/shard_map/ppermute | solution.py:578
  6.0 10.2 %collective-permute-start.3 = (bf16[2,16,16,128]{3,2,1,0:T(8,128)(2,1)}, bf16[2,16,16,128]{3,2,1,0:T(8,128)(2,1)S(1)}, u32[]{:S(2)}, u32[]{:S(2)}) collective-permute-start(bf16[2,16,16,128]{3,2,1,0:T(8,128)(2,1)} %get-tuple-element.28), channel_id=1, source_target_pairs={{0,4},{2,6},{4,0},{6,2},{8,12},{10,14},{12,8},{14,10},{16,20},{18,... | collective-permute-start | bytes 393224 | tf_op jit(solution)/shard_map/ppermute | solution.py:578
  7.1 9.7 %collective-permute-start.4 = (bf16[2,16,16,128]{3,2,1,0:T(8,128)(2,1)}, bf16[2,16,16,128]{3,2,1,0:T(8,128)(2,1)S(1)}, u32[]{:S(2)}, u32[]{:S(2)}) collective-permute-start(bf16[2,16,16,128]{3,2,1,0:T(8,128)(2,1)} %get-tuple-element.29), channel_id=1, source_target_pairs={{0,10},{2,8},{4,14},{6,12},{8,2},{10,0},{12,6},{14,4},{16,26},{18,... | collective-permute-start | bytes 393224 | tf_op jit(solution)/shard_map/ppermute | solution.py:578
  10.4 7.4 %collective-permute-start.5 = (bf16[2,16,16,128]{3,2,1,0:T(8,128)(2,1)}, bf16[2,16,16,128]{3,2,1,0:T(8,128)(2,1)S(1)}, u32[]{:S(2)}, u32[]{:S(2)}) collective-permute-start(bf16[2,16,16,128]{3,2,1,0:T(8,128)(2,1)} %get-tuple-element.30), channel_id=1, source_target_pairs={{0,6},{2,4},{4,2},{6,0},{8,14},{10,12},{12,10},{14,8},{16,22},{18,... | collective-permute-start | bytes 393224 | tf_op jit(solution)/shard_map/ppermute | solution.py:578
  11.4 6.3 %collective-permute-start.6 = (bf16[2,16,16,128]{3,2,1,0:T(8,128)(2,1)}, bf16[2,16,16,128]{3,2,1,0:T(8,128)(2,1)S(1)}, u32[]{:S(2)}, u32[]{:S(2)}) collective-permute-start(bf16[2,16,16,128]{3,2,1,0:T(8,128)(2,1)} %get-tuple-element.31), channel_id=1, source_target_pairs={{0,2},{2,0},{4,6},{6,4},{8,10},{10,8},{12,14},{14,12},{16,18},{18,... | collective-permute-start | bytes 393224 | tf_op jit(solution)/shard_map/ppermute | solution.py:578
  15.6 7.7 %copy-start.3 = (bf16[2,64]{1,0:T(2,128)(2,1)S(1)}, bf16[2,64]{1,0:T(2,128)(2,1)}, u32[]{:S(2)}) copy-start(bf16[2,64]{1,0:T(2,128)(2,1)} %param.7) | copy-start | bytes 772
  17.7 27.8 %all-to-all-start = ((bf16[16,16,16,128]{3,2,1,0:T(8,128)(2,1)}), bf16[16,16,16,128]{3,2,1,0:T(8,128)(2,1)S(1)}, u32[]{:S(2)}, u32[]{:S(2)}) async-start(bf16[16,16,16,128]{3,2,1,0:T(8,128)(2,1)} %bitcast.38), calls=%async_computation | async-start | bytes 2097152 | tf_op jit(solution)/shard_map/all_to_all | solution.py:587
  24.1 1.0 %copy-start.1 = (bf16[2,16,16,128]{3,2,1,0:T(8,128)(2,1)S(1)}, bf16[2,16,16,128]{3,2,1,0:T(8,128)(2,1)}, u32[]{:S(2)}) copy-start(bf16[2,16,16,128]{3,2,1,0:T(8,128)(2,1)} %get-tuple-element.33.refs_0_) | copy-start | bytes 393220
  24.9 4.8 %copy-start.2 = (f32[2,8,64]{2,1,0:T(8,128)S(1)}, f32[2,8,64]{2,1,0:T(8,128)}, u32[]{:S(2)}) copy-start(f32[2,8,64]{2,1,0:T(8,128)} %param.9) | copy-start | bytes 12292
  25.8 15.9 %collective-permute-start.7 = (bf16[4,128,128]{2,1,0:T(8,128)(2,1)S(1)}, bf16[4,128,128]{2,1,0:T(8,128)(2,1)S(1)}, u32[]{:S(2)}, u32[]{:S(2)}) collective-permute-start(bf16[4,128,128]{2,1,0:T(8,128)(2,1)S(1)} %get-tuple-element.41), channel_id=1, source_target_pairs={{0,16},{1,17},{2,18},{3,19},{4,20},{5,21},{6,22},{7,23},{8,24},{9,... | collective-permute-start | bytes 393224 | tf_op jit(solution)/shard_map/ppermute | solution.py:585
  28.5 17.0 %collective-permute-start.8 = (bf16[4,128,128]{2,1,0:T(8,128)(2,1)S(1)}, bf16[4,128,128]{2,1,0:T(8,128)(2,1)S(1)}, u32[]{:S(2)}, u32[]{:S(2)}) collective-permute-start(bf16[4,128,128]{2,1,0:T(8,128)(2,1)S(1)} %get-tuple-element.42), channel_id=1, source_target_pairs={{0,17},{1,16},{2,19},{3,18},{4,21},{5,20},{6,23},{7,22},{8,25},{9,... | collective-permute-start | bytes 393224 | tf_op jit(solution)/shard_map/ppermute | solution.py:586
  51.1 3.7 %collective-permute-start.9 = (f32[2,8,128]{2,1,0:T(8,128)S(1)}, f32[2,8,128]{2,1,0:T(8,128)S(1)}, u32[]{:S(2)}, u32[]{:S(2)}) collective-permute-start(f32[2,8,128]{2,1,0:T(8,128)S(1)} %get-tuple-element.44), channel_id=1, source_target_pairs={{0,1},{1,0},{2,3},{3,2},{4,5},{5,4},{6,7},{7,6},{8,9},{9,8},{10,11... | collective-permute-start | bytes 24584 | tf_op jit(solution)/shard_map/ppermute | solution.py:611

commit v10 on v9

--- a/solution.py
+++ b/solution.py
@@ -578,8 +578,15 @@
         block if n == 0 else lax.ppermute(block, "elem", [(m, m ^ n) for m in range(elems)])
         for n, block in zip(far_first(members), blocks)
     ]
+    pulse = pulse_kernel(replica, gates)[:, :, :gates]
+    pulse = pulse.reshape(2, 2, ranges, gate_count, ranges, gate_count)
+    pulse = pulse.transpose(2, 0, 3, 4, 1, 5).reshape(2 * gates, 2 * gates)
+    own_steering = lax.dynamic_slice_in_dim(steering, side * bins, bins, 1)
+    steer_row = jnp.concatenate([own_steering[0], -own_steering[1]], axis=1)
     (sent,) = spectra(near_half, place, echoes, members, ranges, False)
-    sent, *blocks[1:] = lax.optimization_barrier((sent, *blocks[1:]))
+    sent, spread_weights, pulse, steer_row, *blocks[1:] = lax.optimization_barrier(
+        (sent, spread_weights, pulse, steer_row, *blocks[1:])
+    )
     same, other = crossing_sums(place, seat, blocks, spread_weights, bins)
     across = [(n + group) % devices for n in range(devices)]
     same = lax.ppermute(same, ("elem", "range"), list(enumerate(across)))
@@ -593,11 +600,6 @@
         axis_index_groups=[list(range(group)), list(range(group, devices))],
     )
     near = near.reshape(members, ranges, own_elements // 2, 4 * bins, gate_count)
-    pulse = pulse_kernel(replica, gates)[:, :, :gates]
-    pulse = pulse.reshape(2, 2, ranges, gate_count, ranges, gate_count)
-    pulse = pulse.transpose(2, 0, 3, 4, 1, 5).reshape(2 * gates, 2 * gates)
-    own_steering = lax.dynamic_slice_in_dim(steering, side * bins, bins, 1)
-    steer_row = jnp.concatenate([own_steering[0], -own_steering[1]], axis=1)
     shape = jax.ShapeDtypeStruct((2, 2 * bins, gate_count), jnp.float32)
     own, send = pl.pallas_call(
         beams_body,

time: 55.6 us -> 55.7 us (level)
    ppermute x7, waiting for transfers between devices: 4.82 us -> 0.98 us  [on_device_owned(): lax.ppermute(block, 'elem', [(m, m ^ n) for m in range(elems)])]
    ppermute x1, waiting for transfers between devices: 10.6 us -> 14.1 us  [on_device_owned(): same = lax.ppermute(same, ('elem', 'range'), list(enumerate(across)))]
  transfers between devices with their start and end apart: 11 -> 11, of which waited for: 8 -> 5; matrix products, arithmetic and copies ran while one was open for 6% -> 6% of each run, Pallas kernels for 7% -> 7%
where the time goes in v10:
time: 55.7 us; the launch traced here: 55.4 us
  waiting for transfers between devices  22.5 us (40%)
  starting transfers between devices  16.7 us (30%)
  Pallas kernels  12.3 us (22%)
  local copies, waits for them, and re-layouts  2.82 us (5%)
  other arithmetic  0.89 us (2%)
    ppermute x1, waiting for transfers between devices, on_device_owned(): same = lax.ppermute(same, ('elem', 'range'), list(enumerate(across)))  14.1 us
    ppermute x7, starting transfers between devices, on_device_owned(): lax.ppermute(block, 'elem', [(m, m ^ n) for m in range(elems)])  7.49 us
    pallas_call x2, Pallas kernels, spectra(): pl.pallas_call(functools.partial(spectra_body, apart=apart), in_specs=[pl...  5.7 us
    pallas_call x1, Pallas kernels, on_device_owned(): pl.pallas_call(beams_body, in_specs=[pl.BlockSpec(memory_space=pltpu.SMEM...  5.56 us
    all_to_all x1, starting transfers between devices, on_device_owned(): lax.all_to_all(sent.reshape(group, *sent.shape[2:]), ('elem', 'range'), 0...  5.26 us
    ppermute x1, waiting for transfers between devices, on_device_owned(): lax.ppermute(other, ('elem', 'range'), [(n, to ^ 1) for n, to in enumerat...  3.77 us
    ppermute x1, waiting for transfers between devices, on_device_owned(): return own + lax.ppermute(send, 'range', [(0, 1), (1, 0)])  3.62 us
    ppermute x1, starting transfers between devices, on_device_owned(): same = lax.ppermute(same, ('elem', 'range'), list(enumerate(across)))  2.66 us
  transfers between devices with their start and end apart: 11, of which 5 were waited for; matrix products, arithmetic and copies ran while one was open for 6% of the time, Pallas kernels for 7%

profile of v10, /device:TPU:8, one launch (start us, length us, event | category | flops | bytes accessed | tf_op | source)
XLA Modules:
  0.0 55.4 jit_solution(12523505626829858429)
XLA Ops:
  0.0 3.0 %spectra.3 = (bf16[2,16,16,128]{3,2,1,0:T(8,128)(2,1)}, bf16[2,16,16,128]{3,2,1,0:T(8,128)(2,1)}, bf16[2,16,16,128]{3,2,1,0:T(8,128)(2,1)}, bf16[2,16,16,128]{3,...) custom-call(s32[1]{0:T(128)} %bitcast.17.half_ref, ...), custom_call_target="tpu_custom_call" | custom-call | tf_op jit(solution)/shard_map/spectra/pallas_call | solution.py:202
  3.0 1.5 %collective-permute-start = (bf16[2,16,16,128]{3,2,1,0:T(8,128)(2,1)}, bf16[2,16,16,128]{3,2,1,0:T(8,128)(2,1)S(1)}, u32[]{:S(2)}, u32[]{:S(2)}) collective-permute-start(bf16[2,16,16,128]{3,2,1,0:T(8,128)(2,1)} %get-tuple-element.28), channel_id=1, source_target_pairs={{0,12},{2,14},{4,8},{6,10},{8,4},{10,6},{12,0},{14,2},{16,28},{18,... | collective-permute-start | bytes 393224 | tf_op jit(solution)/shard_map/ppermute | solution.py:578
  4.5 0.7 %collective-permute-start.1 = (bf16[2,16,16,128]{3,2,1,0:T(8,128)(2,1)}, bf16[2,16,16,128]{3,2,1,0:T(8,128)(2,1)S(1)}, u32[]{:S(2)}, u32[]{:S(2)}) collective-permute-start(bf16[2,16,16,128]{3,2,1,0:T(8,128)(2,1)} %get-tuple-element.29), channel_id=1, source_target_pairs={{0,14},{2,12},{4,10},{6,8},{8,6},{10,4},{12,2},{14,0},{16,30},{18,... | collective-permute-start | bytes 393224 | tf_op jit(solution)/shard_map/ppermute | solution.py:578
  5.1 0.9 %collective-permute-start.2 = (bf16[2,16,16,128]{3,2,1,0:T(8,128)(2,1)}, bf16[2,16,16,128]{3,2,1,0:T(8,128)(2,1)S(1)}, u32[]{:S(2)}, u32[]{:S(2)}) collective-permute-start(bf16[2,16,16,128]{3,2,1,0:T(8,128)(2,1)} %get-tuple-element.30), channel_id=1, source_target_pairs={{0,8},{2,10},{4,12},{6,14},{8,0},{10,2},{12,4},{14,6},{16,24},{18,... | collective-permute-start | bytes 393224 | tf_op jit(solution)/shard_map/ppermute | solution.py:578
  6.0 1.1 %collective-permute-start.3 = (bf16[2,16,16,128]{3,2,1,0:T(8,128)(2,1)}, bf16[2,16,16,128]{3,2,1,0:T(8,128)(2,1)S(1)}, u32[]{:S(2)}, u32[]{:S(2)}) collective-permute-start(bf16[2,16,16,128]{3,2,1,0:T(8,128)(2,1)} %get-tuple-element.31), channel_id=1, source_target_pairs={{0,4},{2,6},{4,0},{6,2},{8,12},{10,14},{12,8},{14,10},{16,20},{18,... | collective-permute-start | bytes 393224 | tf_op jit(solution)/shard_map/ppermute | solution.py:578
  7.1 1.6 %collective-permute-start.4 = (bf16[2,16,16,128]{3,2,1,0:T(8,128)(2,1)}, bf16[2,16,16,128]{3,2,1,0:T(8,128)(2,1)S(1)}, u32[]{:S(2)}, u32[]{:S(2)}) collective-permute-start(bf16[2,16,16,128]{3,2,1,0:T(8,128)(2,1)} %get-tuple-element.32), channel_id=1, source_target_pairs={{0,10},{2,8},{4,14},{6,12},{8,2},{10,0},{12,6},{14,4},{16,26},{18,... | collective-permute-start | bytes 393224 | tf_op jit(solution)/shard_map/ppermute | solution.py:578
  8.8 0.3 tile.21
  9.0 0.4 reshape.37
  9.5 0.0 copy-start.2
  9.6 0.3 tile.9
  9.9 0.4 reshape.36
  10.3 0.1 maximum_bitcast_fusion
  10.6 0.3 collective-permute-start.5
  10.8 0.6 %collective-permute-done.1.refs_2_ = bf16[2,16,16,128]{3,2,1,0:T(8,128)(2,1)S(1)} collective-permute-done((bf16[2,16,16,128]{3,2,1,0:T(8,128)(2,1)}, bf16[2,16,16,128]{3,2,1,0:T(8,128)(2,1)S(1)}, u32[]{:S(2)}, u32[]{:S(2)}) %collective-permute-start.1) | collective-permute-done | bytes 131104 | tf_op jit(solution)/shard_map/ppermute | solution.py:578
  11.4 1.5 %collective-permute-start.6 = (bf16[2,16,16,128]{3,2,1,0:T(8,128)(2,1)S(1)}, bf16[2,16,16,128]{3,2,1,0:T(8,128)(2,1)S(1)}, u32[]{:S(2)}, u32[]{:S(2)}) collective-permute-start(bf16[2,16,16,128]{3,2,1,0:T(8,128)(2,1)S(1)} %copy-done.4), channel_id=1, source_target_pairs={{0,2},{2,0},{4,6},{6,4},{8,10},{10,8},{12,14},{14,12},{16,18},{18,... | collective-permute-start | bytes 393224 | tf_op jit(solution)/shard_map/ppermute | solution.py:578
  13.0 2.7 %spectra.2 = bf16[8,2,16,16,128]{4,3,2,1,0:T(8,128)(2,1)} custom-call(s32[1]{0:T(128)} %bitcast.1.half_ref, s32[1]{0:T(128)} %bitcast.2.place_ref, bf16[2,8,16,256]{3,2,1,0:T(8,128)(2,1)} %constant.46.clone.table_hbm, bf16[2,32,128,128]{3,2,1,0:T(8,128)(2,1)} %echo_hbm.3), custom_call_target="tpu_custom_call" | custom-call | tf_op jit(solution)/shard_map/spectra/pallas_call | solution.py:202
  15.7 0.3 spread.1.spread_ref
  16.0 0.1 reshape.43
  16.1 1.0 %copy.8 = bf16[2,2,128,2,2,128]{5,4,3,2,1,0:T(2,128)(2,1)S(1)} copy(bf16[2,2,128,2,2,128]{2,0,5,3,4,1:T(2,128)(2,1)S(1)} %bitcast.39) | data formatting | bytes 1048576 | tf_op jit(solution)/shard_map/transpose | solution.py:583
  17.1 0.2 reshape.39.pulse_ref
  17.3 0.1 pad_maximum_fusion.1.steer_ref
  17.4 0.4 collective-permute-done.5.refs_6_
  17.7 5.3 %all-to-all-start = ((bf16[16,16,16,128]{3,2,1,0:T(8,128)(2,1)}), bf16[16,16,16,128]{3,2,1,0:T(8,128)(2,1)S(1)}, u32[]{:S(2)}, u32[]{:S(2)}) async-start(bf16[16,16,16,128]{3,2,1,0:T(8,128)(2,1)} %bitcast.38), calls=%async_computation | async-start | bytes 2097152 | tf_op jit(solution)/shard_map/all_to_all | solution.py:594
  23.0 0.7 %crossing_sums.1 = (bf16[4,128,128]{2,1,0:T(8,128)(2,1)S(1)}, bf16[4,128,128]{2,1,0:T(8,128)(2,1)S(1)}) custom-call(s32[1]{0:T(128)} %bitcast.2.place_ref, s32[1]{0:T(128)} %bitcast.side_ref, bf16[8,128,256]{2,1,0:T(8,128)(2,1)S(1)} %spread.1.spread_ref, bf16[2,16,16,128]{3,2,1,0:T(8,128)(2,1)S(1)} %copy-done.1, ...), custom_call_target="tpu_custom_call" | custom-call | tf_op jit(solution)/shard_map/crossing_sums/pallas_call | solution.py:287
  23.8 2.7 %collective-permute-start.7 = (bf16[4,128,128]{2,1,0:T(8,128)(2,1)S(1)}, bf16[4,128,128]{2,1,0:T(8,128)(2,1)S(1)}, u32[]{:S(2)}, u32[]{:S(2)}) collective-permute-start(bf16[4,128,128]{2,1,0:T(8,128)(2,1)S(1)} %get-tuple-element.45), channel_id=1, source_target_pairs={{0,16},{1,17},{2,18},{3,19},{4,20},{5,21},{6,22},{7,23},{8,24},{9,... | collective-permute-start | bytes 393224 | tf_op jit(solution)/shard_map/ppermute | solution.py:592
  26.4 1.2 %collective-permute-start.8 = (bf16[4,128,128]{2,1,0:T(8,128)(2,1)S(1)}, bf16[4,128,128]{2,1,0:T(8,128)(2,1)S(1)}, u32[]{:S(2)}, u32[]{:S(2)}) collective-permute-start(bf16[4,128,128]{2,1,0:T(8,128)(2,1)S(1)} %get-tuple-element.46), channel_id=1, source_target_pairs={{0,17},{1,16},{2,19},{3,18},{4,21},{5,20},{6,23},{7,22},{8,25},{9,... | collective-permute-start | bytes 393224 | tf_op jit(solution)/shard_map/ppermute | solution.py:593
  27.6 14.1 %collective-permute-done.7.same_ref = bf16[4,128,128]{2,1,0:T(8,128)(2,1)S(1)} collective-permute-done((bf16[4,128,128]{2,1,0:T(8,128)(2,1)S(1)}, bf16[4,128,128]{2,1,0:T(8,128)(2,1)S(1)}, u32[]{:S(2)}, u32[]{:S(2)}) %collective-permute-start.7) | collective-permute-done | bytes 131104 | tf_op jit(solution)/shard_map/ppermute | solution.py:592
  41.8 3.8 %collective-permute-done.8.other_ref = bf16[4,128,128]{2,1,0:T(8,128)(2,1)S(1)} collective-permute-done((bf16[4,128,128]{2,1,0:T(8,128)(2,1)S(1)}, bf16[4,128,128]{2,1,0:T(8,128)(2,1)S(1)}, u32[]{:S(2)}, u32[]{:S(2)}) %collective-permute-start.8) | collective-permute-done | bytes 131104 | tf_op jit(solution)/shard_map/ppermute | solution.py:593
  45.5 5.6 %beams.1 = (f32[2,8,128]{2,1,0:T(8,128)S(1)}, f32[2,8,128]{2,1,0:T(8,128)S(1)}) custom-call(s32[1]{0:T(128)} %bitcast.side_ref, bf16[8,2,16,16,128]{4,3,2,1,0:T(8,128)(2,1)S(1)} %bitcast.37, bf16[8,128,256]{2,1,0:T(8,128)(2,1)S(1)} %spread.1.spread_ref, bf16[4,128,128]{2,1,0:T(8,128)(2,1)S(1)} %collective-permute-done.7.same_ref, ...), custom_call_target="tpu_custom_call" | custom-call | tf_op jit(solution)/shard_map/beams/pallas_call | solution.py:604
  51.1 0.1 collective-permute-start.9
  51.2 3.6 %collective-permute-done.9 = f32[2,8,128]{2,1,0:T(8,128)S(1)} collective-permute-done((f32[2,8,128]{2,1,0:T(8,128)S(1)}, f32[2,8,128]{2,1,0:T(8,128)S(1)}, u32[]{:S(2)}, u32[]{:S(2)}) %collective-permute-start.9) | collective-permute-done | bytes 8224 | tf_op jit(solution)/shard_map/ppermute | solution.py:613
  54.8 0.6 %add.21 = f32[2,8,128]{2,1,0:T(8,128)} add(f32[2,8,128]{2,1,0:T(8,128)S(1)} %get-tuple-element.49, f32[2,8,128]{2,1,0:T(8,128)S(1)} %collective-permute-done.9) | non-fusion elementwise | flops 2048 | bytes 24576 | tf_op jit(solution)/shard_map/add | solution.py:613
  (26 shorter events, 0.2 us)
Async XLA Ops:
  0.0 10.5 %copy-start = (bf16[2,64,512]{2,1,0:T(8,128)(2,1)S(1)}, bf16[2,64,512]{2,1,0:T(8,128)(2,1)}, u32[]{:S(2)}) copy-start(bf16[2,64,512]{2,1,0:T(8,128)(2,1)} %param.8) | copy-start | bytes 393220
  0.0 8.7 %copy-start.3 = (bf16[2,64]{1,0:T(2,128)(2,1)S(1)}, bf16[2,64]{1,0:T(2,128)(2,1)}, u32[]{:S(2)}) copy-start(bf16[2,64]{1,0:T(2,128)(2,1)} %param.7) | copy-start | bytes 772
  3.0 7.6 %collective-permute-start = (bf16[2,16,16,128]{3,2,1,0:T(8,128)(2,1)}, bf16[2,16,16,128]{3,2,1,0:T(8,128)(2,1)S(1)}, u32[]{:S(2)}, u32[]{:S(2)}) collective-permute-start(bf16[2,16,16,128]{3,2,1,0:T(8,128)(2,1)} %get-tuple-element.28), channel_id=1, source_target_pairs={{0,12},{2,14},{4,8},{6,10},{8,4},{10,6},{12,0},{14,2},{16,28},{18,... | collective-permute-start | bytes 393224 | tf_op jit(solution)/shard_map/ppermute | solution.py:578
  4.5 7.0 %collective-permute-start.1 = (bf16[2,16,16,128]{3,2,1,0:T(8,128)(2,1)}, bf16[2,16,16,128]{3,2,1,0:T(8,128)(2,1)S(1)}, u32[]{:S(2)}, u32[]{:S(2)}) collective-permute-start(bf16[2,16,16,128]{3,2,1,0:T(8,128)(2,1)} %get-tuple-element.29), channel_id=1, source_target_pairs={{0,14},{2,12},{4,10},{6,8},{8,6},{10,4},{12,2},{14,0},{16,30},{18,... | collective-permute-start | bytes 393224 | tf_op jit(solution)/shard_map/ppermute | solution.py:578
  5.1 12.2 %collective-permute-start.2 = (bf16[2,16,16,128]{3,2,1,0:T(8,128)(2,1)}, bf16[2,16,16,128]{3,2,1,0:T(8,128)(2,1)S(1)}, u32[]{:S(2)}, u32[]{:S(2)}) collective-permute-start(bf16[2,16,16,128]{3,2,1,0:T(8,128)(2,1)} %get-tuple-element.30), channel_id=1, source_target_pairs={{0,8},{2,10},{4,12},{6,14},{8,0},{10,2},{12,4},{14,6},{16,24},{18,... | collective-permute-start | bytes 393224 | tf_op jit(solution)/shard_map/ppermute | solution.py:578
  6.0 11.3 %collective-permute-start.3 = (bf16[2,16,16,128]{3,2,1,0:T(8,128)(2,1)}, bf16[2,16,16,128]{3,2,1,0:T(8,128)(2,1)S(1)}, u32[]{:S(2)}, u32[]{:S(2)}) collective-permute-start(bf16[2,16,16,128]{3,2,1,0:T(8,128)(2,1)} %get-tuple-element.31), channel_id=1, source_target_pairs={{0,4},{2,6},{4,0},{6,2},{8,12},{10,14},{12,8},{14,10},{16,20},{18,... | collective-permute-start | bytes 393224 | tf_op jit(solution)/shard_map/ppermute | solution.py:578
  7.1 10.3 %collective-permute-start.4 = (bf16[2,16,16,128]{3,2,1,0:T(8,128)(2,1)}, bf16[2,16,16,128]{3,2,1,0:T(8,128)(2,1)S(1)}, u32[]{:S(2)}, u32[]{:S(2)}) collective-permute-start(bf16[2,16,16,128]{3,2,1,0:T(8,128)(2,1)} %get-tuple-element.32), channel_id=1, source_target_pairs={{0,10},{2,8},{4,14},{6,12},{8,2},{10,0},{12,6},{14,4},{16,26},{18,... | collective-permute-start | bytes 393224 | tf_op jit(solution)/shard_map/ppermute | solution.py:578
  9.5 1.1 %copy-start.5 = (bf16[2,16,16,128]{3,2,1,0:T(8,128)(2,1)S(1)}, bf16[2,16,16,128]{3,2,1,0:T(8,128)(2,1)}, u32[]{:S(2)}) copy-start(bf16[2,16,16,128]{3,2,1,0:T(8,128)(2,1)} %get-tuple-element.33) | copy-start | bytes 393220
  9.5 1.9 %copy-start.4 = (bf16[2,16,16,128]{3,2,1,0:T(8,128)(2,1)S(1)}, bf16[2,16,16,128]{3,2,1,0:T(8,128)(2,1)}, u32[]{:S(2)}) copy-start(bf16[2,16,16,128]{3,2,1,0:T(8,128)(2,1)} %get-tuple-element.34) | copy-start | bytes 393220
  9.5 3.4 %copy-start.2 = (f32[2,8,64]{2,1,0:T(8,128)S(1)}, f32[2,8,64]{2,1,0:T(8,128)}, u32[]{:S(2)}) copy-start(f32[2,8,64]{2,1,0:T(8,128)} %param.9) | copy-start | bytes 12292
  10.6 7.2 %collective-permute-start.5 = (bf16[2,16,16,128]{3,2,1,0:T(8,128)(2,1)S(1)}, bf16[2,16,16,128]{3,2,1,0:T(8,128)(2,1)S(1)}, u32[]{:S(2)}, u32[]{:S(2)}) collective-permute-start(bf16[2,16,16,128]{3,2,1,0:T(8,128)(2,1)S(1)} %copy-done.5), channel_id=1, source_target_pairs={{0,6},{2,4},{4,2},{6,0},{8,14},{10,12},{12,10},{14,8},{16,22},{18,... | collective-permute-start | bytes 393224 | tf_op jit(solution)/shard_map/ppermute | solution.py:578
  11.4 6.3 %collective-permute-start.6 = (bf16[2,16,16,128]{3,2,1,0:T(8,128)(2,1)S(1)}, bf16[2,16,16,128]{3,2,1,0:T(8,128)(2,1)S(1)}, u32[]{:S(2)}, u32[]{:S(2)}) collective-permute-start(bf16[2,16,16,128]{3,2,1,0:T(8,128)(2,1)S(1)} %copy-done.4), channel_id=1, source_target_pairs={{0,2},{2,0},{4,6},{6,4},{8,10},{10,8},{12,14},{14,12},{16,18},{18,... | collective-permute-start | bytes 393224 | tf_op jit(solution)/shard_map/ppermute | solution.py:578
  16.1 6.9 %copy-start.1 = (bf16[2,16,16,128]{3,2,1,0:T(8,128)(2,1)S(1)}, bf16[2,16,16,128]{3,2,1,0:T(8,128)(2,1)}, u32[]{:S(2)}) copy-start(bf16[2,16,16,128]{3,2,1,0:T(8,128)(2,1)} %get-tuple-element.37.refs_0_) | copy-start | bytes 393220
  17.7 27.8 %all-to-all-start = ((bf16[16,16,16,128]{3,2,1,0:T(8,128)(2,1)}), bf16[16,16,16,128]{3,2,1,0:T(8,128)(2,1)S(1)}, u32[]{:S(2)}, u32[]{:S(2)}) async-start(bf16[16,16,16,128]{3,2,1,0:T(8,128)(2,1)} %bitcast.38), calls=%async_computation | async-start | bytes 2097152 | tf_op jit(solution)/shard_map/all_to_all | solution.py:594
  23.8 18.0 %collective-permute-start.7 = (bf16[4,128,128]{2,1,0:T(8,128)(2,1)S(1)}, bf16[4,128,128]{2,1,0:T(8,128)(2,1)S(1)}, u32[]{:S(2)}, u32[]{:S(2)}) collective-permute-start(bf16[4,128,128]{2,1,0:T(8,128)(2,1)S(1)} %get-tuple-element.45), channel_id=1, source_target_pairs={{0,16},{1,17},{2,18},{3,19},{4,20},{5,21},{6,22},{7,23},{8,24},{9,... | collective-permute-start | bytes 393224 | tf_op jit(solution)/shard_map/ppermute | solution.py:592
  26.4 19.1 %collective-permute-start.8 = (bf16[4,128,128]{2,1,0:T(8,128)(2,1)S(1)}, bf16[4,128,128]{2,1,0:T(8,128)(2,1)S(1)}, u32[]{:S(2)}, u32[]{:S(2)}) collective-permute-start(bf16[4,128,128]{2,1,0:T(8,128)(2,1)S(1)} %get-tuple-element.46), channel_id=1, source_target_pairs={{0,17},{1,16},{2,19},{3,18},{4,21},{5,20},{6,23},{7,22},{8,25},{9,... | collective-permute-start | bytes 393224 | tf_op jit(solution)/shard_map/ppermute | solution.py:593
  51.1 3.7 %collective-permute-start.9 = (f32[2,8,128]{2,1,0:T(8,128)S(1)}, f32[2,8,128]{2,1,0:T(8,128)S(1)}, u32[]{:S(2)}, u32[]{:S(2)}) collective-permute-start(f32[2,8,128]{2,1,0:T(8,128)S(1)} %get-tuple-element.50), channel_id=1, source_target_pairs={{0,1},{1,0},{2,3},{3,2},{4,5},{5,4},{6,7},{7,6},{8,9},{9,8},{10,11... | collective-permute-start | bytes 24584 | tf_op jit(solution)/shard_map/ppermute | solution.py:613

commit v11 on v9

--- a/solution.py
+++ b/solution.py
@@ -125,7 +125,7 @@
 
 
 def far_first(members):
-    return [0] + sorted(range(1, members), key=lambda n: (-(n >> 1).bit_count(), n & 1, -n))
+    return [0] + sorted(range(1, members), key=lambda n: (n & 1, -n))
 
 
 def spectra_body(half_ref, place_ref, table_hbm, echo_hbm, *refs, apart):

time: 55.6 us -> 55.7 us (level)
  starting transfers between devices: 16.5 us -> 15.5 us
  waiting for transfers between devices: 22.8 us -> 23.8 us
    ppermute x7, waiting for transfers between devices: 4.82 us -> 5.84 us  [on_device_owned(): lax.ppermute(block, 'elem', [(m, m ^ n) for m in range(elems)])]
    ppermute x7, starting transfers between devices: 7.21 us -> 6.26 us  [on_device_owned(): lax.ppermute(block, 'elem', [(m, m ^ n) for m in range(elems)])]
  transfers between devices with their start and end apart: 11 -> 11, of which waited for: 8 -> 7; matrix products, arithmetic and copies ran while one was open for 6% -> 6% of each run, Pallas kernels for 7% -> 7%
where the time goes in v11:
time: 55.7 us; the launch traced here: 55.4 us
  waiting for transfers between devices  23.8 us (43%)
  starting transfers between devices  15.5 us (28%)
  Pallas kernels  12.2 us (22%)
  local copies, waits for them, and re-layouts  2.81 us (5%)
  other arithmetic  0.89 us (2%)
    ppermute x1, waiting for transfers between devices, on_device_owned(): same = lax.ppermute(same, ('elem', 'range'), list(enumerate(across)))  10.6 us
    ppermute x7, starting transfers between devices, on_device_owned(): lax.ppermute(block, 'elem', [(m, m ^ n) for m in range(elems)])  6.26 us
    ppermute x7, waiting for transfers between devices, on_device_owned(): lax.ppermute(block, 'elem', [(m, m ^ n) for m in range(elems)])  5.84 us
    pallas_call x2, Pallas kernels, spectra(): pl.pallas_call(functools.partial(spectra_body, apart=apart), in_specs=[pl...  5.65 us
    pallas_call x1, Pallas kernels, on_device_owned(): pl.pallas_call(beams_body, in_specs=[pl.BlockSpec(memory_space=pltpu.SMEM...  5.55 us
    all_to_all x1, starting transfers between devices, on_device_owned(): lax.all_to_all(sent.reshape(group, *sent.shape[2:]), ('elem', 'range'), 0...  5.2 us
    ppermute x1, waiting for transfers between devices, on_device_owned(): lax.ppermute(other, ('elem', 'range'), [(n, to ^ 1) for n, to in enumerat...  3.77 us
    ppermute x1, waiting for transfers between devices, on_device_owned(): return own + lax.ppermute(send, 'range', [(0, 1), (1, 0)])  3.61 us
  transfers between devices with their start and end apart: 11, of which 7 were waited for; matrix products, arithmetic and copies ran while one was open for 6% of the time, Pallas kernels for 7%

profile of v11, /device:TPU:8, one launch (start us, length us, event | category | flops | bytes accessed | tf_op | source)
XLA Modules:
  0.0 55.4 jit_solution(8216625287081125936)
XLA Ops:
  0.0 3.0 %spectra.3 = (bf16[2,16,16,128]{3,2,1,0:T(8,128)(2,1)}, bf16[2,16,16,128]{3,2,1,0:T(8,128)(2,1)}, bf16[2,16,16,128]{3,2,1,0:T(8,128)(2,1)}, bf16[2,16,16,128]{3,...) custom-call(s32[1]{0:T(128)} %bitcast.3.half_ref, ...), custom_call_target="tpu_custom_call" | custom-call | tf_op jit(solution)/shard_map/spectra/pallas_call | solution.py:202
  3.0 1.5 %collective-permute-start = (bf16[2,16,16,128]{3,2,1,0:T(8,128)(2,1)}, bf16[2,16,16,128]{3,2,1,0:T(8,128)(2,1)S(1)}, u32[]{:S(2)}, u32[]{:S(2)}) collective-permute-start(bf16[2,16,16,128]{3,2,1,0:T(8,128)(2,1)} %get-tuple-element.25), channel_id=1, source_target_pairs={{0,12},{2,14},{4,8},{6,10},{8,4},{10,6},{12,0},{14,2},{16,28},{18,... | collective-permute-start | bytes 393224 | tf_op jit(solution)/shard_map/ppermute | solution.py:578
  4.4 1.6 %collective-permute-start.1 = (bf16[2,16,16,128]{3,2,1,0:T(8,128)(2,1)}, bf16[2,16,16,128]{3,2,1,0:T(8,128)(2,1)S(1)}, u32[]{:S(2)}, u32[]{:S(2)}) collective-permute-start(bf16[2,16,16,128]{3,2,1,0:T(8,128)(2,1)} %get-tuple-element.26), channel_id=1, source_target_pairs={{0,8},{2,10},{4,12},{6,14},{8,0},{10,2},{12,4},{14,6},{16,24},{18,... | collective-permute-start | bytes 393224 | tf_op jit(solution)/shard_map/ppermute | solution.py:578
  6.0 0.5 collective-permute-start.2
  6.5 2.7 %collective-permute-start.4 = (bf16[2,16,16,128]{3,2,1,0:T(8,128)(2,1)}, bf16[2,16,16,128]{3,2,1,0:T(8,128)(2,1)S(1)}, u32[]{:S(2)}, u32[]{:S(2)}) collective-permute-start(bf16[2,16,16,128]{3,2,1,0:T(8,128)(2,1)} %get-tuple-element.29), channel_id=1, source_target_pairs={{0,10},{2,8},{4,14},{6,12},{8,2},{10,0},{12,6},{14,4},{16,26},{18,... | collective-permute-start | bytes 393224 | tf_op jit(solution)/shard_map/ppermute | solution.py:578
  9.2 1.3 %collective-permute-done.refs_1_ = bf16[2,16,16,128]{3,2,1,0:T(8,128)(2,1)S(1)} collective-permute-done((bf16[2,16,16,128]{3,2,1,0:T(8,128)(2,1)}, bf16[2,16,16,128]{3,2,1,0:T(8,128)(2,1)S(1)}, u32[]{:S(2)}, u32[]{:S(2)}) %collective-permute-start) | collective-permute-done | bytes 131104 | tf_op jit(solution)/shard_map/ppermute | solution.py:578
  10.5 2.9 %collective-permute-done.1.refs_2_ = bf16[2,16,16,128]{3,2,1,0:T(8,128)(2,1)S(1)} collective-permute-done((bf16[2,16,16,128]{3,2,1,0:T(8,128)(2,1)}, bf16[2,16,16,128]{3,2,1,0:T(8,128)(2,1)S(1)}, u32[]{:S(2)}, u32[]{:S(2)}) %collective-permute-start.1) | collective-permute-done | bytes 131104 | tf_op jit(solution)/shard_map/ppermute | solution.py:578
  13.4 2.7 %spectra.2 = bf16[8,2,16,16,128]{4,3,2,1,0:T(8,128)(2,1)} custom-call(s32[1]{0:T(128)} %bitcast.1.half_ref, s32[1]{0:T(128)} %bitcast.2.place_ref, bf16[2,8,16,256]{3,2,1,0:T(8,128)(2,1)} %constant.46.clone.table_hbm, bf16[2,32,128,128]{3,2,1,0:T(8,128)(2,1)} %echo_hbm.3), custom_call_target="tpu_custom_call" | custom-call | tf_op jit(solution)/shard_map/spectra/pallas_call | solution.py:202
  16.1 0.0 copy-start.3
  16.1 0.6 %collective-permute-done.4.refs_5_ = bf16[2,16,16,128]{3,2,1,0:T(8,128)(2,1)S(1)} collective-permute-done((bf16[2,16,16,128]{3,2,1,0:T(8,128)(2,1)}, bf16[2,16,16,128]{3,2,1,0:T(8,128)(2,1)S(1)}, u32[]{:S(2)}, u32[]{:S(2)}) %collective-permute-start.4) | collective-permute-done | bytes 131104 | tf_op jit(solution)/shard_map/ppermute | solution.py:578
  16.7 1.1 %collective-permute-done.5.refs_6_ = bf16[2,16,16,128]{3,2,1,0:T(8,128)(2,1)S(1)} collective-permute-done((bf16[2,16,16,128]{3,2,1,0:T(8,128)(2,1)}, bf16[2,16,16,128]{3,2,1,0:T(8,128)(2,1)S(1)}, u32[]{:S(2)}, u32[]{:S(2)}) %collective-permute-start.5) | collective-permute-done | bytes 131104 | tf_op jit(solution)/shard_map/ppermute | solution.py:578
  17.8 5.2 %all-to-all-start = ((bf16[16,16,16,128]{3,2,1,0:T(8,128)(2,1)}), bf16[16,16,16,128]{3,2,1,0:T(8,128)(2,1)S(1)}, u32[]{:S(2)}, u32[]{:S(2)}) async-start(bf16[16,16,16,128]{3,2,1,0:T(8,128)(2,1)} %bitcast.38), calls=%async_computation | async-start | bytes 2097152 | tf_op jit(solution)/shard_map/all_to_all | solution.py:587
  23.0 0.3 spread.1.spread_ref
  23.4 0.3 tile.21
  23.7 0.4 reshape.40
  24.2 0.3 tile.9
  24.4 0.4 reshape.39
  24.9 0.0 copy-start.2
  24.9 0.1 maximum_bitcast_fusion
  25.1 0.7 %crossing_sums.1 = (bf16[4,128,128]{2,1,0:T(8,128)(2,1)S(1)}, bf16[4,128,128]{2,1,0:T(8,128)(2,1)S(1)}) custom-call(s32[1]{0:T(128)} %bitcast.2.place_ref, s32[1]{0:T(128)} %bitcast.side_ref, bf16[8,128,256]{2,1,0:T(8,128)(2,1)S(1)} %spread.1.spread_ref, bf16[2,16,16,128]{3,2,1,0:T(8,128)(2,1)S(1)} %copy-done.1, ...), custom_call_target="tpu_custom_call" | custom-call | tf_op jit(solution)/shard_map/crossing_sums/pallas_call | solution.py:287
  25.9 2.7 %collective-permute-start.7 = (bf16[4,128,128]{2,1,0:T(8,128)(2,1)S(1)}, bf16[4,128,128]{2,1,0:T(8,128)(2,1)S(1)}, u32[]{:S(2)}, u32[]{:S(2)}) collective-permute-start(bf16[4,128,128]{2,1,0:T(8,128)(2,1)S(1)} %get-tuple-element.41), channel_id=1, source_target_pairs={{0,16},{1,17},{2,18},{3,19},{4,20},{5,21},{6,22},{7,23},{8,24},{9,... | collective-permute-start | bytes 393224 | tf_op jit(solution)/shard_map/ppermute | solution.py:585
  28.5 1.2 %collective-permute-start.8 = (bf16[4,128,128]{2,1,0:T(8,128)(2,1)S(1)}, bf16[4,128,128]{2,1,0:T(8,128)(2,1)S(1)}, u32[]{:S(2)}, u32[]{:S(2)}) collective-permute-start(bf16[4,128,128]{2,1,0:T(8,128)(2,1)S(1)} %get-tuple-element.42), channel_id=1, source_target_pairs={{0,17},{1,16},{2,19},{3,18},{4,21},{5,20},{6,23},{7,22},{8,25},{9,... | collective-permute-start | bytes 393224 | tf_op jit(solution)/shard_map/ppermute | solution.py:586
  29.8 0.1 reshape.43
  29.9 1.0 %copy.8 = bf16[2,2,128,2,2,128]{5,4,3,2,1,0:T(2,128)(2,1)S(1)} copy(bf16[2,2,128,2,2,128]{2,0,5,3,4,1:T(2,128)(2,1)S(1)} %bitcast.39) | data formatting | bytes 1048576 | tf_op jit(solution)/shard_map/transpose | solution.py:598
  30.9 0.2 reshape.42.pulse_ref
  31.1 0.1 pad_maximum_fusion.1.steer_ref
  31.1 10.6 %collective-permute-done.7.same_ref = bf16[4,128,128]{2,1,0:T(8,128)(2,1)S(1)} collective-permute-done((bf16[4,128,128]{2,1,0:T(8,128)(2,1)S(1)}, bf16[4,128,128]{2,1,0:T(8,128)(2,1)S(1)}, u32[]{:S(2)}, u32[]{:S(2)}) %collective-permute-start.7) | collective-permute-done | bytes 131104 | tf_op jit(solution)/shard_map/ppermute | solution.py:585
  41.8 3.8 %collective-permute-done.8.other_ref = bf16[4,128,128]{2,1,0:T(8,128)(2,1)S(1)} collective-permute-done((bf16[4,128,128]{2,1,0:T(8,128)(2,1)S(1)}, bf16[4,128,128]{2,1,0:T(8,128)(2,1)S(1)}, u32[]{:S(2)}, u32[]{:S(2)}) %collective-permute-start.8) | collective-permute-done | bytes 131104 | tf_op jit(solution)/shard_map/ppermute | solution.py:586
  45.5 5.6 %beams.1 = (f32[2,8,128]{2,1,0:T(8,128)S(1)}, f32[2,8,128]{2,1,0:T(8,128)S(1)}) custom-call(s32[1]{0:T(128)} %bitcast.side_ref, bf16[8,2,16,16,128]{4,3,2,1,0:T(8,128)(2,1)S(1)} %bitcast.37, bf16[8,128,256]{2,1,0:T(8,128)(2,1)S(1)} %spread.1.spread_ref, bf16[4,128,128]{2,1,0:T(8,128)(2,1)S(1)} %collective-permute-done.7.same_ref, ...), custom_call_target="tpu_custom_call" | custom-call | tf_op jit(solution)/shard_map/beams/pallas_call | solution.py:602
  51.1 0.1 collective-permute-start.9
  51.2 3.6 %collective-permute-done.9 = f32[2,8,128]{2,1,0:T(8,128)S(1)} collective-permute-done((f32[2,8,128]{2,1,0:T(8,128)S(1)}, f32[2,8,128]{2,1,0:T(8,128)S(1)}, u32[]{:S(2)}, u32[]{:S(2)}) %collective-permute-start.9) | collective-permute-done | bytes 8224 | tf_op jit(solution)/shard_map/ppermute | solution.py:611
  54.8 0.6 %add.21 = f32[2,8,128]{2,1,0:T(8,128)} add(f32[2,8,128]{2,1,0:T(8,128)S(1)} %get-tuple-element.43, f32[2,8,128]{2,1,0:T(8,128)S(1)} %collective-permute-done.9) | non-fusion elementwise | flops 2048 | bytes 24576 | tf_op jit(solution)/shard_map/add | solution.py:611
  (22 shorter events, 0.2 us)
Async XLA Ops:
  0.0 23.0 %copy-start = (bf16[2,64,512]{2,1,0:T(8,128)(2,1)S(1)}, bf16[2,64,512]{2,1,0:T(8,128)(2,1)}, u32[]{:S(2)}) copy-start(bf16[2,64,512]{2,1,0:T(8,128)(2,1)} %param.8) | copy-start | bytes 393220
  3.0 7.6 %collective-permute-start = (bf16[2,16,16,128]{3,2,1,0:T(8,128)(2,1)}, bf16[2,16,16,128]{3,2,1,0:T(8,128)(2,1)S(1)}, u32[]{:S(2)}, u32[]{:S(2)}) collective-permute-start(bf16[2,16,16,128]{3,2,1,0:T(8,128)(2,1)} %get-tuple-element.25), channel_id=1, source_target_pairs={{0,12},{2,14},{4,8},{6,10},{8,4},{10,6},{12,0},{14,2},{16,28},{18,... | collective-permute-start | bytes 393224 | tf_op jit(solution)/shard_map/ppermute | solution.py:578
  4.4 9.0 %collective-permute-start.1 = (bf16[2,16,16,128]{3,2,1,0:T(8,128)(2,1)}, bf16[2,16,16,128]{3,2,1,0:T(8,128)(2,1)S(1)}, u32[]{:S(2)}, u32[]{:S(2)}) collective-permute-start(bf16[2,16,16,128]{3,2,1,0:T(8,128)(2,1)} %get-tuple-element.26), channel_id=1, source_target_pairs={{0,8},{2,10},{4,12},{6,14},{8,0},{10,2},{12,4},{14,6},{16,24},{18,... | collective-permute-start | bytes 393224 | tf_op jit(solution)/shard_map/ppermute | solution.py:578
  6.0 10.1 %collective-permute-start.2 = (bf16[2,16,16,128]{3,2,1,0:T(8,128)(2,1)}, bf16[2,16,16,128]{3,2,1,0:T(8,128)(2,1)S(1)}, u32[]{:S(2)}, u32[]{:S(2)}) collective-permute-start(bf16[2,16,16,128]{3,2,1,0:T(8,128)(2,1)} %get-tuple-element.27), channel_id=1, source_target_pairs={{0,4},{2,6},{4,0},{6,2},{8,12},{10,14},{12,8},{14,10},{16,20},{18,... | collective-permute-start | bytes 393224 | tf_op jit(solution)/shard_map/ppermute | solution.py:578
  6.5 9.6 %collective-permute-start.3 = (bf16[2,16,16,128]{3,2,1,0:T(8,128)(2,1)}, bf16[2,16,16,128]{3,2,1,0:T(8,128)(2,1)S(1)}, u32[]{:S(2)}, u32[]{:S(2)}) collective-permute-start(bf16[2,16,16,128]{3,2,1,0:T(8,128)(2,1)} %get-tuple-element.28), channel_id=1, source_target_pairs={{0,14},{2,12},{4,10},{6,8},{8,6},{10,4},{12,2},{14,0},{16,30},{18,... | collective-permute-start | bytes 393224 | tf_op jit(solution)/shard_map/ppermute | solution.py:578
  6.5 10.2 %collective-permute-start.4 = (bf16[2,16,16,128]{3,2,1,0:T(8,128)(2,1)}, bf16[2,16,16,128]{3,2,1,0:T(8,128)(2,1)S(1)}, u32[]{:S(2)}, u32[]{:S(2)}) collective-permute-start(bf16[2,16,16,128]{3,2,1,0:T(8,128)(2,1)} %get-tuple-element.29), channel_id=1, source_target_pairs={{0,10},{2,8},{4,14},{6,12},{8,2},{10,0},{12,6},{14,4},{16,26},{18,... | collective-permute-start | bytes 393224 | tf_op jit(solution)/shard_map/ppermute | solution.py:578
  10.5 7.3 %collective-permute-start.5 = (bf16[2,16,16,128]{3,2,1,0:T(8,128)(2,1)}, bf16[2,16,16,128]{3,2,1,0:T(8,128)(2,1)S(1)}, u32[]{:S(2)}, u32[]{:S(2)}) collective-permute-start(bf16[2,16,16,128]{3,2,1,0:T(8,128)(2,1)} %get-tuple-element.30), channel_id=1, source_target_pairs={{0,6},{2,4},{4,2},{6,0},{8,14},{10,12},{12,10},{14,8},{16,22},{18,... | collective-permute-start | bytes 393224 | tf_op jit(solution)/shard_map/ppermute | solution.py:578
  13.4 4.4 %collective-permute-start.6 = (bf16[2,16,16,128]{3,2,1,0:T(8,128)(2,1)}, bf16[2,16,16,128]{3,2,1,0:T(8,128)(2,1)S(1)}, u32[]{:S(2)}, u32[]{:S(2)}) collective-permute-start(bf16[2,16,16,128]{3,2,1,0:T(8,128)(2,1)} %get-tuple-element.31), channel_id=1, source_target_pairs={{0,2},{2,0},{4,6},{6,4},{8,10},{10,8},{12,14},{14,12},{16,18},{18,... | collective-permute-start | bytes 393224 | tf_op jit(solution)/shard_map/ppermute | solution.py:578
  16.1 7.2 %copy-start.3 = (bf16[2,64]{1,0:T(2,128)(2,1)S(1)}, bf16[2,64]{1,0:T(2,128)(2,1)}, u32[]{:S(2)}) copy-start(bf16[2,64]{1,0:T(2,128)(2,1)} %param.7) | copy-start | bytes 772
  17.8 27.7 %all-to-all-start = ((bf16[16,16,16,128]{3,2,1,0:T(8,128)(2,1)}), bf16[16,16,16,128]{3,2,1,0:T(8,128)(2,1)S(1)}, u32[]{:S(2)}, u32[]{:S(2)}) async-start(bf16[16,16,16,128]{3,2,1,0:T(8,128)(2,1)} %bitcast.38), calls=%async_computation | async-start | bytes 2097152 | tf_op jit(solution)/shard_map/all_to_all | solution.py:587
  24.1 1.0 %copy-start.1 = (bf16[2,16,16,128]{3,2,1,0:T(8,128)(2,1)S(1)}, bf16[2,16,16,128]{3,2,1,0:T(8,128)(2,1)}, u32[]{:S(2)}) copy-start(bf16[2,16,16,128]{3,2,1,0:T(8,128)(2,1)} %get-tuple-element.33.refs_0_) | copy-start | bytes 393220
  24.9 4.8 %copy-start.2 = (f32[2,8,64]{2,1,0:T(8,128)S(1)}, f32[2,8,64]{2,1,0:T(8,128)}, u32[]{:S(2)}) copy-start(f32[2,8,64]{2,1,0:T(8,128)} %param.9) | copy-start | bytes 12292
  25.9 15.9 %collective-permute-start.7 = (bf16[4,128,128]{2,1,0:T(8,128)(2,1)S(1)}, bf16[4,128,128]{2,1,0:T(8,128)(2,1)S(1)}, u32[]{:S(2)}, u32[]{:S(2)}) collective-permute-start(bf16[4,128,128]{2,1,0:T(8,128)(2,1)S(1)} %get-tuple-element.41), channel_id=1, source_target_pairs={{0,16},{1,17},{2,18},{3,19},{4,20},{5,21},{6,22},{7,23},{8,24},{9,... | collective-permute-start | bytes 393224 | tf_op jit(solution)/shard_map/ppermute | solution.py:585
  28.5 17.0 %collective-permute-start.8 = (bf16[4,128,128]{2,1,0:T(8,128)(2,1)S(1)}, bf16[4,128,128]{2,1,0:T(8,128)(2,1)S(1)}, u32[]{:S(2)}, u32[]{:S(2)}) collective-permute-start(bf16[4,128,128]{2,1,0:T(8,128)(2,1)S(1)} %get-tuple-element.42), channel_id=1, source_target_pairs={{0,17},{1,16},{2,19},{3,18},{4,21},{5,20},{6,23},{7,22},{8,25},{9,... | collective-permute-start | bytes 393224 | tf_op jit(solution)/shard_map/ppermute | solution.py:586
  51.1 3.7 %collective-permute-start.9 = (f32[2,8,128]{2,1,0:T(8,128)S(1)}, f32[2,8,128]{2,1,0:T(8,128)S(1)}, u32[]{:S(2)}, u32[]{:S(2)}) collective-permute-start(f32[2,8,128]{2,1,0:T(8,128)S(1)} %get-tuple-element.44), channel_id=1, source_target_pairs={{0,1},{1,0},{2,3},{3,2},{4,5},{5,4},{6,7},{7,6},{8,9},{9,8},{10,11... | collective-permute-start | bytes 24584 | tf_op jit(solution)/shard_map/ppermute | solution.py:611
